TPU v7x, 512 devices: a whole 4x4x16 slice. The times are simulated.
512 devices in a mesh: role: 2 (over y_hi), dp: 8 (over x, core), hidden: 32 (over z, y_lo).
Axes of the slice: x: 4, y: 4 (y_hi: 2, y_lo: 2; y = y_hi * 2 + y_lo), z: 16, core: 2. Of those that a mesh axis runs over, the one named last changes fastest.
Arguments:
- token_rows: bfloat16 [2, 1024, 5120], P('role', 'dp'), may hold values from -6 to 6
- cotangent: bfloat16 [1024, 5120], P('dp'), may hold values from -6 to 6
- staleness: int32 [1024], P('dp'), may hold values from 0 to 7
- prefill_rows: int32 [8], P('dp'), may hold values from 1 to 128, as said below
- frozen_gate_up_weight: bfloat16 [2, 5120, 13824], P(None, ('role', 'dp'), 'hidden'), may hold values from -0.078125 to 0.078125
- down_weight: bfloat16 [13824, 5120], P('hidden', ('role', 'dp')), may hold values from -0.0546875 to 0.0546875
- adapter_in: float32 [2, 5120, 32], P(None, 'hidden'), may hold values from -0.078125 to 0.078125
- adapter_out: float32 [2, 32, 13824], P(None, None, 'hidden'), may hold values from -0.6 to 0.6
- moment_in: float32 [2, 5120, 32], P(None, 'hidden'), may hold values from -549.5361 to 549.5361
- square_in: float32 [2, 5120, 32], P(None, 'hidden'), may hold values from 20.97152 to 2097.152
- moment_out: float32 [2, 32, 13824], P(None, None, 'hidden'), may hold values from -1.2 to 1.2
- square_out: float32 [2, 32, 13824], P(None, None, 'hidden'), may hold values from 0.01 to 1
Outputs:
- layer_old: bfloat16 [2, 1024, 5120], P('role', 'dp', 'hidden')
- layer_new: bfloat16 [2, 1024, 5120], P('role', 'dp', 'hidden')
- new_adapter_in: float32 [2, 2, 5120, 32], P('role', None, 'hidden')
- new_adapter_out: float32 [2, 2, 32, 13824], P('role', None, None, 'hidden')
- new_moment_in: float32 [2, 2, 5120, 32], P('role', None, 'hidden')
- new_square_in: float32 [2, 2, 5120, 32], P('role', None, 'hidden')
- new_moment_out: float32 [2, 2, 32, 13824], P('role', None, None, 'hidden')
- new_square_out: float32 [2, 2, 32, 13824], P('role', None, None, 'hidden')
Inputs may be any that keep to these rules, and one draw needn't show every extreme that they name: The first prefill_rows[g] rows of rollout group g are live, the rest are padding; some group is full in every draw.
All inputs are finite; a program needn't handle non-finite values.
Results may differ from a plain program's by a relative error of at most 0.025.
Values may be sent and summed in bfloat16 or wider, within the bound.
No kernel may reach another device: no remote copies, remote signals or barrier semaphores. Data moves between devices by JAX's collectives and lax.ppermute only.
A program may use at most 128 MiB of HBM per device.

v0:
```python
import jax
import jax.numpy as jnp
from jax import lax
from jax.experimental import pallas as pl
from jax.experimental.pallas import tpu as pltpu
from jax.sharding import Mesh
from jax.sharding import PartitionSpec as P


D = 5120
OPT_STEP = 10

ADAPTER_SCALE = 2.0
BETA_ONE = 0.9
BETA_TWO = 0.999
RATE_FACTOR = 0.34
ADAM_EPS = 1e-08
KEEP_RATE = 0.75

DP = ("x", "core")
ALL_GROUPS = ("role", "x", "core")
NEAR = ("zl", "ylo")
HIDDEN = ("zh", "zl", "ylo")
BF = jnp.bfloat16
F32 = jnp.float32


VMEM = pl.BlockSpec(memory_space=pltpu.VMEM)
SMEM = pl.BlockSpec(memory_space=pltpu.SMEM)
ANY = pl.BlockSpec(memory_space=pl.ANY)


def exchange(pieces, axis):
    return lax.all_to_all(pieces, axis, split_axis=0, concat_axis=0, tiled=True)


def swapped(value, axis):
    return lax.ppermute(value, axis, [(0, 1), (1, 0)])


def spread(value, axis):
    count = lax.axis_size(axis)
    return exchange(jnp.broadcast_to(value, (count, *value.shape)), axis)


def sum_first(pieces):
    return pieces.astype(F32).sum(axis=0)


def hidden_total(value):
    near = sum_first(spread(value.astype(BF), NEAR)).astype(BF)
    return sum_first(spread(near, "zh"))


def shifted(value, axis, step):
    count = lax.axis_size(axis)
    return lax.ppermute(value, axis, [(i, (i + step) % count) for i in range(count)])


def plus_partner(value, axis, step):
    count = lax.axis_size(axis)
    return value + lax.ppermute(value, axis, [(i, i ^ step) for i in range(count)])


def shifted_sum(pieces, axis):
    index = lax.axis_index(axis)
    count = lax.axis_size(axis)
    total = lax.dynamic_index_in_dim(pieces, index, 0, keepdims=False).astype(F32)
    for step in range(1, count):
        piece = lax.dynamic_index_in_dim(pieces, lax.rem(index + step, count), 0, keepdims=False)
        total = total + shifted(piece, axis, step).astype(F32)
    return total


def adam_update(param, grad, first, second):
    learn_rate = RATE_FACTOR / D**0.5
    first_new = BETA_ONE * first + (1.0 - BETA_ONE) * grad
    second_new = BETA_TWO * second + (1.0 - BETA_TWO) * grad * grad
    first_fix = first_new / (1.0 - BETA_ONE**OPT_STEP)
    second_fix = second_new / (1.0 - BETA_TWO**OPT_STEP)
    return (
        param - learn_rate * first_fix / (jnp.sqrt(second_fix) + ADAM_EPS),
        first_new,
        second_new,
    )


def dot(a, b, dims):
    return lax.dot_general(a, b, (dims, ((), ())), preferred_element_type=F32)


def rows_kernel(token_ref, cotangent_ref, scale_ref, out_ref):
    width = out_ref.shape[4]
    scale = scale_ref[...]
    for half in range(2):
        for x in range(4):
            columns = slice((half * 4 + x) * width, (half * 4 + x + 1) * width)
            out_ref[x, 0, half] = token_ref[:, columns]
            out_ref[x, 1, half] = (scale * cotangent_ref[:, columns].astype(F32)).astype(BF)


def rows_by_x(tokens, cotangent, scale):
    group, width = tokens.shape
    return pl.pallas_call(
        rows_kernel,
        out_shape=jax.ShapeDtypeStruct((4, 2, 2, group, width // 8), BF),
        in_specs=[VMEM, VMEM, VMEM],
        out_specs=VMEM,
        name="rows_by_x",
    )(tokens, cotangent, scale)


def partial_kernel(flag_ref, rows_ref, *refs):
    weight_refs, down_refs = refs[:4], refs[4:6]
    out_ref, weight, down, held, in_sems, out_sems = refs[6:]
    role, core = flag_ref[0], flag_ref[1]
    depth = weight_refs[0].shape[1]
    weight_loads, down_loads = [], []
    for i in range(2):
        side = core if i == 0 else 1 - core
        place = pl.ds(pl.multiple_of(side * depth, depth), depth)
        for j in range(2):
            half = role if j == 0 else 1 - role
            n = 2 * i + j
            down_loads.append(pltpu.make_async_copy(down_refs[i].at[j], down.at[half, place, :], in_sems.at[n]))
            weight_loads.append(pltpu.make_async_copy(weight_refs[n], weight.at[half, :, place, :], in_sems.at[4 + n]))
    for copy in down_loads + weight_loads:
        copy.start()

    count, group = rows_ref.shape[0], rows_ref.shape[3]

    def all_rows(which, half):
        return jnp.concatenate([rows_ref[x, which, half] for x in range(count)], axis=0)

    stores = []
    for k in (2, 0, 1):
        for copy in {2: down_loads, 0: weight_loads, 1: []}[k]:
            copy.wait()
        total = 0.0
        for half in range(2):
            if k < 2:
                total += dot(all_rows(0, half), weight[half, k], ((1,), (0,)))
            else:
                total += dot(all_rows(1, half), down[half], ((1,), (0,)))
        turned = total.astype(BF).T
        for x in range(count):
            held[k, x] = turned[:, x * group : (x + 1) * group]
        copy = pltpu.make_async_copy(held.at[k], out_ref.at[:, k], out_sems.at[k])
        copy.start()
        stores.append(copy)
    for copy in stores:
        copy.wait()


def partials(flags, rows, weights, downs):
    count, _, _, group, _ = rows.shape
    _, depth, cols = weights[0].shape
    return pl.pallas_call(
        partial_kernel,
        out_shape=jax.ShapeDtypeStruct((count, 3, cols, group), BF),
        in_specs=[SMEM, VMEM] + [ANY] * 6,
        out_specs=ANY,
        scratch_shapes=[
            pltpu.VMEM((2, 2, 2 * depth, cols), BF),
            pltpu.VMEM((2, 2 * depth, cols), BF),
            pltpu.VMEM((3, count, cols, group), BF),
            pltpu.SemaphoreType.DMA((8,)),
            pltpu.SemaphoreType.DMA((3,)),
        ],
        name="partials",
    )(flags, rows, *weights, *downs)


def middle_kernel(flag_ref, pieces_ref, reduced_ref, lift_ref, base_ref, hidden_ref, through_ref, grad_ref):
    total = [pieces_ref[0, k].astype(F32) for k in range(3)]
    for x in range(1, pieces_ref.shape[0]):
        for k in range(3):
            total[k] = total[k] + pieces_ref[x, k].astype(F32)
    rank = lift_ref.shape[1]
    pre = []
    for k in range(2):
        base_ref[k] = total[k]
        part = reduced_ref[k * rank : (k + 1) * rank, :]
        pre.append(total[k] + ADAPTER_SCALE * dot(lift_ref[k], part, ((0,), (0,))))
    gate, up = pre
    sigma = jax.nn.sigmoid(gate)
    silu = gate * sigma
    hidden_ref[...] = (silu * up).astype(BF)
    grad_hidden = jnp.where(flag_ref[0] == 0, total[2], jnp.zeros_like(total[2]))
    grads = (
        (grad_hidden * up * sigma * (1.0 + gate * (1.0 - sigma))).astype(BF),
        (grad_hidden * silu).astype(BF),
    )
    for k in range(2):
        block = slice(k * rank, (k + 1) * rank)
        through_ref[block, :] = dot(lift_ref[k], grads[k], ((1,), (0,))).astype(BF)
        grad_ref[block, :] = (
            ADAPTER_SCALE * dot(reduced_ref[block, :], grads[k], ((1,), (1,)))
        ).astype(BF)


def middle(flags, pieces, reduced, lift):
    _, _, cols, group = pieces.shape
    ranks = reduced.shape[0]
    return pl.pallas_call(
        middle_kernel,
        out_shape=(
            jax.ShapeDtypeStruct((2, cols, group), F32),
            jax.ShapeDtypeStruct((cols, group), BF),
            jax.ShapeDtypeStruct((ranks, group), BF),
            jax.ShapeDtypeStruct((ranks, cols), BF),
        ),
        in_specs=[SMEM, VMEM, VMEM, VMEM],
        out_specs=(VMEM, VMEM, VMEM, VMEM),
        name="middle",
    )(flags, pieces, reduced, lift)


def down_product(flag_ref, hidden, block_refs, out_ref):
    role, x, core = flag_ref[0], flag_ref[2], flag_ref[1]
    size = out_ref.shape[1]
    for i in range(2):
        side = core if i == 0 else 1 - core
        for step in range(4):
            source = lax.rem(x + 4 - step, 4)
            for j in range(2):
                half = role if j == 0 else 1 - role
                product = dot(block_refs[4 * i + step][j], hidden, ((1,), (0,))).astype(BF)
                block = half * 8 + 2 * source + side
                for s in range(2):
                    place = 2 * block + s
                    out_ref[lax.rem(place, 8) * 4 + lax.div(place, 8)] = product[s * size : (s + 1) * size]


def old_kernel(flag_ref, hidden_ref, *refs):
    down_product(flag_ref, hidden_ref[...], refs[:-1], refs[-1])


def new_kernel(flag_ref, base_ref, reduced_ref, lift_ref, *refs):
    rank = lift_ref.shape[1]
    post = []
    for k in range(2):
        part = reduced_ref[k * rank : (k + 1) * rank, :]
        post.append(base_ref[k] + ADAPTER_SCALE * dot(lift_ref[k], part, ((0,), (0,))))
    hidden = (post[0] * jax.nn.sigmoid(post[0]) * post[1]).astype(BF)
    down_product(flag_ref, hidden, refs[:-1], refs[-1])


def layer_call(kernel, group, width, blocks, *operands):
    return pl.pallas_call(
        kernel,
        out_shape=jax.ShapeDtypeStruct((32, width, group), BF),
        in_specs=[SMEM] + [VMEM] * (len(operands) - 1 + len(blocks)),
        out_specs=VMEM,
    )(*operands, *blocks)


def step(
    token_rows,
    cotangent,
    staleness,
    prefill_rows,
    frozen_gate_up_weight,
    down_weight,
    adapter_in,
    adapter_out,
    moment_in,
    square_in,
    moment_out,
    square_out,
):
    role = lax.axis_index("role")
    core = lax.axis_index("core")
    shard_index = lax.axis_index(HIDDEN)
    flags = jnp.stack([role, core, lax.axis_index("x")]).astype(jnp.int32)
    token_batch = token_rows[0]
    group_rows = token_batch.shape[0]
    slice_width = adapter_in.shape[1]
    cols = frozen_gate_up_weight.shape[2]
    token_part = lax.dynamic_slice_in_dim(token_batch, shard_index * slice_width, slice_width, 1)

    in_bf = adapter_in.astype(BF)
    out_bf = adapter_out.astype(BF)
    ranks = 2 * in_bf.shape[2]

    def to_rank(matrix):
        part = jnp.einsum("knq,rn->kqr", matrix, token_part, preferred_element_type=F32)
        return part.reshape(ranks, group_rows)

    reduced = plus_partner(to_rank(in_bf), "ylo", 1)
    row_weight = KEEP_RATE ** staleness.astype(F32)
    rows = rows_by_x(token_batch, cotangent, row_weight[:, None])
    rows, own_weight, own_down, reduced = lax.optimization_barrier(
        (rows, frozen_gate_up_weight, down_weight.T, reduced)
    )
    rows = exchange(rows, "x")

    other_half = swapped(own_weight, "role")
    other_down = swapped(own_down, "role")
    reduced = plus_partner(plus_partner(reduced, "zl", 1), "zl", 2)
    other_half, other_down, reduced = lax.optimization_barrier((other_half, other_down, reduced))
    weights = (own_weight, other_half, swapped(own_weight, "core"), swapped(other_half, "core"))
    reduced = plus_partner(reduced, "zh", 1)
    down_pair = jnp.stack([own_down, other_down])
    downs = (down_pair, swapped(down_pair, "core"))
    rows, reduced = lax.optimization_barrier((rows, reduced))
    pieces = exchange(partials(flags, rows, weights, downs), "x")
    reduced = plus_partner(reduced, "zh", 2).astype(BF)
    base, hidden_old, through_part, out_part = middle(flags, pieces, reduced, out_bf)

    down_first, _ = lax.optimization_barrier((down_pair, pieces))
    through = spread(through_part, NEAR)
    through, down_later = lax.optimization_barrier((through, down_first))
    same_core = [shifted(down_first, "x", 1)]
    same_core += [shifted(down_later, "x", step) for step in (2, 3)]

    through = spread(sum_first(through).astype(BF), "zh")
    through = sum_first(through).astype(BF)
    in_part = ADAPTER_SCALE * jnp.dot(through, token_part, preferred_element_type=F32)
    packed = jnp.concatenate([out_part, in_part.astype(BF)], axis=1)
    packed, same_core = lax.optimization_barrier((packed, same_core))
    grads = spread(packed, ALL_GROUPS)
    blocks = [down_pair, *same_core, downs[1], *(swapped(b, "core") for b in same_core)]
    old_parts = layer_call(old_kernel, group_rows, slice_width, blocks, flags, hidden_old)
    grads, old_parts = lax.optimization_barrier((grads, old_parts))
    grads = sum_first(grads)
    grad_in = grads[:, cols:].reshape(2, -1, slice_width).transpose(0, 2, 1)
    grad_out = grads[:, :cols].reshape(2, -1, cols)
    new_in, new_m_in, new_s_in = adam_update(adapter_in, grad_in, moment_in, square_in)
    new_out, new_m_out, new_s_out = adam_update(adapter_out, grad_out, moment_out, square_out)

    positions = jnp.arange(group_rows)
    live = jnp.logical_or(role == 0, positions < prefill_rows[0])

    def finish(total):
        total = total.astype(BF).T
        return jnp.where(live[:, None], total, jnp.zeros_like(total))

    old_parts = old_parts.reshape(4, 2, 4, slice_width, group_rows)
    side = lax.axis_index("ylo")
    give = swapped(lax.dynamic_index_in_dim(old_parts, 1 - side, 1, keepdims=False), "ylo")
    keep = lax.dynamic_index_in_dim(old_parts, side, 1, keepdims=False)
    pair = (keep.astype(F32) + give.astype(F32)).astype(BF)
    renewed = hidden_total(to_rank(new_in.astype(BF))).astype(BF)
    near_old = shifted_sum(pair, "zl")
    new_parts = layer_call(
        new_kernel, group_rows, slice_width, blocks, flags, base, renewed, new_out.astype(BF)
    )
    near_new = sum_first(exchange(new_parts.reshape(8, 4, slice_width, group_rows), NEAR))
    near = jnp.stack([near_old, near_new], axis=1).astype(BF)
    layers = sum_first(exchange(near, "zh"))
    layer_old, layer_new = finish(layers[0]), finish(layers[1])
    return (
        layer_old[None],
        layer_new[None],
        new_in[None],
        new_out[None],
        new_m_in[None],
        new_s_in[None],
        new_m_out[None],
        new_s_out[None],
    )


def solution(mesh):
    fine = Mesh(mesh.devices.reshape(2, 4, 2, 4, 4, 2), ("role", "x", "core", "zh", "zl", "ylo"))
    wide = ("role", "x", "core")
    in_specs = (
        P("role", DP, None),
        P(DP, None),
        P(DP),
        P(DP),
        P(None, wide, HIDDEN),
        P(HIDDEN, wide),
        P(None, HIDDEN, None),
        P(None, None, HIDDEN),
        P(None, HIDDEN, None),
        P(None, HIDDEN, None),
        P(None, None, HIDDEN),
        P(None, None, HIDDEN),
    )
    out_specs = (
        P("role", DP, HIDDEN),
        P("role", DP, HIDDEN),
        P("role", None, HIDDEN, None),
        P("role", None, None, HIDDEN),
        P("role", None, HIDDEN, None),
        P("role", None, HIDDEN, None),
        P("role", None, None, HIDDEN),
        P("role", None, None, HIDDEN),
    )
    return jax.shard_map(step, mesh=fine, in_specs=in_specs, out_specs=out_specs, check_vma=False)
```

profile of v0, /device:TPU:73, one launch (start us, length us, event | category | flops | bytes accessed | tf_op | source)
XLA Modules:
  0.0 289.4 jit_solution(14647737944255447304)
XLA Ops:
  6.1 3.7 %rows_by_x.1 = bf16[4,2,2,128,640]{4,3,2,1,0:T(8,128)(2,1)} custom-call(bf16[128,5120]{1,0:T(8,128)(2,1)} %bitcast.94, bf16[128,5120]{1,0:T(8,128)(2,1)} %cotangent_ref.1, f32[128,1]{1,0:T(8,128)} %copy.25.scale_ref), custom_call_target="tpu_custom_call" | custom-call | tf_op jit(solution)/shard_map/rows_by_x/pallas_call | solution.py:104
  9.8 4.2 %all-to-all-start = ((bf16[4,2,2,128,640]{4,3,2,1,0:T(8,128)(2,1)}), bf16[4,2,2,128,640]{4,3,2,1,0:T(8,128)(2,1)S(1)}, u32[]{:S(2)}, u32[]{:S(2)}) async-start(bf16[4,2,2,128,640]{4,3,2,1,0:T(8,128)(2,1)} %rows_by_x.1), calls=%async_computation | async-start | bytes 5242880 | tf_op jit(solution)/shard_map/all_to_all | solution.py:34
  13.9 4.2 %collective-permute-start.1 = (bf16[2,320,432]{2,1,0:T(8,128)(2,1)}, bf16[2,320,432]{2,1,0:T(8,128)(2,1)}, u32[]{:S(2)}, u32[]{:S(2)}) collective-permute-start(bf16[2,320,432]{2,1,0:T(8,128)(2,1)} %refs_0_), channel_id=1, source_target_pairs={{0,256},{256,0},{1,257},{257,1},{2,258},{258,2},{3,259},{259,3},{4... | collective-permute-start | bytes 1658888 | tf_op jit(solution)/shard_map/ppermute | solution.py:38
  20.7 3.5 %collective-permute-start.3 = (f32[64,128]{1,0:T(8,128)S(1)}, f32[64,128]{1,0:T(8,128)S(1)}, u32[]{:S(2)}, u32[]{:S(2)}) collective-permute-start(f32[64,128]{1,0:T(8,128)S(1)} %add.93), channel_id=1, source_target_pairs={{0,2},{2,0},{4,6},{6,4},{1,3},{3,1},{5,7},{7,5},{8,10},{10,8},{12,... | collective-permute-start | bytes 98312 | tf_op jit(solution)/shard_map/ppermute | solution.py:62
  27.9 8.8 %collective-permute-start.6 = (bf16[2,320,432]{2,1,0:T(8,128)(2,1)}, bf16[2,320,432]{2,1,0:T(8,128)(2,1)}, u32[]{:S(2)}, u32[]{:S(2)}) collective-permute-start(bf16[2,320,432]{2,1,0:T(8,128)(2,1)} %refs_0_), channel_id=1, source_target_pairs={{0,32},{32,0},{1,33},{33,1},{2,34},{34,2},{3,35},{35,3},{4,36},{36... | collective-permute-start | bytes 1658888 | tf_op jit(solution)/shard_map/ppermute | solution.py:38
  36.7 2.9 collective-permute-done.2
  39.6 4.0 %collective-permute-start.7 = (bf16[2,320,432]{2,1,0:T(8,128)(2,1)}, bf16[2,320,432]{2,1,0:T(8,128)(2,1)}, u32[]{:S(2)}, u32[]{:S(2)}) collective-permute-start(bf16[2,320,432]{2,1,0:T(8,128)(2,1)} %collective-permute-done.1.refs_1_), channel_id=1, source_target_pairs={{0,32},{32,0},{1,33},{33,1},{2,34},{34,2},{3,35},{35,3},{4,36},{36... | collective-permute-start | bytes 1658888 | tf_op jit(solution)/shard_map/ppermute | solution.py:38
  46.6 8.8 %collective-permute-start.5 = (f32[64,128]{1,0:T(8,128)S(1)}, f32[64,128]{1,0:T(8,128)S(1)}, u32[]{:S(2)}, u32[]{:S(2)}) collective-permute-start(f32[64,128]{1,0:T(8,128)S(1)} %add.95), channel_id=1, source_target_pairs={{0,8},{8,0},{16,24},{24,16},{1,9},{9,1},{17,25},{25,17},{2,10},{10... | collective-permute-start | bytes 98312 | tf_op jit(solution)/shard_map/ppermute | solution.py:62
  58.2 6.8 %partials.1 = bf16[4,3,432,128]{3,2,1,0:T(8,128)(2,1)} custom-call(s32[3]{0:T(128)} %pad_add_fusion.flag_ref, bf16[4,2,2,128,640]{4,3,2,1,0:T(8,128)(2,1)} %copy-done, bf16[2,320,432]{2,1,0:T(8,128)(2,1)} %refs_0_, bf16[2,320,432]{2,1,0:T(8,128)(2,1)} %collective-permute-done.1.refs_1_, bf16[2,320,432]{2,1,0:T(8,128)(2,1)} %collective-permute-done.6.refs_2_, ...), custom_call_target="tpu_custom_call" | custom-call | tf_op jit(solution)/shard_map/partials/pallas_call | solution.py:158
  65.1 4.4 %all-to-all-start.1 = ((bf16[4,3,432,128]{3,2,1,0:T(8,128)(2,1)}), bf16[4,3,432,128]{3,2,1,0:T(8,128)(2,1)S(1)}, u32[]{:S(2)}, u32[]{:S(2)}) async-start(bf16[4,3,432,128]{3,2,1,0:T(8,128)(2,1)} %partials.1), calls=%async_computation.1 | async-start | bytes 2654208 | tf_op jit(solution)/shard_map/all_to_all | solution.py:34
  69.5 12.2 %collective-permute-start.9 = (f32[64,128]{1,0:T(8,128)S(1)}, f32[64,128]{1,0:T(8,128)S(1)}, u32[]{:S(2)}, u32[]{:S(2)}) collective-permute-start(f32[64,128]{1,0:T(8,128)S(1)} %add.96), channel_id=1, source_target_pairs={{0,16},{8,24},{16,0},{24,8},{1,17},{9,25},{17,1},{25,9},{2,18},{10... | collective-permute-start | bytes 98312 | tf_op jit(solution)/shard_map/ppermute | solution.py:62
  87.1 2.6 middle.1
  91.1 7.2 %all-to-all-start.2 = ((bf16[8,64,128]{2,1,0:T(8,128)(2,1)}), bf16[8,64,128]{2,1,0:T(8,128)(2,1)S(1)}, u32[]{:S(2)}, u32[]{:S(2)}) async-start(bf16[8,64,128]{2,1,0:T(8,128)(2,1)} %broadcast_in_dim.57), calls=%async_computation.2 | async-start | bytes 262144 | tf_op jit(solution)/shard_map/all_to_all | solution.py:34
  101.0 3.2 %collective-permute-start.11 = (bf16[2,320,432]{2,1,0:T(8,128)(2,1)S(1)}, bf16[2,320,432]{2,1,0:T(8,128)(2,1)S(1)}, u32[]{:S(2)}, u32[]{:S(2)}) collective-permute-start(bf16[2,320,432]{2,1,0:T(8,128)(2,1)S(1)} %copy-done.2), channel_id=1, source_target_pairs={{0,128},{64,192},{128,0},{192,64},{1,129},{65,193},{129,1},{193,65... | collective-permute-start | bytes 1658888 | tf_op jit(solution)/shard_map/ppermute | solution.py:57
  104.2 3.3 %collective-permute-start.12 = (bf16[2,320,432]{2,1,0:T(8,128)(2,1)S(1)}, bf16[2,320,432]{2,1,0:T(8,128)(2,1)S(1)}, u32[]{:S(2)}, u32[]{:S(2)}) collective-permute-start(bf16[2,320,432]{2,1,0:T(8,128)(2,1)S(1)} %copy-done.2), channel_id=1, source_target_pairs={{0,192},{64,0},{128,64},{192,128},{1,193},{65,1},{129,65},{193,129... | collective-permute-start | bytes 1658888 | tf_op jit(solution)/shard_map/ppermute | solution.py:57
  107.6 21.1 %all_to_all.45 = bf16[4,64,128]{2,1,0:T(8,128)(2,1)S(1)} all-to-all(bf16[4,64,128]{2,1,0:T(8,128)(2,1)S(1)} %broadcast_in_dim.58), channel_id=1, replica_groups=mesh['role'=2,'x'=4,'core'=2,'zh'=4,'zl'=4,'ylo'=2] {'zh'}, dimensions={0} | all-to-all | bytes 131072 | tf_op jit(solution)/shard_map/all_to_all | solution.py:34
  130.8 2.8 collective-permute-done.12.refs_3_
  135.0 9.2 %all-to-all-start.4 = ((bf16[16,64,592]{2,1,0:T(8,128)(2,1)}), bf16[16,64,592]{2,1,0:T(8,128)(2,1)S(1)}, u32[]{:S(2)}, u32[]{:S(2)}) async-start(bf16[16,64,592]{2,1,0:T(8,128)(2,1)} %broadcast_in_dim.59), calls=%async_computation.4 | async-start | bytes 2621440 | tf_op jit(solution)/shard_map/all_to_all | solution.py:34
  153.4 5.1 %shard_map.179 = bf16[32,160,128]{2,1,0:T(8,128)(2,1)} custom-call(s32[3]{0:T(128)} %pad_add_fusion.flag_ref, bf16[432,128]{1,0:T(8,128)(2,1)} %get-tuple-element.45.hidden_ref, bf16[2,320,432]{2,1,0:T(8,128)(2,1)} %copy-done.1, bf16[2,320,432]{2,1,0:T(8,128)(2,1)} %copy-done.5, bf16[2,320,432]{2,1,0:T(8,128)(2,1)} %copy-done.6, ...), custom_call_target="tpu_custom_call" | custom-call | tf_op jit(solution)/shard_map/pallas_call | solution.py:250
  158.5 5.7 %all-to-all-done.4 = bf16[16,64,592]{2,1,0:T(8,128)(2,1)S(1)} async-done(((bf16[16,64,592]{2,1,0:T(8,128)(2,1)}), bf16[16,64,592]{2,1,0:T(8,128)(2,1)S(1)}, u32[]{:S(2)}, u32[]{:S(2)}) %all-to-all-start.4) | async-done | bytes 1212448 | tf_op jit(solution)/shard_map/all_to_all | solution.py:34
  167.1 7.2 %all-to-all-start.5 = ((bf16[8,64,128]{2,1,0:T(8,128)(2,1)}), bf16[8,64,128]{2,1,0:T(8,128)(2,1)S(1)}, u32[]{:S(2)}, u32[]{:S(2)}) async-start(bf16[8,64,128]{2,1,0:T(8,128)(2,1)} %broadcast_in_dim.60), calls=%async_computation.5 | async-start | bytes 262144 | tf_op jit(solution)/shard_map/all_to_all | solution.py:34
  174.3 3.0 %all-to-all-done.5 = bf16[8,64,128]{2,1,0:T(8,128)(2,1)S(1)} async-done(((bf16[8,64,128]{2,1,0:T(8,128)(2,1)}), bf16[8,64,128]{2,1,0:T(8,128)(2,1)S(1)}, u32[]{:S(2)}, u32[]{:S(2)}) %all-to-all-start.5) | async-done | bytes 131104 | tf_op jit(solution)/shard_map/all_to_all | solution.py:34
  177.9 6.6 %all-to-all-start.6 = ((bf16[4,64,128]{2,1,0:T(8,128)(2,1)}), bf16[4,64,128]{2,1,0:T(8,128)(2,1)S(1)}, u32[]{:S(2)}, u32[]{:S(2)}) async-start(bf16[4,64,128]{2,1,0:T(8,128)(2,1)} %broadcast_in_dim.61), calls=%async_computation.6 | async-start | bytes 131072 | tf_op jit(solution)/shard_map/all_to_all | solution.py:34
  185.4 11.1 %all-to-all-done.6 = bf16[4,64,128]{2,1,0:T(8,128)(2,1)S(1)} async-done(((bf16[4,64,128]{2,1,0:T(8,128)(2,1)}), bf16[4,64,128]{2,1,0:T(8,128)(2,1)S(1)}, u32[]{:S(2)}, u32[]{:S(2)}) %all-to-all-start.6) | async-done | bytes 65568 | tf_op jit(solution)/shard_map/all_to_all | solution.py:34
  197.1 5.6 %shard_map.180 = bf16[32,160,128]{2,1,0:T(8,128)(2,1)} custom-call(s32[3]{0:T(128)} %pad_add_fusion.flag_ref, f32[2,432,128]{2,1,0:T(8,128)} %get-tuple-element.50.base_ref, bf16[64,128]{1,0:T(8,128)(2,1)} %reduce_sum.79.reduced_ref, bf16[2,32,432]{2,1,0:T(8,128)(2,1)} %get-tuple-element.52.lift_ref, bf16[2,320,432]{2,1,0:T(8,128)(2,1)} %copy-done.1, ...), custom_call_target="tpu_custom_call" | custom-call | tf_op jit(solution)/shard_map/pallas_call | solution.py:250
  202.7 7.7 %all-to-all-start.7 = ((bf16[8,4,160,128]{3,2,1,0:T(8,128)(2,1)}), bf16[8,4,160,128]{3,2,1,0:T(8,128)(2,1)S(1)}, u32[]{:S(2)}, u32[]{:S(2)}) async-start(bf16[8,4,160,128]{3,2,1,0:T(8,128)(2,1)} %bitcast.91), calls=%async_computation.7 | async-start | bytes 2621440 | tf_op jit(solution)/shard_map/all_to_all | solution.py:34
  212.6 26.7 %collective-permute-done.16 = bf16[4,4,160,128]{3,2,1,0:T(8,128)(2,1)} collective-permute-done((bf16[4,4,160,128]{3,2,1,0:T(8,128)(2,1)S(1)}, bf16[4,4,160,128]{3,2,1,0:T(8,128)(2,1)}, u32[]{:S(2)}, u32[]{:S(2)}) %collective-permute-start.16) | collective-permute-done | bytes 655392 | tf_op jit(solution)/shard_map/ppermute | solution.py:38
  242.8 5.6 %collective-permute-start.18 = (bf16[4,160,128]{2,1,0:T(8,128)(2,1)S(1)}, bf16[4,160,128]{2,1,0:T(8,128)(2,1)S(1)}, u32[]{:S(2)}, u32[]{:S(2)}) collective-permute-start(bf16[4,160,128]{2,1,0:T(8,128)(2,1)S(1)} %get-tuple-element.58), channel_id=1, source_target_pairs={{0,4},{2,6},{4,0},{6,2},{1,5},{3,7},{5,1},{7,3},{8,12},{10,14},{12... | collective-permute-start | bytes 491528 | tf_op jit(solution)/shard_map/ppermute | solution.py:57
  250.3 7.5 %collective-permute-done.18 = bf16[4,160,128]{2,1,0:T(8,128)(2,1)S(1)} collective-permute-done((bf16[4,160,128]{2,1,0:T(8,128)(2,1)S(1)}, bf16[4,160,128]{2,1,0:T(8,128)(2,1)S(1)}, u32[]{:S(2)}, u32[]{:S(2)}) %collective-permute-start.18) | collective-permute-done | bytes 163872 | tf_op jit(solution)/shard_map/ppermute | solution.py:57
  257.8 3.9 %collective-permute-done.17 = bf16[4,160,128]{2,1,0:T(8,128)(2,1)S(1)} collective-permute-done((bf16[4,160,128]{2,1,0:T(8,128)(2,1)S(1)}, bf16[4,160,128]{2,1,0:T(8,128)(2,1)S(1)}, u32[]{:S(2)}, u32[]{:S(2)}) %collective-permute-start.17) | collective-permute-done | bytes 163872 | tf_op jit(solution)/shard_map/ppermute | solution.py:57
  262.7 3.5 %all-to-all-start.8 = ((bf16[4,2,160,128]{3,2,1,0:T(8,128)(2,1)}), bf16[4,2,160,128]{3,2,1,0:T(8,128)(2,1)S(1)}, u32[]{:S(2)}, u32[]{:S(2)}) async-start(bf16[4,2,160,128]{3,2,1,0:T(8,128)(2,1)} %pad_maximum_fusion.1), calls=%async_computation.8 | async-start | bytes 655360 | tf_op jit(solution)/shard_map/all_to_all | solution.py:34
  266.9 21.8 %all-to-all-done.8 = bf16[4,2,160,128]{3,2,1,0:T(8,128)(2,1)S(1)} async-done(((bf16[4,2,160,128]{3,2,1,0:T(8,128)(2,1)}), bf16[4,2,160,128]{3,2,1,0:T(8,128)(2,1)S(1)}, u32[]{:S(2)}, u32[]{:S(2)}) %all-to-all-start.8) | async-done | bytes 327712 | tf_op jit(solution)/shard_map/all_to_all | solution.py:34
  (104 shorter events, 53.6 us)
Async XLA Ops:
  2.6 7.2 %collective-permute-start = (f32[64,128]{1,0:T(8,128)S(1)}, f32[64,128]{1,0:T(8,128)S(1)}, u32[]{:S(2)}, u32[]{:S(2)}) collective-permute-start(f32[64,128]{1,0:T(8,128)S(1)} %convolution_bitcast_fusion), channel_id=1, source_target_pairs={{0,1},{1,0},{2,3},{3,2},{4,5},{5,4},{6,7},{7,6},{8,9},{9,8},{10,11... | collective-permute-start | bytes 98312 | tf_op jit(solution)/shard_map/ppermute | solution.py:62
  9.8 47.0 %all-to-all-start = ((bf16[4,2,2,128,640]{4,3,2,1,0:T(8,128)(2,1)}), bf16[4,2,2,128,640]{4,3,2,1,0:T(8,128)(2,1)S(1)}, u32[]{:S(2)}, u32[]{:S(2)}) async-start(bf16[4,2,2,128,640]{4,3,2,1,0:T(8,128)(2,1)} %rows_by_x.1), calls=%async_computation | async-start | bytes 5242880 | tf_op jit(solution)/shard_map/all_to_all | solution.py:34
  13.9 25.7 %collective-permute-start.1 = (bf16[2,320,432]{2,1,0:T(8,128)(2,1)}, bf16[2,320,432]{2,1,0:T(8,128)(2,1)}, u32[]{:S(2)}, u32[]{:S(2)}) collective-permute-start(bf16[2,320,432]{2,1,0:T(8,128)(2,1)} %refs_0_), channel_id=1, source_target_pairs={{0,256},{256,0},{1,257},{257,1},{2,258},{258,2},{3,259},{259,3},{4... | collective-permute-start | bytes 1658888 | tf_op jit(solution)/shard_map/ppermute | solution.py:38
  18.2 21.4 %collective-permute-start.2 = (bf16[320,432]{1,0:T(8,128)(2,1)S(1)}, bf16[320,432]{1,0:T(8,128)(2,1)S(1)}, u32[]{:S(2)}, u32[]{:S(2)}) collective-permute-start(bf16[320,432]{1,0:T(8,128)(2,1)S(1)} %bitcast.98), channel_id=1, source_target_pairs={{0,256},{256,0},{1,257},{257,1},{2,258},{258,2},{3,259},{259,3},{4... | collective-permute-start | bytes 829448 | tf_op jit(solution)/shard_map/ppermute | solution.py:38
  20.7 5.2 %collective-permute-start.3 = (f32[64,128]{1,0:T(8,128)S(1)}, f32[64,128]{1,0:T(8,128)S(1)}, u32[]{:S(2)}, u32[]{:S(2)}) collective-permute-start(f32[64,128]{1,0:T(8,128)S(1)} %add.93), channel_id=1, source_target_pairs={{0,2},{2,0},{4,6},{6,4},{1,3},{3,1},{5,7},{7,5},{8,10},{10,8},{12,... | collective-permute-start | bytes 98312 | tf_op jit(solution)/shard_map/ppermute | solution.py:62
  26.0 10.7 %collective-permute-start.4 = (f32[64,128]{1,0:T(8,128)S(1)}, f32[64,128]{1,0:T(8,128)S(1)}, u32[]{:S(2)}, u32[]{:S(2)}) collective-permute-start(f32[64,128]{1,0:T(8,128)S(1)} %add.94), channel_id=1, source_target_pairs={{0,4},{2,6},{4,0},{6,2},{1,5},{3,7},{5,1},{7,3},{8,12},{10,14},{12... | collective-permute-start | bytes 98312 | tf_op jit(solution)/shard_map/ppermute | solution.py:62
  27.9 28.8 %collective-permute-start.6 = (bf16[2,320,432]{2,1,0:T(8,128)(2,1)}, bf16[2,320,432]{2,1,0:T(8,128)(2,1)}, u32[]{:S(2)}, u32[]{:S(2)}) collective-permute-start(bf16[2,320,432]{2,1,0:T(8,128)(2,1)} %refs_0_), channel_id=1, source_target_pairs={{0,32},{32,0},{1,33},{33,1},{2,34},{34,2},{3,35},{35,3},{4,36},{36... | collective-permute-start | bytes 1658888 | tf_op jit(solution)/shard_map/ppermute | solution.py:38
  39.6 17.1 %collective-permute-start.7 = (bf16[2,320,432]{2,1,0:T(8,128)(2,1)}, bf16[2,320,432]{2,1,0:T(8,128)(2,1)}, u32[]{:S(2)}, u32[]{:S(2)}) collective-permute-start(bf16[2,320,432]{2,1,0:T(8,128)(2,1)} %collective-permute-done.1.refs_1_), channel_id=1, source_target_pairs={{0,32},{32,0},{1,33},{33,1},{2,34},{34,2},{3,35},{35,3},{4,36},{36... | collective-permute-start | bytes 1658888 | tf_op jit(solution)/shard_map/ppermute | solution.py:38
  44.7 12.1 %collective-permute-start.8 = (bf16[2,320,432]{2,1,0:T(8,128)(2,1)S(1)}, bf16[2,320,432]{2,1,0:T(8,128)(2,1)}, u32[]{:S(2)}, u32[]{:S(2)}) collective-permute-start(bf16[2,320,432]{2,1,0:T(8,128)(2,1)S(1)} %pad_maximum_fusion.refs_4_.refs_0_), channel_id=1, source_target_pairs={{0,32},{32,0},{1,33},{33,1},{2,34},{34,2},{3,35},{35,3},{4,36},{36... | collective-permute-start | bytes 1658888 | tf_op jit(solution)/shard_map/ppermute | solution.py:38
  46.6 10.1 %collective-permute-start.5 = (f32[64,128]{1,0:T(8,128)S(1)}, f32[64,128]{1,0:T(8,128)S(1)}, u32[]{:S(2)}, u32[]{:S(2)}) collective-permute-start(f32[64,128]{1,0:T(8,128)S(1)} %add.95), channel_id=1, source_target_pairs={{0,8},{8,0},{16,24},{24,16},{1,9},{9,1},{17,25},{25,17},{2,10},{10... | collective-permute-start | bytes 98312 | tf_op jit(solution)/shard_map/ppermute | solution.py:62
  65.1 16.6 %copy-start.11 = (f32[2,32,432]{2,1,0:T(8,128)S(1)}, f32[2,32,432]{2,1,0:T(8,128)}, u32[]{:S(2)}) copy-start(f32[2,32,432]{2,1,0:T(8,128)} %param.19) | copy-start | bytes 331780
  65.1 20.9 %all-to-all-start.1 = ((bf16[4,3,432,128]{3,2,1,0:T(8,128)(2,1)}), bf16[4,3,432,128]{3,2,1,0:T(8,128)(2,1)S(1)}, u32[]{:S(2)}, u32[]{:S(2)}) async-start(bf16[4,3,432,128]{3,2,1,0:T(8,128)(2,1)} %partials.1), calls=%async_computation.1 | async-start | bytes 2654208 | tf_op jit(solution)/shard_map/all_to_all | solution.py:34
  69.5 28.9 %copy-start.2 = (bf16[2,320,432]{2,1,0:T(8,128)(2,1)S(1)}, bf16[2,320,432]{2,1,0:T(8,128)(2,1)}, u32[]{:S(2)}) copy-start(bf16[2,320,432]{2,1,0:T(8,128)(2,1)} %copy-done.1) | copy-start | bytes 1658884
  69.5 13.5 %collective-permute-start.9 = (f32[64,128]{1,0:T(8,128)S(1)}, f32[64,128]{1,0:T(8,128)S(1)}, u32[]{:S(2)}, u32[]{:S(2)}) collective-permute-start(f32[64,128]{1,0:T(8,128)S(1)} %add.96), channel_id=1, source_target_pairs={{0,16},{8,24},{16,0},{24,8},{1,17},{9,25},{17,1},{25,9},{2,18},{10... | collective-permute-start | bytes 98312 | tf_op jit(solution)/shard_map/ppermute | solution.py:62
  91.1 9.9 %all-to-all-start.2 = ((bf16[8,64,128]{2,1,0:T(8,128)(2,1)}), bf16[8,64,128]{2,1,0:T(8,128)(2,1)S(1)}, u32[]{:S(2)}, u32[]{:S(2)}) async-start(bf16[8,64,128]{2,1,0:T(8,128)(2,1)} %broadcast_in_dim.57), calls=%async_computation.2 | async-start | bytes 262144 | tf_op jit(solution)/shard_map/all_to_all | solution.py:34
  98.3 32.4 %collective-permute-start.10 = (bf16[2,320,432]{2,1,0:T(8,128)(2,1)S(1)}, bf16[2,320,432]{2,1,0:T(8,128)(2,1)S(1)}, u32[]{:S(2)}, u32[]{:S(2)}) collective-permute-start(bf16[2,320,432]{2,1,0:T(8,128)(2,1)S(1)} %copy-done.2), channel_id=1, source_target_pairs={{0,64},{64,128},{128,192},{192,0},{1,65},{65,129},{129,193},{193,1... | collective-permute-start | bytes 1658888 | tf_op jit(solution)/shard_map/ppermute | solution.py:57
  101.0 29.7 %collective-permute-start.11 = (bf16[2,320,432]{2,1,0:T(8,128)(2,1)S(1)}, bf16[2,320,432]{2,1,0:T(8,128)(2,1)S(1)}, u32[]{:S(2)}, u32[]{:S(2)}) collective-permute-start(bf16[2,320,432]{2,1,0:T(8,128)(2,1)S(1)} %copy-done.2), channel_id=1, source_target_pairs={{0,128},{64,192},{128,0},{192,64},{1,129},{65,193},{129,1},{193,65... | collective-permute-start | bytes 1658888 | tf_op jit(solution)/shard_map/ppermute | solution.py:57
  104.2 29.4 %collective-permute-start.12 = (bf16[2,320,432]{2,1,0:T(8,128)(2,1)S(1)}, bf16[2,320,432]{2,1,0:T(8,128)(2,1)S(1)}, u32[]{:S(2)}, u32[]{:S(2)}) collective-permute-start(bf16[2,320,432]{2,1,0:T(8,128)(2,1)S(1)} %copy-done.2), channel_id=1, source_target_pairs={{0,192},{64,0},{128,64},{192,128},{1,193},{65,1},{129,65},{193,129... | collective-permute-start | bytes 1658888 | tf_op jit(solution)/shard_map/ppermute | solution.py:57
  135.0 29.3 %all-to-all-start.4 = ((bf16[16,64,592]{2,1,0:T(8,128)(2,1)}), bf16[16,64,592]{2,1,0:T(8,128)(2,1)S(1)}, u32[]{:S(2)}, u32[]{:S(2)}) async-start(bf16[16,64,592]{2,1,0:T(8,128)(2,1)} %broadcast_in_dim.59), calls=%async_computation.4 | async-start | bytes 2621440 | tf_op jit(solution)/shard_map/all_to_all | solution.py:34
  144.2 6.4 %collective-permute-start.13 = (bf16[2,320,432]{2,1,0:T(8,128)(2,1)S(1)}, bf16[2,320,432]{2,1,0:T(8,128)(2,1)S(1)}, u32[]{:S(2)}, u32[]{:S(2)}) collective-permute-start(bf16[2,320,432]{2,1,0:T(8,128)(2,1)S(1)} %collective-permute-done.10.refs_1_), channel_id=1, source_target_pairs={{0,32},{32,0},{1,33},{33,1},{2,34},{34,2},{3,35},{35,3},{4,36},{36... | collective-permute-start | bytes 1658888 | tf_op jit(solution)/shard_map/ppermute | solution.py:38
  146.2 4.4 %collective-permute-start.14 = (bf16[2,320,432]{2,1,0:T(8,128)(2,1)S(1)}, bf16[2,320,432]{2,1,0:T(8,128)(2,1)S(1)}, u32[]{:S(2)}, u32[]{:S(2)}) collective-permute-start(bf16[2,320,432]{2,1,0:T(8,128)(2,1)S(1)} %collective-permute-done.11.refs_2_), channel_id=1, source_target_pairs={{0,32},{32,0},{1,33},{33,1},{2,34},{34,2},{3,35},{35,3},{4,36},{36... | collective-permute-start | bytes 1658888 | tf_op jit(solution)/shard_map/ppermute | solution.py:38
  148.6 4.0 %collective-permute-start.15 = (bf16[2,320,432]{2,1,0:T(8,128)(2,1)S(1)}, bf16[2,320,432]{2,1,0:T(8,128)(2,1)S(1)}, u32[]{:S(2)}, u32[]{:S(2)}) collective-permute-start(bf16[2,320,432]{2,1,0:T(8,128)(2,1)S(1)} %collective-permute-done.12.refs_3_), channel_id=1, source_target_pairs={{0,32},{32,0},{1,33},{33,1},{2,34},{34,2},{3,35},{35,3},{4,36},{36... | collective-permute-start | bytes 1658888 | tf_op jit(solution)/shard_map/ppermute | solution.py:38
  158.5 26.0 %copy-start.14 = (f32[2,32,432]{2,1,0:T(8,128)S(1)}, f32[2,32,432]{2,1,0:T(8,128)}, u32[]{:S(2)}) copy-start(f32[2,32,432]{2,1,0:T(8,128)} %param.23) | copy-start | bytes 331780
  158.5 26.0 %copy-start.15 = (f32[2,32,432]{2,1,0:T(8,128)S(1)}, f32[2,32,432]{2,1,0:T(8,128)}, u32[]{:S(2)}) copy-start(f32[2,32,432]{2,1,0:T(8,128)} %param.22) | copy-start | bytes 331780
  167.1 10.2 %all-to-all-start.5 = ((bf16[8,64,128]{2,1,0:T(8,128)(2,1)}), bf16[8,64,128]{2,1,0:T(8,128)(2,1)S(1)}, u32[]{:S(2)}, u32[]{:S(2)}) async-start(bf16[8,64,128]{2,1,0:T(8,128)(2,1)} %broadcast_in_dim.60), calls=%async_computation.5 | async-start | bytes 262144 | tf_op jit(solution)/shard_map/all_to_all | solution.py:34
  177.9 18.5 %all-to-all-start.6 = ((bf16[4,64,128]{2,1,0:T(8,128)(2,1)}), bf16[4,64,128]{2,1,0:T(8,128)(2,1)S(1)}, u32[]{:S(2)}, u32[]{:S(2)}) async-start(bf16[4,64,128]{2,1,0:T(8,128)(2,1)} %broadcast_in_dim.61), calls=%async_computation.6 | async-start | bytes 131072 | tf_op jit(solution)/shard_map/all_to_all | solution.py:34
  202.7 59.1 %all-to-all-start.7 = ((bf16[8,4,160,128]{3,2,1,0:T(8,128)(2,1)}), bf16[8,4,160,128]{3,2,1,0:T(8,128)(2,1)S(1)}, u32[]{:S(2)}, u32[]{:S(2)}) async-start(bf16[8,4,160,128]{3,2,1,0:T(8,128)(2,1)} %bitcast.91), calls=%async_computation.7 | async-start | bytes 2621440 | tf_op jit(solution)/shard_map/all_to_all | solution.py:34
  210.4 29.0 %collective-permute-start.16 = (bf16[4,4,160,128]{3,2,1,0:T(8,128)(2,1)S(1)}, bf16[4,4,160,128]{3,2,1,0:T(8,128)(2,1)}, u32[]{:S(2)}, u32[]{:S(2)}) collective-permute-start(bf16[4,4,160,128]{3,2,1,0:T(8,128)(2,1)S(1)} %dynamic-slice_bitcast_fusion), channel_id=1, source_target_pairs={{0,1},{1,0},{2,3},{3,2},{4,5},{5,4},{6,7},{7,6},{8,9},{9,8},{10,11... | collective-permute-start | bytes 1966088 | tf_op jit(solution)/shard_map/ppermute | solution.py:38
  240.7 9.6 %collective-permute-start.19 = (bf16[4,160,128]{2,1,0:T(8,128)(2,1)S(1)}, bf16[4,160,128]{2,1,0:T(8,128)(2,1)S(1)}, u32[]{:S(2)}, u32[]{:S(2)}) collective-permute-start(bf16[4,160,128]{2,1,0:T(8,128)(2,1)S(1)} %get-tuple-element.57), channel_id=1, source_target_pairs={{0,6},{2,0},{4,2},{6,4},{1,7},{3,1},{5,3},{7,5},{8,14},{10,8},{12,... | collective-permute-start | bytes 491528 | tf_op jit(solution)/shard_map/ppermute | solution.py:57
  242.8 15.0 %collective-permute-start.18 = (bf16[4,160,128]{2,1,0:T(8,128)(2,1)S(1)}, bf16[4,160,128]{2,1,0:T(8,128)(2,1)S(1)}, u32[]{:S(2)}, u32[]{:S(2)}) collective-permute-start(bf16[4,160,128]{2,1,0:T(8,128)(2,1)S(1)} %get-tuple-element.58), channel_id=1, source_target_pairs={{0,4},{2,6},{4,0},{6,2},{1,5},{3,7},{5,1},{7,3},{8,12},{10,14},{12... | collective-permute-start | bytes 491528 | tf_op jit(solution)/shard_map/ppermute | solution.py:57
  248.4 13.3 %collective-permute-start.17 = (bf16[4,160,128]{2,1,0:T(8,128)(2,1)S(1)}, bf16[4,160,128]{2,1,0:T(8,128)(2,1)S(1)}, u32[]{:S(2)}, u32[]{:S(2)}) collective-permute-start(bf16[4,160,128]{2,1,0:T(8,128)(2,1)S(1)} %get-tuple-element.56), channel_id=1, source_target_pairs={{0,2},{2,4},{4,6},{6,0},{1,3},{3,5},{5,7},{7,1},{8,10},{10,12},{12... | collective-permute-start | bytes 491528 | tf_op jit(solution)/shard_map/ppermute | solution.py:57
  262.7 26.0 %all-to-all-start.8 = ((bf16[4,2,160,128]{3,2,1,0:T(8,128)(2,1)}), bf16[4,2,160,128]{3,2,1,0:T(8,128)(2,1)S(1)}, u32[]{:S(2)}, u32[]{:S(2)}) async-start(bf16[4,2,160,128]{3,2,1,0:T(8,128)(2,1)} %pad_maximum_fusion.1), calls=%async_computation.8 | async-start | bytes 655360 | tf_op jit(solution)/shard_map/all_to_all | solution.py:34
  (14 other events, 97.6 us)
where the time goes:
time: 291 us; the launch traced here: 289 us
  starting transfers between devices  127 us (44%)
  waiting for transfers between devices  93.3 us (32%)
  Pallas kernels  23.8 us (8%)
  blocking collectives  21.1 us (7%)
  other arithmetic  10.8 us (4%)
  local copies, waits for them, and re-layouts  8.45 us (3%)
  matrix products  3.31 us (1%)
    all_to_all x8, starting transfers between devices, exchange(): return lax.all_to_all(pieces, axis, split_axis=0, concat_axis=0, tiled=True)  50 us
    all_to_all x8, waiting for transfers between devices, exchange(): return lax.all_to_all(pieces, axis, split_axis=0, concat_axis=0, tiled=True)  44.5 us
    ppermute x9, waiting for transfers between devices, swapped(): return lax.ppermute(value, axis, [(0, 1), (1, 0)])  31.6 us
    ppermute x9, starting transfers between devices, swapped(): return lax.ppermute(value, axis, [(0, 1), (1, 0)])  30 us
    ppermute x5, starting transfers between devices, plus_partner(): lax.ppermute(value, axis, [(i, i ^ step) for i in range(count)])  28.6 us
    all_to_all x1, blocking collectives, exchange(): return lax.all_to_all(pieces, axis, split_axis=0, concat_axis=0, tiled=True)  21.1 us
    ppermute x6, starting transfers between devices, shifted(): lax.ppermute(value, axis, [(i, (i + step) % count) for i in range(count)])  18.2 us
    ppermute x6, waiting for transfers between devices, shifted(): lax.ppermute(value, axis, [(i, (i + step) % count) for i in range(count)])  14.2 us
  transfers between devices with their start and end apart: 28, of which 15 were waited for; matrix products, arithmetic and copies ran while one was open for 3% of the time, Pallas kernels for 3%

commit v1 on v0

--- a/solution.py
+++ b/solution.py
@@ -18,7 +18,6 @@
 KEEP_RATE = 0.75
 
 DP = ("x", "core")
-ALL_GROUPS = ("role", "x", "core")
 NEAR = ("zl", "ylo")
 HIDDEN = ("zh", "zl", "ylo")
 BF = jnp.bfloat16
@@ -45,11 +44,6 @@
 
 def sum_first(pieces):
     return pieces.astype(F32).sum(axis=0)
-
-
-def hidden_total(value):
-    near = sum_first(spread(value.astype(BF), NEAR)).astype(BF)
-    return sum_first(spread(near, "zh"))
 
 
 def shifted(value, axis, step):
@@ -290,37 +284,41 @@
     reduced = plus_partner(to_rank(in_bf), "ylo", 1)
     row_weight = KEEP_RATE ** staleness.astype(F32)
     rows = rows_by_x(token_batch, cotangent, row_weight[:, None])
-    rows, own_weight, own_down, reduced = lax.optimization_barrier(
-        (rows, frozen_gate_up_weight, down_weight.T, reduced)
-    )
     rows = exchange(rows, "x")
+    own_weight, own_down, reduced = lax.optimization_barrier((frozen_gate_up_weight, down_weight.T, reduced))
 
     other_half = swapped(own_weight, "role")
     other_down = swapped(own_down, "role")
     reduced = plus_partner(plus_partner(reduced, "zl", 1), "zl", 2)
     other_half, other_down, reduced = lax.optimization_barrier((other_half, other_down, reduced))
     weights = (own_weight, other_half, swapped(own_weight, "core"), swapped(other_half, "core"))
-    reduced = plus_partner(reduced, "zh", 1)
     down_pair = jnp.stack([own_down, other_down])
     downs = (down_pair, swapped(down_pair, "core"))
     rows, reduced = lax.optimization_barrier((rows, reduced))
     pieces = exchange(partials(flags, rows, weights, downs), "x")
-    reduced = plus_partner(reduced, "zh", 2).astype(BF)
+    reduced = plus_partner(plus_partner(reduced, "zh", 1), "zh", 2).astype(BF)
     base, hidden_old, through_part, out_part = middle(flags, pieces, reduced, out_bf)
 
     down_first, _ = lax.optimization_barrier((down_pair, pieces))
-    through = spread(through_part, NEAR)
-    through, down_later = lax.optimization_barrier((through, down_first))
-    same_core = [shifted(down_first, "x", 1)]
-    same_core += [shifted(down_later, "x", step) for step in (2, 3)]
-
-    through = spread(sum_first(through).astype(BF), "zh")
+    through = sum_first(spread(through_part, NEAR)).astype(BF)
+    through = spread(through, "zh")
     through = sum_first(through).astype(BF)
+    behind, ahead = shifted(down_first, "x", 1), shifted(down_first, "x", 3)
+    across = jnp.stack([shifted(behind[0], "x", 1), shifted(ahead[1], "x", 3)])
+    same_core = [behind, across, ahead]
+
+    def to_both_halves(value):
+        return value + lax.ppermute(value, "role", [(0, 1)])
+
+    out_part = to_both_halves(out_part)
     in_part = ADAPTER_SCALE * jnp.dot(through, token_part, preferred_element_type=F32)
-    packed = jnp.concatenate([out_part, in_part.astype(BF)], axis=1)
+    in_part = to_both_halves(in_part.astype(BF))
+    other_behind, other_ahead = swapped(behind, "core"), swapped(ahead, "core")
+    packed = jnp.concatenate([out_part, in_part], axis=1)
     packed, same_core = lax.optimization_barrier((packed, same_core))
-    grads = spread(packed, ALL_GROUPS)
-    blocks = [down_pair, *same_core, downs[1], *(swapped(b, "core") for b in same_core)]
+    grads = spread(packed, DP)
+    other_across = swapped(same_core[1], "core")
+    blocks = [down_pair, *same_core, downs[1], other_behind, other_across, other_ahead]
     old_parts = layer_call(old_kernel, group_rows, slice_width, blocks, flags, hidden_old)
     grads, old_parts = lax.optimization_barrier((grads, old_parts))
     grads = sum_first(grads)
@@ -341,11 +339,11 @@
     give = swapped(lax.dynamic_index_in_dim(old_parts, 1 - side, 1, keepdims=False), "ylo")
     keep = lax.dynamic_index_in_dim(old_parts, side, 1, keepdims=False)
     pair = (keep.astype(F32) + give.astype(F32)).astype(BF)
-    renewed = hidden_total(to_rank(new_in.astype(BF))).astype(BF)
+    renewed = to_rank(new_in.astype(BF)).astype(BF)
+    renewed = spread(renewed, NEAR)
+    renewed = sum_first(spread(sum_first(renewed).astype(BF), "zh")).astype(BF)
     near_old = shifted_sum(pair, "zl")
-    new_parts = layer_call(
-        new_kernel, group_rows, slice_width, blocks, flags, base, renewed, new_out.astype(BF)
-    )
+    new_parts = layer_call(new_kernel, group_rows, slice_width, blocks, flags, base, renewed, new_out.astype(BF))
     near_new = sum_first(exchange(new_parts.reshape(8, 4, slice_width, group_rows), NEAR))
     near = jnp.stack([near_old, near_new], axis=1).astype(BF)
     layers = sum_first(exchange(near, "zh"))

time: 291 us -> 284 us (0.976)
  the two profiles are of different devices: /device:TPU:73 before, /device:TPU:41 now
where the time goes in v1:
time: 284 us; the launch traced here: 282 us
  starting transfers between devices  140 us (49%)
  waiting for transfers between devices  93.3 us (33%)
  Pallas kernels  23.8 us (8%)
  other arithmetic  11.3 us (4%)
  local copies, waits for them, and re-layouts  8.76 us (3%)
  matrix products  3.32 us (1%)
    all_to_all x9, starting transfers between devices, exchange(): return lax.all_to_all(pieces, axis, split_axis=0, concat_axis=0, tiled=True)  48.8 us
    all_to_all x9, waiting for transfers between devices, exchange(): return lax.all_to_all(pieces, axis, split_axis=0, concat_axis=0, tiled=True)  44.9 us
    ppermute x9, starting transfers between devices, swapped(): return lax.ppermute(value, axis, [(0, 1), (1, 0)])  33.4 us
    ppermute x9, waiting for transfers between devices, swapped(): return lax.ppermute(value, axis, [(0, 1), (1, 0)])  31.5 us
    ppermute x5, starting transfers between devices, plus_partner(): lax.ppermute(value, axis, [(i, i ^ step) for i in range(count)])  30.7 us
    ppermute x7, starting transfers between devices, shifted(): lax.ppermute(value, axis, [(i, (i + step) % count) for i in range(count)])  21.9 us
    pallas_call x2, Pallas kernels, layer_call(): pl.pallas_call(kernel, out_shape=jax.ShapeDtypeStruct((32, width, group),...  10.8 us
    ppermute x7, waiting for transfers between devices, shifted(): lax.ppermute(value, axis, [(i, (i + step) % count) for i in range(count)])  9.69 us
  transfers between devices with their start and end apart: 32, of which 13 were waited for; matrix products, arithmetic and copies ran while one was open for 5% of the time, Pallas kernels for 3%

profile of v1, /device:TPU:41, one launch (start us, length us, event | category | flops | bytes accessed | tf_op | source)
XLA Modules:
  0.0 282.4 jit_solution(5032289296802049063)
XLA Ops:
  2.0 3.7 %rows_by_x.1 = bf16[4,2,2,128,640]{4,3,2,1,0:T(8,128)(2,1)} custom-call(bf16[128,5120]{1,0:T(8,128)(2,1)} %bitcast.100, bf16[128,5120]{1,0:T(8,128)(2,1)} %cotangent_ref.1, f32[128,1]{1,0:T(8,128)} %copy.25.scale_ref), custom_call_target="tpu_custom_call" | custom-call | tf_op jit(solution)/shard_map/rows_by_x/pallas_call | solution.py:98
  5.7 4.1 %all-to-all-start = ((bf16[4,2,2,128,640]{4,3,2,1,0:T(8,128)(2,1)}), bf16[4,2,2,128,640]{4,3,2,1,0:T(8,128)(2,1)S(1)}, u32[]{:S(2)}, u32[]{:S(2)}) async-start(bf16[4,2,2,128,640]{4,3,2,1,0:T(8,128)(2,1)} %rows_by_x.1), calls=%async_computation | async-start | bytes 5242880 | tf_op jit(solution)/shard_map/all_to_all | solution.py:33
  15.9 3.9 %collective-permute-start.1 = (bf16[2,320,432]{2,1,0:T(8,128)(2,1)}, bf16[2,320,432]{2,1,0:T(8,128)(2,1)}, u32[]{:S(2)}, u32[]{:S(2)}) collective-permute-start(bf16[2,320,432]{2,1,0:T(8,128)(2,1)} %refs_0_), channel_id=1, source_target_pairs={{0,256},{256,0},{1,257},{257,1},{2,258},{258,2},{3,259},{259,3},{4... | collective-permute-start | bytes 1658888 | tf_op jit(solution)/shard_map/ppermute | solution.py:37
  27.8 4.9 %collective-permute-start.4 = (f32[64,128]{1,0:T(8,128)S(1)}, f32[64,128]{1,0:T(8,128)S(1)}, u32[]{:S(2)}, u32[]{:S(2)}) collective-permute-start(f32[64,128]{1,0:T(8,128)S(1)} %add.100), channel_id=1, source_target_pairs={{0,4},{2,6},{4,0},{6,2},{1,5},{3,7},{5,1},{7,3},{8,12},{10,14},{12... | collective-permute-start | bytes 98312 | tf_op jit(solution)/shard_map/ppermute | solution.py:56
  32.7 5.3 %collective-permute-start.5 = (bf16[2,320,432]{2,1,0:T(8,128)(2,1)}, bf16[2,320,432]{2,1,0:T(8,128)(2,1)}, u32[]{:S(2)}, u32[]{:S(2)}) collective-permute-start(bf16[2,320,432]{2,1,0:T(8,128)(2,1)} %refs_0_), channel_id=1, source_target_pairs={{0,32},{32,0},{1,33},{33,1},{2,34},{34,2},{3,35},{35,3},{4,36},{36... | collective-permute-start | bytes 1658888 | tf_op jit(solution)/shard_map/ppermute | solution.py:37
  42.1 4.6 %collective-permute-start.7 = (bf16[2,320,432]{2,1,0:T(8,128)(2,1)S(1)}, bf16[2,320,432]{2,1,0:T(8,128)(2,1)}, u32[]{:S(2)}, u32[]{:S(2)}) collective-permute-start(bf16[2,320,432]{2,1,0:T(8,128)(2,1)S(1)} %pad_maximum_fusion.refs_4_.refs_0_), channel_id=1, source_target_pairs={{0,32},{32,0},{1,33},{33,1},{2,34},{34,2},{3,35},{35,3},{4,36},{36... | collective-permute-start | bytes 1658888 | tf_op jit(solution)/shard_map/ppermute | solution.py:37
  51.0 6.8 %partials.1 = bf16[4,3,432,128]{3,2,1,0:T(8,128)(2,1)} custom-call(s32[3]{0:T(128)} %pad_add_fusion.flag_ref, bf16[4,2,2,128,640]{4,3,2,1,0:T(8,128)(2,1)} %copy-done, bf16[2,320,432]{2,1,0:T(8,128)(2,1)} %refs_0_, bf16[2,320,432]{2,1,0:T(8,128)(2,1)} %collective-permute-done.1.refs_1_, bf16[2,320,432]{2,1,0:T(8,128)(2,1)} %collective-permute-done.5.refs_2_, ...), custom_call_target="tpu_custom_call" | custom-call | tf_op jit(solution)/shard_map/partials/pallas_call | solution.py:152
  57.9 4.4 %all-to-all-start.1 = ((bf16[4,3,432,128]{3,2,1,0:T(8,128)(2,1)}), bf16[4,3,432,128]{3,2,1,0:T(8,128)(2,1)S(1)}, u32[]{:S(2)}, u32[]{:S(2)}) async-start(bf16[4,3,432,128]{3,2,1,0:T(8,128)(2,1)} %partials.1), calls=%async_computation.1 | async-start | bytes 2654208 | tf_op jit(solution)/shard_map/all_to_all | solution.py:33
  62.2 8.8 %collective-permute-start.8 = (f32[64,128]{1,0:T(8,128)S(1)}, f32[64,128]{1,0:T(8,128)S(1)}, u32[]{:S(2)}, u32[]{:S(2)}) collective-permute-start(f32[64,128]{1,0:T(8,128)S(1)} %add.101), channel_id=1, source_target_pairs={{0,8},{8,0},{16,24},{24,16},{1,9},{9,1},{17,25},{25,17},{2,10},{10... | collective-permute-start | bytes 98312 | tf_op jit(solution)/shard_map/ppermute | solution.py:56
  72.3 13.0 %collective-permute-start.9 = (f32[64,128]{1,0:T(8,128)S(1)}, f32[64,128]{1,0:T(8,128)S(1)}, u32[]{:S(2)}, u32[]{:S(2)}) collective-permute-start(f32[64,128]{1,0:T(8,128)S(1)} %add.102), channel_id=1, source_target_pairs={{0,16},{8,24},{16,0},{24,8},{1,17},{9,25},{17,1},{25,9},{2,18},{10... | collective-permute-start | bytes 98312 | tf_op jit(solution)/shard_map/ppermute | solution.py:56
  86.0 3.4 %collective-permute-start.12 = (bf16[2,320,432]{2,1,0:T(8,128)(2,1)S(1)}, bf16[2,320,432]{2,1,0:T(8,128)(2,1)S(1)}, u32[]{:S(2)}, u32[]{:S(2)}) collective-permute-start(bf16[2,320,432]{2,1,0:T(8,128)(2,1)S(1)} %copy-done.2), channel_id=1, source_target_pairs={{0,64},{64,128},{128,192},{192,0},{1,65},{65,129},{129,193},{193,1... | collective-permute-start | bytes 1658888 | tf_op jit(solution)/shard_map/ppermute | solution.py:51
  94.1 4.5 %all-to-all-start.2 = ((bf16[8,64,128]{2,1,0:T(8,128)(2,1)}), bf16[8,64,128]{2,1,0:T(8,128)(2,1)S(1)}, u32[]{:S(2)}, u32[]{:S(2)}) async-start(bf16[8,64,128]{2,1,0:T(8,128)(2,1)} %broadcast_in_dim.57), calls=%async_computation.2 | async-start | bytes 262144 | tf_op jit(solution)/shard_map/all_to_all | solution.py:33
  101.8 3.9 %collective-permute-start.10 = (bf16[64,432]{1,0:T(8,128)(2,1)}, bf16[64,432]{1,0:T(8,128)(2,1)S(1)}, u32[]{:S(2)}, u32[]{:S(2)}) collective-permute-start(bf16[64,432]{1,0:T(8,128)(2,1)} %get-tuple-element.35), channel_id=1, source_target_pairs={{0,256},{1,257},{2,258},{3,259},{4,260},{5,261},{6,262},{7,263},{8... | collective-permute-start | bytes 165896 | tf_op jit(solution)/shard_map/ppermute | solution.py:311
  106.4 10.1 %all-to-all-start.3 = ((bf16[4,64,128]{2,1,0:T(8,128)(2,1)}), bf16[4,64,128]{2,1,0:T(8,128)(2,1)S(1)}, u32[]{:S(2)}, u32[]{:S(2)}) async-start(bf16[4,64,128]{2,1,0:T(8,128)(2,1)} %broadcast_in_dim.58), calls=%async_computation.3 | async-start | bytes 131072 | tf_op jit(solution)/shard_map/all_to_all | solution.py:33
  120.0 4.6 %collective-permute-start.15 = (bf16[320,432]{1,0:T(8,128)(2,1)}, bf16[320,432]{1,0:T(8,128)(2,1)S(1)}, u32[]{:S(2)}, u32[]{:S(2)}) collective-permute-start(bf16[320,432]{1,0:T(8,128)(2,1)} %slice_bitcast_fusion), channel_id=1, source_target_pairs={{0,192},{64,0},{128,64},{192,128},{1,193},{65,1},{129,65},{193,129... | collective-permute-start | bytes 829448 | tf_op jit(solution)/shard_map/ppermute | solution.py:51
  124.6 3.8 %all-to-all-done.3 = bf16[4,64,128]{2,1,0:T(8,128)(2,1)S(1)} async-done(((bf16[4,64,128]{2,1,0:T(8,128)(2,1)}), bf16[4,64,128]{2,1,0:T(8,128)(2,1)S(1)}, u32[]{:S(2)}, u32[]{:S(2)}) %all-to-all-start.3) | async-done | bytes 65568 | tf_op jit(solution)/shard_map/all_to_all | solution.py:33
  130.8 8.3 %collective-permute-start.16 = (bf16[2,320,432]{2,1,0:T(8,128)(2,1)S(1)}, bf16[2,320,432]{2,1,0:T(8,128)(2,1)S(1)}, u32[]{:S(2)}, u32[]{:S(2)}) collective-permute-start(bf16[2,320,432]{2,1,0:T(8,128)(2,1)S(1)} %collective-permute-done.12.refs_1_), channel_id=1, source_target_pairs={{0,32},{32,0},{1,33},{33,1},{2,34},{34,2},{3,35},{35,3},{4,36},{36... | collective-permute-start | bytes 1658888 | tf_op jit(solution)/shard_map/ppermute | solution.py:37
  146.6 4.2 %all-to-all-start.4 = ((bf16[8,64,592]{2,1,0:T(8,128)(2,1)}), bf16[8,64,592]{2,1,0:T(8,128)(2,1)}, u32[]{:S(2)}, u32[]{:S(2)}) async-start(bf16[8,64,592]{2,1,0:T(8,128)(2,1)} %broadcast_in_dim.59), calls=%async_computation.4 | async-start | bytes 1310720 | tf_op jit(solution)/shard_map/all_to_all | solution.py:33
  151.8 5.2 %shard_map.179 = bf16[32,160,128]{2,1,0:T(8,128)(2,1)} custom-call(s32[3]{0:T(128)} %pad_add_fusion.flag_ref, bf16[432,128]{1,0:T(8,128)(2,1)} %get-tuple-element.39.hidden_ref, bf16[2,320,432]{2,1,0:T(8,128)(2,1)} %copy-done.1, bf16[2,320,432]{2,1,0:T(8,128)(2,1)} %copy-done.6, bf16[2,320,432]{2,1,0:T(8,128)(2,1)} %copy-done.3, ...), custom_call_target="tpu_custom_call" | custom-call | tf_op jit(solution)/shard_map/pallas_call | solution.py:244
  157.0 4.6 %all-to-all-done.4 = bf16[8,64,592]{2,1,0:T(8,128)(2,1)} async-done(((bf16[8,64,592]{2,1,0:T(8,128)(2,1)}), bf16[8,64,592]{2,1,0:T(8,128)(2,1)}, u32[]{:S(2)}, u32[]{:S(2)}) %all-to-all-start.4) | async-done | bytes 606240 | tf_op jit(solution)/shard_map/all_to_all | solution.py:33
  165.4 5.4 %all-to-all-start.5 = ((bf16[8,64,128]{2,1,0:T(8,128)(2,1)}), bf16[8,64,128]{2,1,0:T(8,128)(2,1)S(1)}, u32[]{:S(2)}, u32[]{:S(2)}) async-start(bf16[8,64,128]{2,1,0:T(8,128)(2,1)} %broadcast_in_dim.60), calls=%async_computation.5 | async-start | bytes 262144 | tf_op jit(solution)/shard_map/all_to_all | solution.py:33
  170.8 4.6 %all-to-all-done.5 = bf16[8,64,128]{2,1,0:T(8,128)(2,1)S(1)} async-done(((bf16[8,64,128]{2,1,0:T(8,128)(2,1)}), bf16[8,64,128]{2,1,0:T(8,128)(2,1)S(1)}, u32[]{:S(2)}, u32[]{:S(2)}) %all-to-all-start.5) | async-done | bytes 131104 | tf_op jit(solution)/shard_map/all_to_all | solution.py:33
  176.1 7.4 %all-to-all-start.6 = ((bf16[4,64,128]{2,1,0:T(8,128)(2,1)}), bf16[4,64,128]{2,1,0:T(8,128)(2,1)S(1)}, u32[]{:S(2)}, u32[]{:S(2)}) async-start(bf16[4,64,128]{2,1,0:T(8,128)(2,1)} %broadcast_in_dim.61), calls=%async_computation.6 | async-start | bytes 131072 | tf_op jit(solution)/shard_map/all_to_all | solution.py:33
  184.3 10.8 %all-to-all-done.6 = bf16[4,64,128]{2,1,0:T(8,128)(2,1)S(1)} async-done(((bf16[4,64,128]{2,1,0:T(8,128)(2,1)}), bf16[4,64,128]{2,1,0:T(8,128)(2,1)S(1)}, u32[]{:S(2)}, u32[]{:S(2)}) %all-to-all-start.6) | async-done | bytes 65568 | tf_op jit(solution)/shard_map/all_to_all | solution.py:33
  195.8 5.6 %shard_map.180 = bf16[32,160,128]{2,1,0:T(8,128)(2,1)} custom-call(s32[3]{0:T(128)} %pad_add_fusion.flag_ref, f32[2,432,128]{2,1,0:T(8,128)} %get-tuple-element.44.base_ref, bf16[64,128]{1,0:T(8,128)(2,1)} %reduce_sum.79.reduced_ref, bf16[2,32,432]{2,1,0:T(8,128)(2,1)} %get-tuple-element.46.lift_ref, bf16[2,320,432]{2,1,0:T(8,128)(2,1)} %copy-done.1, ...), custom_call_target="tpu_custom_call" | custom-call | tf_op jit(solution)/shard_map/pallas_call | solution.py:244
  201.4 5.2 %all-to-all-start.7 = ((bf16[8,4,160,128]{3,2,1,0:T(8,128)(2,1)}), bf16[8,4,160,128]{3,2,1,0:T(8,128)(2,1)S(1)}, u32[]{:S(2)}, u32[]{:S(2)}) async-start(bf16[8,4,160,128]{3,2,1,0:T(8,128)(2,1)} %bitcast.97), calls=%async_computation.7 | async-start | bytes 2621440 | tf_op jit(solution)/shard_map/all_to_all | solution.py:33
  208.8 26.6 %collective-permute-done.19 = bf16[4,4,160,128]{3,2,1,0:T(8,128)(2,1)} collective-permute-done((bf16[4,4,160,128]{3,2,1,0:T(8,128)(2,1)S(1)}, bf16[4,4,160,128]{3,2,1,0:T(8,128)(2,1)}, u32[]{:S(2)}, u32[]{:S(2)}) %collective-permute-start.19) | collective-permute-done | bytes 655392 | tf_op jit(solution)/shard_map/ppermute | solution.py:37
  236.8 3.2 %collective-permute-start.20 = (bf16[4,160,128]{2,1,0:T(8,128)(2,1)S(1)}, bf16[4,160,128]{2,1,0:T(8,128)(2,1)S(1)}, u32[]{:S(2)}, u32[]{:S(2)}) collective-permute-start(bf16[4,160,128]{2,1,0:T(8,128)(2,1)S(1)} %get-tuple-element.50), channel_id=1, source_target_pairs={{0,2},{2,4},{4,6},{6,0},{1,3},{3,5},{5,7},{7,1},{8,10},{10,12},{12... | collective-permute-start | bytes 491528 | tf_op jit(solution)/shard_map/ppermute | solution.py:51
  242.4 3.4 %collective-permute-start.22 = (bf16[4,160,128]{2,1,0:T(8,128)(2,1)S(1)}, bf16[4,160,128]{2,1,0:T(8,128)(2,1)S(1)}, u32[]{:S(2)}, u32[]{:S(2)}) collective-permute-start(bf16[4,160,128]{2,1,0:T(8,128)(2,1)S(1)} %get-tuple-element.51), channel_id=1, source_target_pairs={{0,6},{2,0},{4,2},{6,4},{1,7},{3,1},{5,3},{7,5},{8,14},{10,8},{12,... | collective-permute-start | bytes 491528 | tf_op jit(solution)/shard_map/ppermute | solution.py:51
  245.8 7.6 %collective-permute-done.21 = bf16[4,160,128]{2,1,0:T(8,128)(2,1)S(1)} collective-permute-done((bf16[4,160,128]{2,1,0:T(8,128)(2,1)S(1)}, bf16[4,160,128]{2,1,0:T(8,128)(2,1)S(1)}, u32[]{:S(2)}, u32[]{:S(2)}) %collective-permute-start.21) | collective-permute-done | bytes 163872 | tf_op jit(solution)/shard_map/ppermute | solution.py:51
  256.5 3.5 %all-to-all-start.8 = ((bf16[4,2,160,128]{3,2,1,0:T(8,128)(2,1)}), bf16[4,2,160,128]{3,2,1,0:T(8,128)(2,1)S(1)}, u32[]{:S(2)}, u32[]{:S(2)}) async-start(bf16[4,2,160,128]{3,2,1,0:T(8,128)(2,1)} %pad_maximum_fusion.2), calls=%async_computation.8 | async-start | bytes 655360 | tf_op jit(solution)/shard_map/all_to_all | solution.py:33
  260.6 21.1 %all-to-all-done.8 = bf16[4,2,160,128]{3,2,1,0:T(8,128)(2,1)S(1)} async-done(((bf16[4,2,160,128]{3,2,1,0:T(8,128)(2,1)}), bf16[4,2,160,128]{3,2,1,0:T(8,128)(2,1)S(1)}, u32[]{:S(2)}, u32[]{:S(2)}) %all-to-all-start.8) | async-done | bytes 327712 | tf_op jit(solution)/shard_map/all_to_all | solution.py:33
  (120 shorter events, 64.2 us)
Async XLA Ops:
  5.7 43.5 %all-to-all-start = ((bf16[4,2,2,128,640]{4,3,2,1,0:T(8,128)(2,1)}), bf16[4,2,2,128,640]{4,3,2,1,0:T(8,128)(2,1)S(1)}, u32[]{:S(2)}, u32[]{:S(2)}) async-start(bf16[4,2,2,128,640]{4,3,2,1,0:T(8,128)(2,1)} %rows_by_x.1), calls=%async_computation | async-start | bytes 5242880 | tf_op jit(solution)/shard_map/all_to_all | solution.py:33
  11.0 5.0 %collective-permute-start = (f32[64,128]{1,0:T(8,128)S(1)}, f32[64,128]{1,0:T(8,128)S(1)}, u32[]{:S(2)}, u32[]{:S(2)}) collective-permute-start(f32[64,128]{1,0:T(8,128)S(1)} %convolution_bitcast_fusion), channel_id=1, source_target_pairs={{0,1},{1,0},{2,3},{3,2},{4,5},{5,4},{6,7},{7,6},{8,9},{9,8},{10,11... | collective-permute-start | bytes 98312 | tf_op jit(solution)/shard_map/ppermute | solution.py:56
  15.9 25.1 %collective-permute-start.1 = (bf16[2,320,432]{2,1,0:T(8,128)(2,1)}, bf16[2,320,432]{2,1,0:T(8,128)(2,1)}, u32[]{:S(2)}, u32[]{:S(2)}) collective-permute-start(bf16[2,320,432]{2,1,0:T(8,128)(2,1)} %refs_0_), channel_id=1, source_target_pairs={{0,256},{256,0},{1,257},{257,1},{2,258},{258,2},{3,259},{259,3},{4... | collective-permute-start | bytes 1658888 | tf_op jit(solution)/shard_map/ppermute | solution.py:37
  19.9 21.2 %collective-permute-start.2 = (bf16[320,432]{1,0:T(8,128)(2,1)S(1)}, bf16[320,432]{1,0:T(8,128)(2,1)S(1)}, u32[]{:S(2)}, u32[]{:S(2)}) collective-permute-start(bf16[320,432]{1,0:T(8,128)(2,1)S(1)} %bitcast.104), channel_id=1, source_target_pairs={{0,256},{256,0},{1,257},{257,1},{2,258},{258,2},{3,259},{259,3},{4... | collective-permute-start | bytes 829448 | tf_op jit(solution)/shard_map/ppermute | solution.py:37
  22.7 5.1 %collective-permute-start.3 = (f32[64,128]{1,0:T(8,128)S(1)}, f32[64,128]{1,0:T(8,128)S(1)}, u32[]{:S(2)}, u32[]{:S(2)}) collective-permute-start(f32[64,128]{1,0:T(8,128)S(1)} %add.99), channel_id=1, source_target_pairs={{0,2},{2,0},{4,6},{6,4},{1,3},{3,1},{5,7},{7,5},{8,10},{10,8},{12,... | collective-permute-start | bytes 98312 | tf_op jit(solution)/shard_map/ppermute | solution.py:56
  27.8 10.2 %collective-permute-start.4 = (f32[64,128]{1,0:T(8,128)S(1)}, f32[64,128]{1,0:T(8,128)S(1)}, u32[]{:S(2)}, u32[]{:S(2)}) collective-permute-start(f32[64,128]{1,0:T(8,128)S(1)} %add.100), channel_id=1, source_target_pairs={{0,4},{2,6},{4,0},{6,2},{1,5},{3,7},{5,1},{7,3},{8,12},{10,14},{12... | collective-permute-start | bytes 98312 | tf_op jit(solution)/shard_map/ppermute | solution.py:56
  32.7 16.5 %collective-permute-start.5 = (bf16[2,320,432]{2,1,0:T(8,128)(2,1)}, bf16[2,320,432]{2,1,0:T(8,128)(2,1)}, u32[]{:S(2)}, u32[]{:S(2)}) collective-permute-start(bf16[2,320,432]{2,1,0:T(8,128)(2,1)} %refs_0_), channel_id=1, source_target_pairs={{0,32},{32,0},{1,33},{33,1},{2,34},{34,2},{3,35},{35,3},{4,36},{36... | collective-permute-start | bytes 1658888 | tf_op jit(solution)/shard_map/ppermute | solution.py:37
  42.1 7.1 %collective-permute-start.7 = (bf16[2,320,432]{2,1,0:T(8,128)(2,1)S(1)}, bf16[2,320,432]{2,1,0:T(8,128)(2,1)}, u32[]{:S(2)}, u32[]{:S(2)}) collective-permute-start(bf16[2,320,432]{2,1,0:T(8,128)(2,1)S(1)} %pad_maximum_fusion.refs_4_.refs_0_), channel_id=1, source_target_pairs={{0,32},{32,0},{1,33},{33,1},{2,34},{34,2},{3,35},{35,3},{4,36},{36... | collective-permute-start | bytes 1658888 | tf_op jit(solution)/shard_map/ppermute | solution.py:37
  46.7 4.3 %collective-permute-start.6 = (bf16[2,320,432]{2,1,0:T(8,128)(2,1)}, bf16[2,320,432]{2,1,0:T(8,128)(2,1)}, u32[]{:S(2)}, u32[]{:S(2)}) collective-permute-start(bf16[2,320,432]{2,1,0:T(8,128)(2,1)} %collective-permute-done.1.refs_1_), channel_id=1, source_target_pairs={{0,32},{32,0},{1,33},{33,1},{2,34},{34,2},{3,35},{35,3},{4,36},{36... | collective-permute-start | bytes 1658888 | tf_op jit(solution)/shard_map/ppermute | solution.py:37
  57.9 28.1 %all-to-all-start.1 = ((bf16[4,3,432,128]{3,2,1,0:T(8,128)(2,1)}), bf16[4,3,432,128]{3,2,1,0:T(8,128)(2,1)S(1)}, u32[]{:S(2)}, u32[]{:S(2)}) async-start(bf16[4,3,432,128]{3,2,1,0:T(8,128)(2,1)} %partials.1), calls=%async_computation.1 | async-start | bytes 2654208 | tf_op jit(solution)/shard_map/all_to_all | solution.py:33
  62.2 10.1 %collective-permute-start.8 = (f32[64,128]{1,0:T(8,128)S(1)}, f32[64,128]{1,0:T(8,128)S(1)}, u32[]{:S(2)}, u32[]{:S(2)}) collective-permute-start(f32[64,128]{1,0:T(8,128)S(1)} %add.101), channel_id=1, source_target_pairs={{0,8},{8,0},{16,24},{24,16},{1,9},{9,1},{17,25},{25,17},{2,10},{10... | collective-permute-start | bytes 98312 | tf_op jit(solution)/shard_map/ppermute | solution.py:56
  72.3 17.0 %collective-permute-start.9 = (f32[64,128]{1,0:T(8,128)S(1)}, f32[64,128]{1,0:T(8,128)S(1)}, u32[]{:S(2)}, u32[]{:S(2)}) collective-permute-start(f32[64,128]{1,0:T(8,128)S(1)} %add.102), channel_id=1, source_target_pairs={{0,16},{8,24},{16,0},{24,8},{1,17},{9,25},{17,1},{25,9},{2,18},{10... | collective-permute-start | bytes 98312 | tf_op jit(solution)/shard_map/ppermute | solution.py:56
  86.0 30.5 %collective-permute-start.12 = (bf16[2,320,432]{2,1,0:T(8,128)(2,1)S(1)}, bf16[2,320,432]{2,1,0:T(8,128)(2,1)S(1)}, u32[]{:S(2)}, u32[]{:S(2)}) collective-permute-start(bf16[2,320,432]{2,1,0:T(8,128)(2,1)S(1)} %copy-done.2), channel_id=1, source_target_pairs={{0,64},{64,128},{128,192},{192,0},{1,65},{65,129},{129,193},{193,1... | collective-permute-start | bytes 1658888 | tf_op jit(solution)/shard_map/ppermute | solution.py:51
  94.1 11.6 %all-to-all-start.2 = ((bf16[8,64,128]{2,1,0:T(8,128)(2,1)}), bf16[8,64,128]{2,1,0:T(8,128)(2,1)S(1)}, u32[]{:S(2)}, u32[]{:S(2)}) async-start(bf16[8,64,128]{2,1,0:T(8,128)(2,1)} %broadcast_in_dim.57), calls=%async_computation.2 | async-start | bytes 262144 | tf_op jit(solution)/shard_map/all_to_all | solution.py:33
  98.6 20.6 %collective-permute-start.14 = (bf16[2,320,432]{2,1,0:T(8,128)(2,1)S(1)}, bf16[2,320,432]{2,1,0:T(8,128)(2,1)S(1)}, u32[]{:S(2)}, u32[]{:S(2)}) collective-permute-start(bf16[2,320,432]{2,1,0:T(8,128)(2,1)S(1)} %copy-done.2), channel_id=1, source_target_pairs={{0,192},{64,0},{128,64},{192,128},{1,193},{65,1},{129,65},{193,129... | collective-permute-start | bytes 1658888 | tf_op jit(solution)/shard_map/ppermute | solution.py:51
  101.8 29.0 %collective-permute-start.10 = (bf16[64,432]{1,0:T(8,128)(2,1)}, bf16[64,432]{1,0:T(8,128)(2,1)S(1)}, u32[]{:S(2)}, u32[]{:S(2)}) collective-permute-start(bf16[64,432]{1,0:T(8,128)(2,1)} %get-tuple-element.35), channel_id=1, source_target_pairs={{0,256},{1,257},{2,258},{3,259},{4,260},{5,261},{6,262},{7,263},{8... | collective-permute-start | bytes 165896 | tf_op jit(solution)/shard_map/ppermute | solution.py:311
  106.4 22.0 %all-to-all-start.3 = ((bf16[4,64,128]{2,1,0:T(8,128)(2,1)}), bf16[4,64,128]{2,1,0:T(8,128)(2,1)S(1)}, u32[]{:S(2)}, u32[]{:S(2)}) async-start(bf16[4,64,128]{2,1,0:T(8,128)(2,1)} %broadcast_in_dim.58), calls=%async_computation.3 | async-start | bytes 131072 | tf_op jit(solution)/shard_map/all_to_all | solution.py:33
  117.3 23.9 %collective-permute-start.13 = (bf16[320,432]{1,0:T(8,128)(2,1)}, bf16[320,432]{1,0:T(8,128)(2,1)S(1)}, u32[]{:S(2)}, u32[]{:S(2)}) collective-permute-start(bf16[320,432]{1,0:T(8,128)(2,1)} %slice_bitcast_fusion.1), channel_id=1, source_target_pairs={{0,64},{64,128},{128,192},{192,0},{1,65},{65,129},{129,193},{193,1... | collective-permute-start | bytes 829448 | tf_op jit(solution)/shard_map/ppermute | solution.py:51
  120.0 21.2 %collective-permute-start.15 = (bf16[320,432]{1,0:T(8,128)(2,1)}, bf16[320,432]{1,0:T(8,128)(2,1)S(1)}, u32[]{:S(2)}, u32[]{:S(2)}) collective-permute-start(bf16[320,432]{1,0:T(8,128)(2,1)} %slice_bitcast_fusion), channel_id=1, source_target_pairs={{0,192},{64,0},{128,64},{192,128},{1,193},{65,1},{129,65},{193,129... | collective-permute-start | bytes 829448 | tf_op jit(solution)/shard_map/ppermute | solution.py:51
  129.5 11.6 %collective-permute-start.11 = (bf16[64,160]{1,0:T(8,128)(2,1)S(1)}, bf16[64,160]{1,0:T(8,128)(2,1)S(1)}, u32[]{:S(2)}, u32[]{:S(2)}) collective-permute-start(bf16[64,160]{1,0:T(8,128)(2,1)S(1)} %fusion.1), channel_id=1, source_target_pairs={{0,256},{1,257},{2,258},{3,259},{4,260},{5,261},{6,262},{7,263},{8... | collective-permute-start | bytes 61448 | tf_op jit(solution)/shard_map/ppermute | solution.py:311
  130.8 20.0 %collective-permute-start.16 = (bf16[2,320,432]{2,1,0:T(8,128)(2,1)S(1)}, bf16[2,320,432]{2,1,0:T(8,128)(2,1)S(1)}, u32[]{:S(2)}, u32[]{:S(2)}) collective-permute-start(bf16[2,320,432]{2,1,0:T(8,128)(2,1)S(1)} %collective-permute-done.12.refs_1_), channel_id=1, source_target_pairs={{0,32},{32,0},{1,33},{33,1},{2,34},{34,2},{3,35},{35,3},{4,36},{36... | collective-permute-start | bytes 1658888 | tf_op jit(solution)/shard_map/ppermute | solution.py:37
  139.1 11.6 %collective-permute-start.18 = (bf16[2,320,432]{2,1,0:T(8,128)(2,1)S(1)}, bf16[2,320,432]{2,1,0:T(8,128)(2,1)S(1)}, u32[]{:S(2)}, u32[]{:S(2)}) collective-permute-start(bf16[2,320,432]{2,1,0:T(8,128)(2,1)S(1)} %collective-permute-done.14.refs_3_), channel_id=1, source_target_pairs={{0,32},{32,0},{1,33},{33,1},{2,34},{34,2},{3,35},{35,3},{4,36},{36... | collective-permute-start | bytes 1658888 | tf_op jit(solution)/shard_map/ppermute | solution.py:37
  143.2 7.6 %collective-permute-start.17 = (bf16[2,320,432]{2,1,0:T(8,128)(2,1)S(1)}, bf16[2,320,432]{2,1,0:T(8,128)(2,1)}, u32[]{:S(2)}, u32[]{:S(2)}) collective-permute-start(bf16[2,320,432]{2,1,0:T(8,128)(2,1)S(1)} %pad_maximum_fusion.1.refs_2_), channel_id=1, source_target_pairs={{0,32},{32,0},{1,33},{33,1},{2,34},{34,2},{3,35},{35,3},{4,36},{36... | collective-permute-start | bytes 1658888 | tf_op jit(solution)/shard_map/ppermute | solution.py:37
  146.6 15.0 %all-to-all-start.4 = ((bf16[8,64,592]{2,1,0:T(8,128)(2,1)}), bf16[8,64,592]{2,1,0:T(8,128)(2,1)}, u32[]{:S(2)}, u32[]{:S(2)}) async-start(bf16[8,64,592]{2,1,0:T(8,128)(2,1)} %broadcast_in_dim.59), calls=%async_computation.4 | async-start | bytes 1310720 | tf_op jit(solution)/shard_map/all_to_all | solution.py:33
  165.4 10.0 %all-to-all-start.5 = ((bf16[8,64,128]{2,1,0:T(8,128)(2,1)}), bf16[8,64,128]{2,1,0:T(8,128)(2,1)S(1)}, u32[]{:S(2)}, u32[]{:S(2)}) async-start(bf16[8,64,128]{2,1,0:T(8,128)(2,1)} %broadcast_in_dim.60), calls=%async_computation.5 | async-start | bytes 262144 | tf_op jit(solution)/shard_map/all_to_all | solution.py:33
  176.1 19.1 %all-to-all-start.6 = ((bf16[4,64,128]{2,1,0:T(8,128)(2,1)}), bf16[4,64,128]{2,1,0:T(8,128)(2,1)S(1)}, u32[]{:S(2)}, u32[]{:S(2)}) async-start(bf16[4,64,128]{2,1,0:T(8,128)(2,1)} %broadcast_in_dim.61), calls=%async_computation.6 | async-start | bytes 131072 | tf_op jit(solution)/shard_map/all_to_all | solution.py:33
  201.4 54.2 %all-to-all-start.7 = ((bf16[8,4,160,128]{3,2,1,0:T(8,128)(2,1)}), bf16[8,4,160,128]{3,2,1,0:T(8,128)(2,1)S(1)}, u32[]{:S(2)}, u32[]{:S(2)}) async-start(bf16[8,4,160,128]{3,2,1,0:T(8,128)(2,1)} %bitcast.97), calls=%async_computation.7 | async-start | bytes 2621440 | tf_op jit(solution)/shard_map/all_to_all | solution.py:33
  206.6 28.9 %collective-permute-start.19 = (bf16[4,4,160,128]{3,2,1,0:T(8,128)(2,1)S(1)}, bf16[4,4,160,128]{3,2,1,0:T(8,128)(2,1)}, u32[]{:S(2)}, u32[]{:S(2)}) collective-permute-start(bf16[4,4,160,128]{3,2,1,0:T(8,128)(2,1)S(1)} %dynamic-slice_bitcast_fusion), channel_id=1, source_target_pairs={{0,1},{1,0},{2,3},{3,2},{4,5},{5,4},{6,7},{7,6},{8,9},{9,8},{10,11... | collective-permute-start | bytes 1966088 | tf_op jit(solution)/shard_map/ppermute | solution.py:37
  236.8 9.0 %collective-permute-start.20 = (bf16[4,160,128]{2,1,0:T(8,128)(2,1)S(1)}, bf16[4,160,128]{2,1,0:T(8,128)(2,1)S(1)}, u32[]{:S(2)}, u32[]{:S(2)}) collective-permute-start(bf16[4,160,128]{2,1,0:T(8,128)(2,1)S(1)} %get-tuple-element.50), channel_id=1, source_target_pairs={{0,2},{2,4},{4,6},{6,0},{1,3},{3,5},{5,7},{7,1},{8,10},{10,12},{12... | collective-permute-start | bytes 491528 | tf_op jit(solution)/shard_map/ppermute | solution.py:51
  240.0 13.4 %collective-permute-start.21 = (bf16[4,160,128]{2,1,0:T(8,128)(2,1)S(1)}, bf16[4,160,128]{2,1,0:T(8,128)(2,1)S(1)}, u32[]{:S(2)}, u32[]{:S(2)}) collective-permute-start(bf16[4,160,128]{2,1,0:T(8,128)(2,1)S(1)} %get-tuple-element.52), channel_id=1, source_target_pairs={{0,4},{2,6},{4,0},{6,2},{1,5},{3,7},{5,1},{7,3},{8,12},{10,14},{12... | collective-permute-start | bytes 491528 | tf_op jit(solution)/shard_map/ppermute | solution.py:51
  242.4 13.1 %collective-permute-start.22 = (bf16[4,160,128]{2,1,0:T(8,128)(2,1)S(1)}, bf16[4,160,128]{2,1,0:T(8,128)(2,1)S(1)}, u32[]{:S(2)}, u32[]{:S(2)}) collective-permute-start(bf16[4,160,128]{2,1,0:T(8,128)(2,1)S(1)} %get-tuple-element.51), channel_id=1, source_target_pairs={{0,6},{2,0},{4,2},{6,4},{1,7},{3,1},{5,3},{7,5},{8,14},{10,8},{12,... | collective-permute-start | bytes 491528 | tf_op jit(solution)/shard_map/ppermute | solution.py:51
  256.5 25.2 %all-to-all-start.8 = ((bf16[4,2,160,128]{3,2,1,0:T(8,128)(2,1)}), bf16[4,2,160,128]{3,2,1,0:T(8,128)(2,1)S(1)}, u32[]{:S(2)}, u32[]{:S(2)}) async-start(bf16[4,2,160,128]{3,2,1,0:T(8,128)(2,1)} %pad_maximum_fusion.2), calls=%async_computation.8 | async-start | bytes 655360 | tf_op jit(solution)/shard_map/all_to_all | solution.py:33
  (20 other events, 268.9 us)

commit v2 on v1

--- a/solution.py
+++ b/solution.py
@@ -56,14 +56,18 @@
     return value + lax.ppermute(value, axis, [(i, i ^ step) for i in range(count)])
 
 
-def shifted_sum(pieces, axis):
-    index = lax.axis_index(axis)
-    count = lax.axis_size(axis)
-    total = lax.dynamic_index_in_dim(pieces, index, 0, keepdims=False).astype(F32)
-    for step in range(1, count):
-        piece = lax.dynamic_index_in_dim(pieces, lax.rem(index + step, count), 0, keepdims=False)
-        total = total + shifted(piece, axis, step).astype(F32)
-    return total
+def halved(pieces, axis, bit):
+    mine = lax.axis_index(axis)
+    if bit == 1:
+        both = pieces.reshape(2, 2, *pieces.shape[1:])
+        mine, dim = lax.rem(mine, 2), 1
+    else:
+        both = pieces
+        mine, dim = lax.div(mine, 2), 0
+    keep = lax.dynamic_index_in_dim(both, mine, dim, keepdims=False)
+    give = lax.dynamic_index_in_dim(both, 1 - mine, dim, keepdims=False)
+    got = lax.ppermute(give, axis, [(i, i ^ bit) for i in range(4)])
+    return (keep.astype(F32) + got.astype(F32)).astype(BF)
 
 
 def adam_update(param, grad, first, second):
@@ -304,21 +308,16 @@
     through = spread(through, "zh")
     through = sum_first(through).astype(BF)
     behind, ahead = shifted(down_first, "x", 1), shifted(down_first, "x", 3)
-    across = jnp.stack([shifted(behind[0], "x", 1), shifted(ahead[1], "x", 3)])
+    across = shifted(behind, "x", 1)
     same_core = [behind, across, ahead]
 
-    def to_both_halves(value):
-        return value + lax.ppermute(value, "role", [(0, 1)])
-
-    out_part = to_both_halves(out_part)
     in_part = ADAPTER_SCALE * jnp.dot(through, token_part, preferred_element_type=F32)
-    in_part = to_both_halves(in_part.astype(BF))
-    other_behind, other_ahead = swapped(behind, "core"), swapped(ahead, "core")
-    packed = jnp.concatenate([out_part, in_part], axis=1)
+    packed = jnp.concatenate([out_part, in_part.astype(BF)], axis=1)
+    packed = packed + lax.ppermute(packed, "role", [(0, 1)])
     packed, same_core = lax.optimization_barrier((packed, same_core))
     grads = spread(packed, DP)
-    other_across = swapped(same_core[1], "core")
-    blocks = [down_pair, *same_core, downs[1], other_behind, other_across, other_ahead]
+    other_core = [swapped(b, "core") for b in same_core]
+    blocks = [down_pair, *same_core, downs[1], *other_core]
     old_parts = layer_call(old_kernel, group_rows, slice_width, blocks, flags, hidden_old)
     grads, old_parts = lax.optimization_barrier((grads, old_parts))
     grads = sum_first(grads)
@@ -331,7 +330,7 @@
     live = jnp.logical_or(role == 0, positions < prefill_rows[0])
 
     def finish(total):
-        total = total.astype(BF).T
+        total = total.T
         return jnp.where(live[:, None], total, jnp.zeros_like(total))
 
     old_parts = old_parts.reshape(4, 2, 4, slice_width, group_rows)
@@ -342,12 +341,12 @@
     renewed = to_rank(new_in.astype(BF)).astype(BF)
     renewed = spread(renewed, NEAR)
     renewed = sum_first(spread(sum_first(renewed).astype(BF), "zh")).astype(BF)
-    near_old = shifted_sum(pair, "zl")
+    total_old = halved(pair, "zl", 1)
     new_parts = layer_call(new_kernel, group_rows, slice_width, blocks, flags, base, renewed, new_out.astype(BF))
-    near_new = sum_first(exchange(new_parts.reshape(8, 4, slice_width, group_rows), NEAR))
-    near = jnp.stack([near_old, near_new], axis=1).astype(BF)
-    layers = sum_first(exchange(near, "zh"))
-    layer_old, layer_new = finish(layers[0]), finish(layers[1])
+    near_new = exchange(new_parts.reshape(8, 4, slice_width, group_rows), NEAR)
+    total_old = halved(halved(halved(total_old, "zl", 2), "zh", 1), "zh", 2)
+    total_new = sum_first(exchange(sum_first(near_new).astype(BF), "zh")).astype(BF)
+    layer_old, layer_new = finish(total_old), finish(total_new)
     return (
         layer_old[None],
         layer_new[None],

time: 284 us -> 294 us (1.035)
  the two profiles are of different devices: /device:TPU:41 before, /device:TPU:24 now
where the time goes in v2:
time: 294 us; the launch traced here: 291 us
  starting transfers between devices  147 us (50%)
  waiting for transfers between devices  95.5 us (32%)
  Pallas kernels  23.8 us (8%)
  other arithmetic  11.8 us (4%)
  local copies, waits for them, and re-layouts  7.51 us (3%)
  matrix products  3.32 us (1%)
    all_to_all x9, starting transfers between devices, exchange(): return lax.all_to_all(pieces, axis, split_axis=0, concat_axis=0, tiled=True)  55 us
    ppermute x5, starting transfers between devices, plus_partner(): lax.ppermute(value, axis, [(i, i ^ step) for i in range(count)])  35.2 us
    all_to_all x9, waiting for transfers between devices, exchange(): return lax.all_to_all(pieces, axis, split_axis=0, concat_axis=0, tiled=True)  31.1 us
    ppermute x9, waiting for transfers between devices, swapped(): return lax.ppermute(value, axis, [(0, 1), (1, 0)])  29.9 us
    ppermute x9, starting transfers between devices, swapped(): return lax.ppermute(value, axis, [(0, 1), (1, 0)])  22.8 us
    ppermute x4, starting transfers between devices, halved(): got = lax.ppermute(give, axis, [(i, i ^ bit) for i in range(4)])  22.1 us
    ppermute x4, waiting for transfers between devices, halved(): got = lax.ppermute(give, axis, [(i, i ^ bit) for i in range(4)])  18.5 us
    ppermute x3, starting transfers between devices, shifted(): lax.ppermute(value, axis, [(i, (i + step) % count) for i in range(count)])  10.9 us
  transfers between devices with their start and end apart: 31, of which 19 were waited for; matrix products, arithmetic and copies ran while one was open for 4% of the time, Pallas kernels for 2%

profile of v2, /device:TPU:24, one launch (start us, length us, event | category | flops | bytes accessed | tf_op | source)
XLA Modules:
  0.0 291.1 jit_solution(17750357648638316589)
XLA Ops:
  2.0 3.7 %rows_by_x.1 = bf16[4,2,2,128,640]{4,3,2,1,0:T(8,128)(2,1)} custom-call(bf16[128,5120]{1,0:T(8,128)(2,1)} %bitcast.96, bf16[128,5120]{1,0:T(8,128)(2,1)} %cotangent_ref.1, f32[128,1]{1,0:T(8,128)} %copy.27.scale_ref), custom_call_target="tpu_custom_call" | custom-call | tf_op jit(solution)/shard_map/rows_by_x/pallas_call | solution.py:102
  5.7 4.4 %all-to-all-start = ((bf16[4,2,2,128,640]{4,3,2,1,0:T(8,128)(2,1)}), bf16[4,2,2,128,640]{4,3,2,1,0:T(8,128)(2,1)S(1)}, u32[]{:S(2)}, u32[]{:S(2)}) async-start(bf16[4,2,2,128,640]{4,3,2,1,0:T(8,128)(2,1)} %rows_by_x.1), calls=%async_computation | async-start | bytes 5242880 | tf_op jit(solution)/shard_map/all_to_all | solution.py:33
  17.1 6.3 %collective-permute-start.1 = (bf16[2,320,432]{2,1,0:T(8,128)(2,1)}, bf16[2,320,432]{2,1,0:T(8,128)(2,1)}, u32[]{:S(2)}, u32[]{:S(2)}) collective-permute-start(bf16[2,320,432]{2,1,0:T(8,128)(2,1)} %refs_0_), channel_id=1, source_target_pairs={{0,256},{256,0},{1,257},{257,1},{2,258},{258,2},{3,259},{259,3},{4... | collective-permute-start | bytes 1658888 | tf_op jit(solution)/shard_map/ppermute | solution.py:37
  31.1 4.3 %collective-permute-start.4 = (f32[64,128]{1,0:T(8,128)S(1)}, f32[64,128]{1,0:T(8,128)S(1)}, u32[]{:S(2)}, u32[]{:S(2)}) collective-permute-start(f32[64,128]{1,0:T(8,128)S(1)} %add.110), channel_id=1, source_target_pairs={{0,4},{2,6},{4,0},{6,2},{1,5},{3,7},{5,1},{7,3},{8,12},{10,14},{12... | collective-permute-start | bytes 98312 | tf_op jit(solution)/shard_map/ppermute | solution.py:56
  37.9 5.2 %collective-permute-done.2 = bf16[320,432]{1,0:T(8,128)(2,1)S(1)} collective-permute-done((bf16[320,432]{1,0:T(8,128)(2,1)S(1)}, bf16[320,432]{1,0:T(8,128)(2,1)S(1)}, u32[]{:S(2)}, u32[]{:S(2)}) %collective-permute-start.2) | collective-permute-done | bytes 276512 | tf_op jit(solution)/shard_map/ppermute | solution.py:37
  50.6 6.8 %partials.1 = bf16[4,3,432,128]{3,2,1,0:T(8,128)(2,1)} custom-call(s32[3]{0:T(128)} %pad_add_fusion.flag_ref, bf16[4,2,2,128,640]{4,3,2,1,0:T(8,128)(2,1)} %copy-done, bf16[2,320,432]{2,1,0:T(8,128)(2,1)} %refs_0_, bf16[2,320,432]{2,1,0:T(8,128)(2,1)} %collective-permute-done.1.refs_1_, bf16[2,320,432]{2,1,0:T(8,128)(2,1)} %collective-permute-done.5.refs_2_, ...), custom_call_target="tpu_custom_call" | custom-call | tf_op jit(solution)/shard_map/partials/pallas_call | solution.py:156
  57.4 4.7 %all-to-all-start.1 = ((bf16[4,3,432,128]{3,2,1,0:T(8,128)(2,1)}), bf16[4,3,432,128]{3,2,1,0:T(8,128)(2,1)S(1)}, u32[]{:S(2)}, u32[]{:S(2)}) async-start(bf16[4,3,432,128]{3,2,1,0:T(8,128)(2,1)} %partials.1), calls=%async_computation.1 | async-start | bytes 2654208 | tf_op jit(solution)/shard_map/all_to_all | solution.py:33
  62.1 9.2 %collective-permute-start.8 = (f32[64,128]{1,0:T(8,128)S(1)}, f32[64,128]{1,0:T(8,128)S(1)}, u32[]{:S(2)}, u32[]{:S(2)}) collective-permute-start(f32[64,128]{1,0:T(8,128)S(1)} %add.111), channel_id=1, source_target_pairs={{0,8},{8,0},{16,24},{24,16},{1,9},{9,1},{17,25},{25,17},{2,10},{10... | collective-permute-start | bytes 98312 | tf_op jit(solution)/shard_map/ppermute | solution.py:56
  73.2 16.1 %collective-permute-start.9 = (f32[64,128]{1,0:T(8,128)S(1)}, f32[64,128]{1,0:T(8,128)S(1)}, u32[]{:S(2)}, u32[]{:S(2)}) collective-permute-start(f32[64,128]{1,0:T(8,128)S(1)} %add.112), channel_id=1, source_target_pairs={{0,16},{8,24},{16,0},{24,8},{1,17},{9,25},{17,1},{25,9},{2,18},{10... | collective-permute-start | bytes 98312 | tf_op jit(solution)/shard_map/ppermute | solution.py:56
  96.9 4.0 %all-to-all-start.2 = ((bf16[8,64,128]{2,1,0:T(8,128)(2,1)}), bf16[8,64,128]{2,1,0:T(8,128)(2,1)S(1)}, u32[]{:S(2)}, u32[]{:S(2)}) async-start(bf16[8,64,128]{2,1,0:T(8,128)(2,1)} %broadcast_in_dim.57), calls=%async_computation.2 | async-start | bytes 262144 | tf_op jit(solution)/shard_map/all_to_all | solution.py:33
  100.9 4.1 %collective-permute-start.11 = (bf16[2,320,432]{2,1,0:T(8,128)(2,1)S(1)}, bf16[2,320,432]{2,1,0:T(8,128)(2,1)S(1)}, u32[]{:S(2)}, u32[]{:S(2)}) collective-permute-start(bf16[2,320,432]{2,1,0:T(8,128)(2,1)S(1)} %copy-done.2), channel_id=1, source_target_pairs={{0,64},{64,128},{128,192},{192,0},{1,65},{65,129},{129,193},{193,1... | collective-permute-start | bytes 1658888 | tf_op jit(solution)/shard_map/ppermute | solution.py:51
  107.2 12.0 %all-to-all-start.3 = ((bf16[4,64,128]{2,1,0:T(8,128)(2,1)}), bf16[4,64,128]{2,1,0:T(8,128)(2,1)S(1)}, u32[]{:S(2)}, u32[]{:S(2)}) async-start(bf16[4,64,128]{2,1,0:T(8,128)(2,1)} %broadcast_in_dim.58), calls=%async_computation.3 | async-start | bytes 131072 | tf_op jit(solution)/shard_map/all_to_all | solution.py:33
  119.2 4.9 %collective-permute-start.13 = (bf16[2,320,432]{2,1,0:T(8,128)(2,1)S(1)}, bf16[2,320,432]{2,1,0:T(8,128)(2,1)S(1)}, u32[]{:S(2)}, u32[]{:S(2)}) collective-permute-start(bf16[2,320,432]{2,1,0:T(8,128)(2,1)S(1)} %copy-done.2), channel_id=1, source_target_pairs={{0,192},{64,0},{128,64},{192,128},{1,193},{65,1},{129,65},{193,129... | collective-permute-start | bytes 1658888 | tf_op jit(solution)/shard_map/ppermute | solution.py:51
  126.0 6.2 %all-to-all-done.3 = bf16[4,64,128]{2,1,0:T(8,128)(2,1)S(1)} async-done(((bf16[4,64,128]{2,1,0:T(8,128)(2,1)}), bf16[4,64,128]{2,1,0:T(8,128)(2,1)S(1)}, u32[]{:S(2)}, u32[]{:S(2)}) %all-to-all-start.3) | async-done | bytes 65568 | tf_op jit(solution)/shard_map/all_to_all | solution.py:33
  135.5 6.5 %collective-permute-done.10 = bf16[64,592]{1,0:T(8,128)(2,1)S(1)} collective-permute-done((bf16[64,592]{1,0:T(8,128)(2,1)S(1)}, bf16[64,592]{1,0:T(8,128)(2,1)S(1)}, u32[]{:S(2)}, u32[]{:S(2)}) %collective-permute-start.10) | collective-permute-done | bytes 75808 | tf_op jit(solution)/shard_map/ppermute | solution.py:316
  150.3 4.6 %all-to-all-start.4 = ((bf16[8,64,592]{2,1,0:T(8,128)(2,1)}), bf16[8,64,592]{2,1,0:T(8,128)(2,1)}, u32[]{:S(2)}, u32[]{:S(2)}) async-start(bf16[8,64,592]{2,1,0:T(8,128)(2,1)} %broadcast_in_dim.59), calls=%async_computation.4 | async-start | bytes 1310720 | tf_op jit(solution)/shard_map/all_to_all | solution.py:33
  156.0 5.2 %shard_map.179 = bf16[32,160,128]{2,1,0:T(8,128)(2,1)} custom-call(s32[3]{0:T(128)} %pad_add_fusion.flag_ref, bf16[432,128]{1,0:T(8,128)(2,1)} %get-tuple-element.39.hidden_ref, bf16[2,320,432]{2,1,0:T(8,128)(2,1)} %copy-done.1, bf16[2,320,432]{2,1,0:T(8,128)(2,1)} %copy-done.5, bf16[2,320,432]{2,1,0:T(8,128)(2,1)} %copy-done.7, ...), custom_call_target="tpu_custom_call" | custom-call | tf_op jit(solution)/shard_map/pallas_call | solution.py:248
  161.2 5.6 %all-to-all-done.4 = bf16[8,64,592]{2,1,0:T(8,128)(2,1)} async-done(((bf16[8,64,592]{2,1,0:T(8,128)(2,1)}), bf16[8,64,592]{2,1,0:T(8,128)(2,1)}, u32[]{:S(2)}, u32[]{:S(2)}) %all-to-all-start.4) | async-done | bytes 606240 | tf_op jit(solution)/shard_map/all_to_all | solution.py:33
  170.5 5.1 %all-to-all-start.5 = ((bf16[8,64,128]{2,1,0:T(8,128)(2,1)}), bf16[8,64,128]{2,1,0:T(8,128)(2,1)S(1)}, u32[]{:S(2)}, u32[]{:S(2)}) async-start(bf16[8,64,128]{2,1,0:T(8,128)(2,1)} %broadcast_in_dim.61), calls=%async_computation.5 | async-start | bytes 262144 | tf_op jit(solution)/shard_map/all_to_all | solution.py:33
  175.6 5.6 %all-to-all-done.5 = bf16[8,64,128]{2,1,0:T(8,128)(2,1)S(1)} async-done(((bf16[8,64,128]{2,1,0:T(8,128)(2,1)}), bf16[8,64,128]{2,1,0:T(8,128)(2,1)S(1)}, u32[]{:S(2)}, u32[]{:S(2)}) %all-to-all-start.5) | async-done | bytes 131104 | tf_op jit(solution)/shard_map/all_to_all | solution.py:33
  181.8 6.7 %all-to-all-start.6 = ((bf16[4,64,128]{2,1,0:T(8,128)(2,1)}), bf16[4,64,128]{2,1,0:T(8,128)(2,1)S(1)}, u32[]{:S(2)}, u32[]{:S(2)}) async-start(bf16[4,64,128]{2,1,0:T(8,128)(2,1)} %broadcast_in_dim.62), calls=%async_computation.6 | async-start | bytes 131072 | tf_op jit(solution)/shard_map/all_to_all | solution.py:33
  189.4 12.2 %all-to-all-done.6 = bf16[4,64,128]{2,1,0:T(8,128)(2,1)S(1)} async-done(((bf16[4,64,128]{2,1,0:T(8,128)(2,1)}), bf16[4,64,128]{2,1,0:T(8,128)(2,1)S(1)}, u32[]{:S(2)}, u32[]{:S(2)}) %all-to-all-start.6) | async-done | bytes 65568 | tf_op jit(solution)/shard_map/all_to_all | solution.py:33
  202.1 5.6 %shard_map.180 = bf16[32,160,128]{2,1,0:T(8,128)(2,1)} custom-call(s32[3]{0:T(128)} %pad_add_fusion.flag_ref, f32[2,432,128]{2,1,0:T(8,128)} %get-tuple-element.44.base_ref, bf16[64,128]{1,0:T(8,128)(2,1)} %reduce_sum.85.reduced_ref, bf16[2,32,432]{2,1,0:T(8,128)(2,1)} %get-tuple-element.46.lift_ref, bf16[2,320,432]{2,1,0:T(8,128)(2,1)} %copy-done.1, ...), custom_call_target="tpu_custom_call" | custom-call | tf_op jit(solution)/shard_map/pallas_call | solution.py:248
  207.7 5.4 %all-to-all-start.7 = ((bf16[8,4,160,128]{3,2,1,0:T(8,128)(2,1)}), bf16[8,4,160,128]{3,2,1,0:T(8,128)(2,1)S(1)}, u32[]{:S(2)}, u32[]{:S(2)}) async-start(bf16[8,4,160,128]{3,2,1,0:T(8,128)(2,1)} %bitcast.91), calls=%async_computation.7 | async-start | bytes 2621440 | tf_op jit(solution)/shard_map/all_to_all | solution.py:33
  215.2 23.3 %collective-permute-done.17 = bf16[4,4,160,128]{3,2,1,0:T(8,128)(2,1)} collective-permute-done((bf16[4,4,160,128]{3,2,1,0:T(8,128)(2,1)S(1)}, bf16[4,4,160,128]{3,2,1,0:T(8,128)(2,1)}, u32[]{:S(2)}, u32[]{:S(2)}) %collective-permute-start.17) | collective-permute-done | bytes 655392 | tf_op jit(solution)/shard_map/ppermute | solution.py:37
  239.8 4.4 %collective-permute-start.18 = (bf16[2,4,160,128]{3,2,1,0:T(8,128)(2,1)S(1)}, bf16[2,4,160,128]{3,2,1,0:T(8,128)(2,1)S(1)}, u32[]{:S(2)}, u32[]{:S(2)}) collective-permute-start(bf16[2,4,160,128]{3,2,1,0:T(8,128)(2,1)S(1)} %dynamic-slice_bitcast_fusion.1), channel_id=1, source_target_pairs={{0,2},{2,0},{4,6},{6,4},{1,3},{3,1},{5,7},{7,5},{8,10},{10,8},{12,... | collective-permute-start | bytes 983048 | tf_op jit(solution)/shard_map/ppermute | solution.py:69
  244.2 6.9 %collective-permute-done.18 = bf16[2,4,160,128]{3,2,1,0:T(8,128)(2,1)S(1)} collective-permute-done((bf16[2,4,160,128]{3,2,1,0:T(8,128)(2,1)S(1)}, bf16[2,4,160,128]{3,2,1,0:T(8,128)(2,1)S(1)}, u32[]{:S(2)}, u32[]{:S(2)}) %collective-permute-start.18) | collective-permute-done | bytes 327712 | tf_op jit(solution)/shard_map/ppermute | solution.py:69
  251.3 4.6 %collective-permute-start.19 = (bf16[4,160,128]{2,1,0:T(8,128)(2,1)S(1)}, bf16[4,160,128]{2,1,0:T(8,128)(2,1)S(1)}, u32[]{:S(2)}, u32[]{:S(2)}) collective-permute-start(bf16[4,160,128]{2,1,0:T(8,128)(2,1)S(1)} %dynamic-slice_bitcast_fusion.2), channel_id=1, source_target_pairs={{0,4},{2,6},{4,0},{6,2},{1,5},{3,7},{5,1},{7,3},{8,12},{10,14},{12... | collective-permute-start | bytes 491528 | tf_op jit(solution)/shard_map/ppermute | solution.py:69
  255.9 6.3 %collective-permute-done.19 = bf16[4,160,128]{2,1,0:T(8,128)(2,1)S(1)} collective-permute-done((bf16[4,160,128]{2,1,0:T(8,128)(2,1)S(1)}, bf16[4,160,128]{2,1,0:T(8,128)(2,1)S(1)}, u32[]{:S(2)}, u32[]{:S(2)}) %collective-permute-start.19) | collective-permute-done | bytes 163872 | tf_op jit(solution)/shard_map/ppermute | solution.py:69
  265.3 8.1 %all-to-all-start.8 = ((bf16[4,160,128]{2,1,0:T(8,128)(2,1)}), bf16[4,160,128]{2,1,0:T(8,128)(2,1)S(1)}, u32[]{:S(2)}, u32[]{:S(2)}) async-start(bf16[4,160,128]{2,1,0:T(8,128)(2,1)} %reduce_sum.86), calls=%async_computation.8 | async-start | bytes 327680 | tf_op jit(solution)/shard_map/all_to_all | solution.py:33
  275.7 11.0 %collective-permute-start.21 = (bf16[160,128]{1,0:T(8,128)(2,1)S(1)}, bf16[160,128]{1,0:T(8,128)(2,1)S(1)}, u32[]{:S(2)}, u32[]{:S(2)}) collective-permute-start(bf16[160,128]{1,0:T(8,128)(2,1)S(1)} %dynamic-slice_bitcast_fusion.4), channel_id=1, source_target_pairs={{0,16},{8,24},{16,0},{24,8},{1,17},{9,25},{17,1},{25,9},{2,18},{10... | collective-permute-start | bytes 122888 | tf_op jit(solution)/shard_map/ppermute | solution.py:69
  286.9 3.6 %collective-permute-done.21 = bf16[160,128]{1,0:T(8,128)(2,1)S(1)} collective-permute-done((bf16[160,128]{1,0:T(8,128)(2,1)S(1)}, bf16[160,128]{1,0:T(8,128)(2,1)S(1)}, u32[]{:S(2)}, u32[]{:S(2)}) %collective-permute-start.21) | collective-permute-done | bytes 40992 | tf_op jit(solution)/shard_map/ppermute | solution.py:69
  (112 shorter events, 66.9 us)
Async XLA Ops:
  5.7 43.4 %all-to-all-start = ((bf16[4,2,2,128,640]{4,3,2,1,0:T(8,128)(2,1)}), bf16[4,2,2,128,640]{4,3,2,1,0:T(8,128)(2,1)S(1)}, u32[]{:S(2)}, u32[]{:S(2)}) async-start(bf16[4,2,2,128,640]{4,3,2,1,0:T(8,128)(2,1)} %rows_by_x.1), calls=%async_computation | async-start | bytes 5242880 | tf_op jit(solution)/shard_map/all_to_all | solution.py:33
  11.2 5.8 %collective-permute-start = (f32[64,128]{1,0:T(8,128)S(1)}, f32[64,128]{1,0:T(8,128)S(1)}, u32[]{:S(2)}, u32[]{:S(2)}) collective-permute-start(f32[64,128]{1,0:T(8,128)S(1)} %convolution_bitcast_fusion), channel_id=1, source_target_pairs={{0,1},{1,0},{2,3},{3,2},{4,5},{5,4},{6,7},{7,6},{8,9},{9,8},{10,11... | collective-permute-start | bytes 98312 | tf_op jit(solution)/shard_map/ppermute | solution.py:56
  17.1 26.0 %collective-permute-start.1 = (bf16[2,320,432]{2,1,0:T(8,128)(2,1)}, bf16[2,320,432]{2,1,0:T(8,128)(2,1)}, u32[]{:S(2)}, u32[]{:S(2)}) collective-permute-start(bf16[2,320,432]{2,1,0:T(8,128)(2,1)} %refs_0_), channel_id=1, source_target_pairs={{0,256},{256,0},{1,257},{257,1},{2,258},{258,2},{3,259},{259,3},{4... | collective-permute-start | bytes 1658888 | tf_op jit(solution)/shard_map/ppermute | solution.py:37
  23.4 19.6 %collective-permute-start.2 = (bf16[320,432]{1,0:T(8,128)(2,1)S(1)}, bf16[320,432]{1,0:T(8,128)(2,1)S(1)}, u32[]{:S(2)}, u32[]{:S(2)}) collective-permute-start(bf16[320,432]{1,0:T(8,128)(2,1)S(1)} %bitcast.101), channel_id=1, source_target_pairs={{0,256},{256,0},{1,257},{257,1},{2,258},{258,2},{3,259},{259,3},{4... | collective-permute-start | bytes 829448 | tf_op jit(solution)/shard_map/ppermute | solution.py:37
  25.3 5.8 %collective-permute-start.3 = (f32[64,128]{1,0:T(8,128)S(1)}, f32[64,128]{1,0:T(8,128)S(1)}, u32[]{:S(2)}, u32[]{:S(2)}) collective-permute-start(f32[64,128]{1,0:T(8,128)S(1)} %add.109), channel_id=1, source_target_pairs={{0,2},{2,0},{4,6},{6,4},{1,3},{3,1},{5,7},{7,5},{8,10},{10,8},{12,... | collective-permute-start | bytes 98312 | tf_op jit(solution)/shard_map/ppermute | solution.py:56
  31.1 6.7 %collective-permute-start.4 = (f32[64,128]{1,0:T(8,128)S(1)}, f32[64,128]{1,0:T(8,128)S(1)}, u32[]{:S(2)}, u32[]{:S(2)}) collective-permute-start(f32[64,128]{1,0:T(8,128)S(1)} %add.110), channel_id=1, source_target_pairs={{0,4},{2,6},{4,0},{6,2},{1,5},{3,7},{5,1},{7,3},{8,12},{10,14},{12... | collective-permute-start | bytes 98312 | tf_op jit(solution)/shard_map/ppermute | solution.py:56
  35.4 13.6 %collective-permute-start.5 = (bf16[2,320,432]{2,1,0:T(8,128)(2,1)}, bf16[2,320,432]{2,1,0:T(8,128)(2,1)}, u32[]{:S(2)}, u32[]{:S(2)}) collective-permute-start(bf16[2,320,432]{2,1,0:T(8,128)(2,1)} %refs_0_), channel_id=1, source_target_pairs={{0,32},{32,0},{1,33},{33,1},{2,34},{34,2},{3,35},{35,3},{4,36},{36... | collective-permute-start | bytes 1658888 | tf_op jit(solution)/shard_map/ppermute | solution.py:37
  44.1 5.0 %collective-permute-start.7 = (bf16[2,320,432]{2,1,0:T(8,128)(2,1)S(1)}, bf16[2,320,432]{2,1,0:T(8,128)(2,1)}, u32[]{:S(2)}, u32[]{:S(2)}) collective-permute-start(bf16[2,320,432]{2,1,0:T(8,128)(2,1)S(1)} %pad_maximum_fusion.refs_4_.refs_0_), channel_id=1, source_target_pairs={{0,32},{32,0},{1,33},{33,1},{2,34},{34,2},{3,35},{35,3},{4,36},{36... | collective-permute-start | bytes 1658888 | tf_op jit(solution)/shard_map/ppermute | solution.py:37
  46.0 4.5 %collective-permute-start.6 = (bf16[2,320,432]{2,1,0:T(8,128)(2,1)}, bf16[2,320,432]{2,1,0:T(8,128)(2,1)}, u32[]{:S(2)}, u32[]{:S(2)}) collective-permute-start(bf16[2,320,432]{2,1,0:T(8,128)(2,1)} %collective-permute-done.1.refs_1_), channel_id=1, source_target_pairs={{0,32},{32,0},{1,33},{33,1},{2,34},{34,2},{3,35},{35,3},{4,36},{36... | collective-permute-start | bytes 1658888 | tf_op jit(solution)/shard_map/ppermute | solution.py:37
  57.4 34.4 %all-to-all-start.1 = ((bf16[4,3,432,128]{3,2,1,0:T(8,128)(2,1)}), bf16[4,3,432,128]{3,2,1,0:T(8,128)(2,1)S(1)}, u32[]{:S(2)}, u32[]{:S(2)}) async-start(bf16[4,3,432,128]{3,2,1,0:T(8,128)(2,1)} %partials.1), calls=%async_computation.1 | async-start | bytes 2654208 | tf_op jit(solution)/shard_map/all_to_all | solution.py:33
  62.1 38.9 %copy-start.2 = (bf16[2,320,432]{2,1,0:T(8,128)(2,1)S(1)}, bf16[2,320,432]{2,1,0:T(8,128)(2,1)}, u32[]{:S(2)}) copy-start(bf16[2,320,432]{2,1,0:T(8,128)(2,1)} %copy-done.1) | copy-start | bytes 1658884
  62.1 11.1 %collective-permute-start.8 = (f32[64,128]{1,0:T(8,128)S(1)}, f32[64,128]{1,0:T(8,128)S(1)}, u32[]{:S(2)}, u32[]{:S(2)}) collective-permute-start(f32[64,128]{1,0:T(8,128)S(1)} %add.111), channel_id=1, source_target_pairs={{0,8},{8,0},{16,24},{24,16},{1,9},{9,1},{17,25},{25,17},{2,10},{10... | collective-permute-start | bytes 98312 | tf_op jit(solution)/shard_map/ppermute | solution.py:56
  73.2 18.0 %collective-permute-start.9 = (f32[64,128]{1,0:T(8,128)S(1)}, f32[64,128]{1,0:T(8,128)S(1)}, u32[]{:S(2)}, u32[]{:S(2)}) collective-permute-start(f32[64,128]{1,0:T(8,128)S(1)} %add.112), channel_id=1, source_target_pairs={{0,16},{8,24},{16,0},{24,8},{1,17},{9,25},{17,1},{25,9},{2,18},{10... | collective-permute-start | bytes 98312 | tf_op jit(solution)/shard_map/ppermute | solution.py:56
  96.9 9.6 %all-to-all-start.2 = ((bf16[8,64,128]{2,1,0:T(8,128)(2,1)}), bf16[8,64,128]{2,1,0:T(8,128)(2,1)S(1)}, u32[]{:S(2)}, u32[]{:S(2)}) async-start(bf16[8,64,128]{2,1,0:T(8,128)(2,1)} %broadcast_in_dim.57), calls=%async_computation.2 | async-start | bytes 262144 | tf_op jit(solution)/shard_map/all_to_all | solution.py:33
  100.9 23.1 %collective-permute-start.11 = (bf16[2,320,432]{2,1,0:T(8,128)(2,1)S(1)}, bf16[2,320,432]{2,1,0:T(8,128)(2,1)S(1)}, u32[]{:S(2)}, u32[]{:S(2)}) collective-permute-start(bf16[2,320,432]{2,1,0:T(8,128)(2,1)S(1)} %copy-done.2), channel_id=1, source_target_pairs={{0,64},{64,128},{128,192},{192,0},{1,65},{65,129},{129,193},{193,1... | collective-permute-start | bytes 1658888 | tf_op jit(solution)/shard_map/ppermute | solution.py:51
  107.2 25.0 %all-to-all-start.3 = ((bf16[4,64,128]{2,1,0:T(8,128)(2,1)}), bf16[4,64,128]{2,1,0:T(8,128)(2,1)S(1)}, u32[]{:S(2)}, u32[]{:S(2)}) async-start(bf16[4,64,128]{2,1,0:T(8,128)(2,1)} %broadcast_in_dim.58), calls=%async_computation.3 | async-start | bytes 131072 | tf_op jit(solution)/shard_map/all_to_all | solution.py:33
  119.2 23.8 %collective-permute-start.13 = (bf16[2,320,432]{2,1,0:T(8,128)(2,1)S(1)}, bf16[2,320,432]{2,1,0:T(8,128)(2,1)S(1)}, u32[]{:S(2)}, u32[]{:S(2)}) collective-permute-start(bf16[2,320,432]{2,1,0:T(8,128)(2,1)S(1)} %copy-done.2), channel_id=1, source_target_pairs={{0,192},{64,0},{128,64},{192,128},{1,193},{65,1},{129,65},{193,129... | collective-permute-start | bytes 1658888 | tf_op jit(solution)/shard_map/ppermute | solution.py:51
  124.1 19.0 %collective-permute-start.12 = (bf16[2,320,432]{2,1,0:T(8,128)(2,1)S(1)}, bf16[2,320,432]{2,1,0:T(8,128)(2,1)S(1)}, u32[]{:S(2)}, u32[]{:S(2)}) collective-permute-start(bf16[2,320,432]{2,1,0:T(8,128)(2,1)S(1)} %collective-permute-done.11.refs_1_), channel_id=1, source_target_pairs={{0,64},{64,128},{128,192},{192,0},{1,65},{65,129},{129,193},{193,1... | collective-permute-start | bytes 1658888 | tf_op jit(solution)/shard_map/ppermute | solution.py:51
  134.2 7.8 %collective-permute-start.10 = (bf16[64,592]{1,0:T(8,128)(2,1)S(1)}, bf16[64,592]{1,0:T(8,128)(2,1)S(1)}, u32[]{:S(2)}, u32[]{:S(2)}) collective-permute-start(bf16[64,592]{1,0:T(8,128)(2,1)S(1)} %pad_maximum_fusion.1), channel_id=1, source_target_pairs={{0,256},{1,257},{2,258},{3,259},{4,260},{5,261},{6,262},{7,263},{8... | collective-permute-start | bytes 227336 | tf_op jit(solution)/shard_map/ppermute | solution.py:316
  143.1 11.9 %collective-permute-start.14 = (bf16[2,320,432]{2,1,0:T(8,128)(2,1)S(1)}, bf16[2,320,432]{2,1,0:T(8,128)(2,1)S(1)}, u32[]{:S(2)}, u32[]{:S(2)}) collective-permute-start(bf16[2,320,432]{2,1,0:T(8,128)(2,1)S(1)} %collective-permute-done.11.refs_1_), channel_id=1, source_target_pairs={{0,32},{32,0},{1,33},{33,1},{2,34},{34,2},{3,35},{35,3},{4,36},{36... | collective-permute-start | bytes 1658888 | tf_op jit(solution)/shard_map/ppermute | solution.py:37
  145.0 9.9 %collective-permute-start.15 = (bf16[2,320,432]{2,1,0:T(8,128)(2,1)S(1)}, bf16[2,320,432]{2,1,0:T(8,128)(2,1)S(1)}, u32[]{:S(2)}, u32[]{:S(2)}) collective-permute-start(bf16[2,320,432]{2,1,0:T(8,128)(2,1)S(1)} %collective-permute-done.12.refs_2_), channel_id=1, source_target_pairs={{0,32},{32,0},{1,33},{33,1},{2,34},{34,2},{3,35},{35,3},{4,36},{36... | collective-permute-start | bytes 1658888 | tf_op jit(solution)/shard_map/ppermute | solution.py:37
  147.4 7.5 %collective-permute-start.16 = (bf16[2,320,432]{2,1,0:T(8,128)(2,1)S(1)}, bf16[2,320,432]{2,1,0:T(8,128)(2,1)}, u32[]{:S(2)}, u32[]{:S(2)}) collective-permute-start(bf16[2,320,432]{2,1,0:T(8,128)(2,1)S(1)} %collective-permute-done.13.refs_3_), channel_id=1, source_target_pairs={{0,32},{32,0},{1,33},{33,1},{2,34},{34,2},{3,35},{35,3},{4,36},{36... | collective-permute-start | bytes 1658888 | tf_op jit(solution)/shard_map/ppermute | solution.py:37
  150.3 16.5 %all-to-all-start.4 = ((bf16[8,64,592]{2,1,0:T(8,128)(2,1)}), bf16[8,64,592]{2,1,0:T(8,128)(2,1)}, u32[]{:S(2)}, u32[]{:S(2)}) async-start(bf16[8,64,592]{2,1,0:T(8,128)(2,1)} %broadcast_in_dim.59), calls=%async_computation.4 | async-start | bytes 1310720 | tf_op jit(solution)/shard_map/all_to_all | solution.py:33
  170.5 10.7 %all-to-all-start.5 = ((bf16[8,64,128]{2,1,0:T(8,128)(2,1)}), bf16[8,64,128]{2,1,0:T(8,128)(2,1)S(1)}, u32[]{:S(2)}, u32[]{:S(2)}) async-start(bf16[8,64,128]{2,1,0:T(8,128)(2,1)} %broadcast_in_dim.61), calls=%async_computation.5 | async-start | bytes 262144 | tf_op jit(solution)/shard_map/all_to_all | solution.py:33
  181.8 19.7 %all-to-all-start.6 = ((bf16[4,64,128]{2,1,0:T(8,128)(2,1)}), bf16[4,64,128]{2,1,0:T(8,128)(2,1)S(1)}, u32[]{:S(2)}, u32[]{:S(2)}) async-start(bf16[4,64,128]{2,1,0:T(8,128)(2,1)} %broadcast_in_dim.62), calls=%async_computation.6 | async-start | bytes 131072 | tf_op jit(solution)/shard_map/all_to_all | solution.py:33
  207.7 56.7 %all-to-all-start.7 = ((bf16[8,4,160,128]{3,2,1,0:T(8,128)(2,1)}), bf16[8,4,160,128]{3,2,1,0:T(8,128)(2,1)S(1)}, u32[]{:S(2)}, u32[]{:S(2)}) async-start(bf16[8,4,160,128]{3,2,1,0:T(8,128)(2,1)} %bitcast.91), calls=%async_computation.7 | async-start | bytes 2621440 | tf_op jit(solution)/shard_map/all_to_all | solution.py:33
  213.2 25.3 %collective-permute-start.17 = (bf16[4,4,160,128]{3,2,1,0:T(8,128)(2,1)S(1)}, bf16[4,4,160,128]{3,2,1,0:T(8,128)(2,1)}, u32[]{:S(2)}, u32[]{:S(2)}) collective-permute-start(bf16[4,4,160,128]{3,2,1,0:T(8,128)(2,1)S(1)} %dynamic-slice_bitcast_fusion), channel_id=1, source_target_pairs={{0,1},{1,0},{2,3},{3,2},{4,5},{5,4},{6,7},{7,6},{8,9},{9,8},{10,11... | collective-permute-start | bytes 1966088 | tf_op jit(solution)/shard_map/ppermute | solution.py:37
  239.8 11.4 %collective-permute-start.18 = (bf16[2,4,160,128]{3,2,1,0:T(8,128)(2,1)S(1)}, bf16[2,4,160,128]{3,2,1,0:T(8,128)(2,1)S(1)}, u32[]{:S(2)}, u32[]{:S(2)}) collective-permute-start(bf16[2,4,160,128]{3,2,1,0:T(8,128)(2,1)S(1)} %dynamic-slice_bitcast_fusion.1), channel_id=1, source_target_pairs={{0,2},{2,0},{4,6},{6,4},{1,3},{3,1},{5,7},{7,5},{8,10},{10,8},{12,... | collective-permute-start | bytes 983048 | tf_op jit(solution)/shard_map/ppermute | solution.py:69
  251.3 10.9 %collective-permute-start.19 = (bf16[4,160,128]{2,1,0:T(8,128)(2,1)S(1)}, bf16[4,160,128]{2,1,0:T(8,128)(2,1)S(1)}, u32[]{:S(2)}, u32[]{:S(2)}) collective-permute-start(bf16[4,160,128]{2,1,0:T(8,128)(2,1)S(1)} %dynamic-slice_bitcast_fusion.2), channel_id=1, source_target_pairs={{0,4},{2,6},{4,0},{6,2},{1,5},{3,7},{5,1},{7,3},{8,12},{10,14},{12... | collective-permute-start | bytes 491528 | tf_op jit(solution)/shard_map/ppermute | solution.py:69
  262.3 13.4 %collective-permute-start.20 = (bf16[2,160,128]{2,1,0:T(8,128)(2,1)S(1)}, bf16[2,160,128]{2,1,0:T(8,128)(2,1)S(1)}, u32[]{:S(2)}, u32[]{:S(2)}) collective-permute-start(bf16[2,160,128]{2,1,0:T(8,128)(2,1)S(1)} %dynamic-slice_bitcast_fusion.3), channel_id=1, source_target_pairs={{0,8},{8,0},{16,24},{24,16},{1,9},{9,1},{17,25},{25,17},{2,10},{10... | collective-permute-start | bytes 245768 | tf_op jit(solution)/shard_map/ppermute | solution.py:69
  265.3 21.6 %all-to-all-start.8 = ((bf16[4,160,128]{2,1,0:T(8,128)(2,1)}), bf16[4,160,128]{2,1,0:T(8,128)(2,1)S(1)}, u32[]{:S(2)}, u32[]{:S(2)}) async-start(bf16[4,160,128]{2,1,0:T(8,128)(2,1)} %reduce_sum.86), calls=%async_computation.8 | async-start | bytes 327680 | tf_op jit(solution)/shard_map/all_to_all | solution.py:33
  275.7 14.7 %collective-permute-start.21 = (bf16[160,128]{1,0:T(8,128)(2,1)S(1)}, bf16[160,128]{1,0:T(8,128)(2,1)S(1)}, u32[]{:S(2)}, u32[]{:S(2)}) collective-permute-start(bf16[160,128]{1,0:T(8,128)(2,1)S(1)} %dynamic-slice_bitcast_fusion.4), channel_id=1, source_target_pairs={{0,16},{8,24},{16,0},{24,8},{1,17},{9,25},{17,1},{25,9},{2,18},{10... | collective-permute-start | bytes 122888 | tf_op jit(solution)/shard_map/ppermute | solution.py:69
  (16 other events, 199.2 us)

commit v3 on v1

--- a/solution.py
+++ b/solution.py
@@ -294,9 +294,10 @@
     weights = (own_weight, other_half, swapped(own_weight, "core"), swapped(other_half, "core"))
     down_pair = jnp.stack([own_down, other_down])
     downs = (down_pair, swapped(down_pair, "core"))
+    reduced = plus_partner(reduced, "zh", 1)
     rows, reduced = lax.optimization_barrier((rows, reduced))
     pieces = exchange(partials(flags, rows, weights, downs), "x")
-    reduced = plus_partner(plus_partner(reduced, "zh", 1), "zh", 2).astype(BF)
+    reduced = plus_partner(reduced, "zh", 2).astype(BF)
     base, hidden_old, through_part, out_part = middle(flags, pieces, reduced, out_bf)
 
     down_first, _ = lax.optimization_barrier((down_pair, pieces))
@@ -304,7 +305,7 @@
     through = spread(through, "zh")
     through = sum_first(through).astype(BF)
     behind, ahead = shifted(down_first, "x", 1), shifted(down_first, "x", 3)
-    across = jnp.stack([shifted(behind[0], "x", 1), shifted(ahead[1], "x", 3)])
+    across = shifted(behind, "x", 1)
     same_core = [behind, across, ahead]
 
     def to_both_halves(value):

time: 284 us -> 285 us (level)
  the two profiles are of different devices: /device:TPU:41 before, /device:TPU:57 now
where the time goes in v3:
time: 285 us; the launch traced here: 283 us
  starting transfers between devices  135 us (47%)
  waiting for transfers between devices  99.8 us (35%)
  Pallas kernels  23.8 us (8%)
  other arithmetic  11 us (4%)
  local copies, waits for them, and re-layouts  7.76 us (3%)
  matrix products  3.32 us (1%)
    all_to_all x9, waiting for transfers between devices, exchange(): return lax.all_to_all(pieces, axis, split_axis=0, concat_axis=0, tiled=True)  53.9 us
    all_to_all x9, starting transfers between devices, exchange(): return lax.all_to_all(pieces, axis, split_axis=0, concat_axis=0, tiled=True)  50.2 us
    ppermute x9, starting transfers between devices, swapped(): return lax.ppermute(value, axis, [(0, 1), (1, 0)])  33.5 us
    ppermute x5, starting transfers between devices, plus_partner(): lax.ppermute(value, axis, [(i, i ^ step) for i in range(count)])  31 us
    ppermute x9, waiting for transfers between devices, swapped(): return lax.ppermute(value, axis, [(0, 1), (1, 0)])  29.7 us
    ppermute x6, starting transfers between devices, shifted(): lax.ppermute(value, axis, [(i, (i + step) % count) for i in range(count)])  18.2 us
    pallas_call x2, Pallas kernels, layer_call(): pl.pallas_call(kernel, out_shape=jax.ShapeDtypeStruct((32, width, group),...  10.7 us
    ppermute x6, waiting for transfers between devices, shifted(): lax.ppermute(value, axis, [(i, (i + step) % count) for i in range(count)])  9.92 us
  transfers between devices with their start and end apart: 31, of which 14 were waited for; matrix products, arithmetic and copies ran while one was open for 4% of the time, Pallas kernels for 3%

profile of v3, /device:TPU:57, one launch (start us, length us, event | category | flops | bytes accessed | tf_op | source)
XLA Modules:
  0.0 283.0 jit_solution(591207949511942656)
XLA Ops:
  2.0 3.7 %rows_by_x.1 = bf16[4,2,2,128,640]{4,3,2,1,0:T(8,128)(2,1)} custom-call(bf16[128,5120]{1,0:T(8,128)(2,1)} %bitcast.94, bf16[128,5120]{1,0:T(8,128)(2,1)} %cotangent_ref.1, f32[128,1]{1,0:T(8,128)} %copy.25.scale_ref), custom_call_target="tpu_custom_call" | custom-call | tf_op jit(solution)/shard_map/rows_by_x/pallas_call | solution.py:98
  5.7 4.1 %all-to-all-start = ((bf16[4,2,2,128,640]{4,3,2,1,0:T(8,128)(2,1)}), bf16[4,2,2,128,640]{4,3,2,1,0:T(8,128)(2,1)S(1)}, u32[]{:S(2)}, u32[]{:S(2)}) async-start(bf16[4,2,2,128,640]{4,3,2,1,0:T(8,128)(2,1)} %rows_by_x.1), calls=%async_computation | async-start | bytes 5242880 | tf_op jit(solution)/shard_map/all_to_all | solution.py:33
  18.8 3.9 %collective-permute-start.2 = (bf16[320,432]{1,0:T(8,128)(2,1)S(1)}, bf16[320,432]{1,0:T(8,128)(2,1)S(1)}, u32[]{:S(2)}, u32[]{:S(2)}) collective-permute-start(bf16[320,432]{1,0:T(8,128)(2,1)S(1)} %bitcast.98), channel_id=1, source_target_pairs={{0,256},{256,0},{1,257},{257,1},{2,258},{258,2},{3,259},{259,3},{4... | collective-permute-start | bytes 829448 | tf_op jit(solution)/shard_map/ppermute | solution.py:37
  27.8 4.9 %collective-permute-start.4 = (f32[64,128]{1,0:T(8,128)S(1)}, f32[64,128]{1,0:T(8,128)S(1)}, u32[]{:S(2)}, u32[]{:S(2)}) collective-permute-start(f32[64,128]{1,0:T(8,128)S(1)} %add.100), channel_id=1, source_target_pairs={{0,4},{2,6},{4,0},{6,2},{1,5},{3,7},{5,1},{7,3},{8,12},{10,14},{12... | collective-permute-start | bytes 98312 | tf_op jit(solution)/shard_map/ppermute | solution.py:56
  32.7 5.3 %collective-permute-start.6 = (bf16[2,320,432]{2,1,0:T(8,128)(2,1)}, bf16[2,320,432]{2,1,0:T(8,128)(2,1)}, u32[]{:S(2)}, u32[]{:S(2)}) collective-permute-start(bf16[2,320,432]{2,1,0:T(8,128)(2,1)} %refs_0_), channel_id=1, source_target_pairs={{0,32},{32,0},{1,33},{33,1},{2,34},{34,2},{3,35},{35,3},{4,36},{36... | collective-permute-start | bytes 1658888 | tf_op jit(solution)/shard_map/ppermute | solution.py:37
  42.1 4.6 %collective-permute-start.8 = (bf16[2,320,432]{2,1,0:T(8,128)(2,1)S(1)}, bf16[2,320,432]{2,1,0:T(8,128)(2,1)}, u32[]{:S(2)}, u32[]{:S(2)}) collective-permute-start(bf16[2,320,432]{2,1,0:T(8,128)(2,1)S(1)} %pad_maximum_fusion.refs_4_.refs_0_), channel_id=1, source_target_pairs={{0,32},{32,0},{1,33},{33,1},{2,34},{34,2},{3,35},{35,3},{4,36},{36... | collective-permute-start | bytes 1658888 | tf_op jit(solution)/shard_map/ppermute | solution.py:37
  48.6 8.8 %collective-permute-start.5 = (f32[64,128]{1,0:T(8,128)S(1)}, f32[64,128]{1,0:T(8,128)S(1)}, u32[]{:S(2)}, u32[]{:S(2)}) collective-permute-start(f32[64,128]{1,0:T(8,128)S(1)} %add.101), channel_id=1, source_target_pairs={{0,8},{8,0},{16,24},{24,16},{1,9},{9,1},{17,25},{25,17},{2,10},{10... | collective-permute-start | bytes 98312 | tf_op jit(solution)/shard_map/ppermute | solution.py:56
  60.3 6.8 %partials.1 = bf16[4,3,432,128]{3,2,1,0:T(8,128)(2,1)} custom-call(s32[3]{0:T(128)} %pad_add_fusion.flag_ref, bf16[4,2,2,128,640]{4,3,2,1,0:T(8,128)(2,1)} %copy-done, bf16[2,320,432]{2,1,0:T(8,128)(2,1)} %refs_0_, bf16[2,320,432]{2,1,0:T(8,128)(2,1)} %collective-permute-done.1.refs_1_, bf16[2,320,432]{2,1,0:T(8,128)(2,1)} %collective-permute-done.6.refs_2_, ...), custom_call_target="tpu_custom_call" | custom-call | tf_op jit(solution)/shard_map/partials/pallas_call | solution.py:152
  67.1 4.4 %all-to-all-start.1 = ((bf16[4,3,432,128]{3,2,1,0:T(8,128)(2,1)}), bf16[4,3,432,128]{3,2,1,0:T(8,128)(2,1)S(1)}, u32[]{:S(2)}, u32[]{:S(2)}) async-start(bf16[4,3,432,128]{3,2,1,0:T(8,128)(2,1)} %partials.1), calls=%async_computation.1 | async-start | bytes 2654208 | tf_op jit(solution)/shard_map/all_to_all | solution.py:33
  71.5 13.0 %collective-permute-start.9 = (f32[64,128]{1,0:T(8,128)S(1)}, f32[64,128]{1,0:T(8,128)S(1)}, u32[]{:S(2)}, u32[]{:S(2)}) collective-permute-start(f32[64,128]{1,0:T(8,128)S(1)} %add.102), channel_id=1, source_target_pairs={{0,16},{8,24},{16,0},{24,8},{1,17},{9,25},{17,1},{25,9},{2,18},{10... | collective-permute-start | bytes 98312 | tf_op jit(solution)/shard_map/ppermute | solution.py:56
  94.8 7.6 %all-to-all-start.2 = ((bf16[8,64,128]{2,1,0:T(8,128)(2,1)}), bf16[8,64,128]{2,1,0:T(8,128)(2,1)S(1)}, u32[]{:S(2)}, u32[]{:S(2)}) async-start(bf16[8,64,128]{2,1,0:T(8,128)(2,1)} %broadcast_in_dim.57), calls=%async_computation.2 | async-start | bytes 262144 | tf_op jit(solution)/shard_map/all_to_all | solution.py:33
  102.4 4.3 %collective-permute-start.14 = (bf16[2,320,432]{2,1,0:T(8,128)(2,1)S(1)}, bf16[2,320,432]{2,1,0:T(8,128)(2,1)S(1)}, u32[]{:S(2)}, u32[]{:S(2)}) collective-permute-start(bf16[2,320,432]{2,1,0:T(8,128)(2,1)S(1)} %copy-done.2), channel_id=1, source_target_pairs={{0,192},{64,0},{128,64},{192,128},{1,193},{65,1},{129,65},{193,129... | collective-permute-start | bytes 1658888 | tf_op jit(solution)/shard_map/ppermute | solution.py:51
  107.7 9.1 %all-to-all-start.3 = ((bf16[4,64,128]{2,1,0:T(8,128)(2,1)}), bf16[4,64,128]{2,1,0:T(8,128)(2,1)S(1)}, u32[]{:S(2)}, u32[]{:S(2)}) async-start(bf16[4,64,128]{2,1,0:T(8,128)(2,1)} %broadcast_in_dim.58), calls=%async_computation.3 | async-start | bytes 131072 | tf_op jit(solution)/shard_map/all_to_all | solution.py:33
  120.0 8.6 %all-to-all-done.3 = bf16[4,64,128]{2,1,0:T(8,128)(2,1)S(1)} async-done(((bf16[4,64,128]{2,1,0:T(8,128)(2,1)}), bf16[4,64,128]{2,1,0:T(8,128)(2,1)S(1)}, u32[]{:S(2)}, u32[]{:S(2)}) %all-to-all-start.3) | async-done | bytes 65568 | tf_op jit(solution)/shard_map/all_to_all | solution.py:33
  131.9 7.7 %collective-permute-start.15 = (bf16[2,320,432]{2,1,0:T(8,128)(2,1)S(1)}, bf16[2,320,432]{2,1,0:T(8,128)(2,1)S(1)}, u32[]{:S(2)}, u32[]{:S(2)}) collective-permute-start(bf16[2,320,432]{2,1,0:T(8,128)(2,1)S(1)} %collective-permute-done.12.refs_1_), channel_id=1, source_target_pairs={{0,32},{32,0},{1,33},{33,1},{2,34},{34,2},{3,35},{35,3},{4,36},{36... | collective-permute-start | bytes 1658888 | tf_op jit(solution)/shard_map/ppermute | solution.py:37
  141.7 3.2 %collective-permute-start.16 = (bf16[2,320,432]{2,1,0:T(8,128)(2,1)S(1)}, bf16[2,320,432]{2,1,0:T(8,128)(2,1)}, u32[]{:S(2)}, u32[]{:S(2)}) collective-permute-start(bf16[2,320,432]{2,1,0:T(8,128)(2,1)S(1)} %collective-permute-done.13.refs_2_), channel_id=1, source_target_pairs={{0,32},{32,0},{1,33},{33,1},{2,34},{34,2},{3,35},{35,3},{4,36},{36... | collective-permute-start | bytes 1658888 | tf_op jit(solution)/shard_map/ppermute | solution.py:37
  145.8 4.4 %all-to-all-start.4 = ((bf16[8,64,592]{2,1,0:T(8,128)(2,1)}), bf16[8,64,592]{2,1,0:T(8,128)(2,1)}, u32[]{:S(2)}, u32[]{:S(2)}) async-start(bf16[8,64,592]{2,1,0:T(8,128)(2,1)} %broadcast_in_dim.59), calls=%async_computation.4 | async-start | bytes 1310720 | tf_op jit(solution)/shard_map/all_to_all | solution.py:33
  151.3 5.2 %shard_map.179 = bf16[32,160,128]{2,1,0:T(8,128)(2,1)} custom-call(s32[3]{0:T(128)} %pad_add_fusion.flag_ref, bf16[432,128]{1,0:T(8,128)(2,1)} %get-tuple-element.39.hidden_ref, bf16[2,320,432]{2,1,0:T(8,128)(2,1)} %copy-done.1, bf16[2,320,432]{2,1,0:T(8,128)(2,1)} %copy-done.5, bf16[2,320,432]{2,1,0:T(8,128)(2,1)} %copy-done.7, ...), custom_call_target="tpu_custom_call" | custom-call | tf_op jit(solution)/shard_map/pallas_call | solution.py:244
  156.5 4.6 %all-to-all-done.4 = bf16[8,64,592]{2,1,0:T(8,128)(2,1)} async-done(((bf16[8,64,592]{2,1,0:T(8,128)(2,1)}), bf16[8,64,592]{2,1,0:T(8,128)(2,1)}, u32[]{:S(2)}, u32[]{:S(2)}) %all-to-all-start.4) | async-done | bytes 606240 | tf_op jit(solution)/shard_map/all_to_all | solution.py:33
  164.9 4.7 %all-to-all-start.5 = ((bf16[8,64,128]{2,1,0:T(8,128)(2,1)}), bf16[8,64,128]{2,1,0:T(8,128)(2,1)S(1)}, u32[]{:S(2)}, u32[]{:S(2)}) async-start(bf16[8,64,128]{2,1,0:T(8,128)(2,1)} %broadcast_in_dim.60), calls=%async_computation.5 | async-start | bytes 262144 | tf_op jit(solution)/shard_map/all_to_all | solution.py:33
  169.6 4.6 %all-to-all-done.5 = bf16[8,64,128]{2,1,0:T(8,128)(2,1)S(1)} async-done(((bf16[8,64,128]{2,1,0:T(8,128)(2,1)}), bf16[8,64,128]{2,1,0:T(8,128)(2,1)S(1)}, u32[]{:S(2)}, u32[]{:S(2)}) %all-to-all-start.5) | async-done | bytes 131104 | tf_op jit(solution)/shard_map/all_to_all | solution.py:33
  174.9 6.7 %all-to-all-start.6 = ((bf16[4,64,128]{2,1,0:T(8,128)(2,1)}), bf16[4,64,128]{2,1,0:T(8,128)(2,1)S(1)}, u32[]{:S(2)}, u32[]{:S(2)}) async-start(bf16[4,64,128]{2,1,0:T(8,128)(2,1)} %broadcast_in_dim.61), calls=%async_computation.6 | async-start | bytes 131072 | tf_op jit(solution)/shard_map/all_to_all | solution.py:33
  182.4 10.8 %all-to-all-done.6 = bf16[4,64,128]{2,1,0:T(8,128)(2,1)S(1)} async-done(((bf16[4,64,128]{2,1,0:T(8,128)(2,1)}), bf16[4,64,128]{2,1,0:T(8,128)(2,1)S(1)}, u32[]{:S(2)}, u32[]{:S(2)}) %all-to-all-start.6) | async-done | bytes 65568 | tf_op jit(solution)/shard_map/all_to_all | solution.py:33
  193.9 5.6 %shard_map.180 = bf16[32,160,128]{2,1,0:T(8,128)(2,1)} custom-call(s32[3]{0:T(128)} %pad_add_fusion.flag_ref, f32[2,432,128]{2,1,0:T(8,128)} %get-tuple-element.44.base_ref, bf16[64,128]{1,0:T(8,128)(2,1)} %reduce_sum.79.reduced_ref, bf16[2,32,432]{2,1,0:T(8,128)(2,1)} %get-tuple-element.46.lift_ref, bf16[2,320,432]{2,1,0:T(8,128)(2,1)} %copy-done.1, ...), custom_call_target="tpu_custom_call" | custom-call | tf_op jit(solution)/shard_map/pallas_call | solution.py:244
  199.5 5.7 %all-to-all-start.7 = ((bf16[8,4,160,128]{3,2,1,0:T(8,128)(2,1)}), bf16[8,4,160,128]{3,2,1,0:T(8,128)(2,1)S(1)}, u32[]{:S(2)}, u32[]{:S(2)}) async-start(bf16[8,4,160,128]{3,2,1,0:T(8,128)(2,1)} %bitcast.91), calls=%async_computation.7 | async-start | bytes 2621440 | tf_op jit(solution)/shard_map/all_to_all | solution.py:33
  207.4 26.6 %collective-permute-done.18 = bf16[4,4,160,128]{3,2,1,0:T(8,128)(2,1)} collective-permute-done((bf16[4,4,160,128]{3,2,1,0:T(8,128)(2,1)S(1)}, bf16[4,4,160,128]{3,2,1,0:T(8,128)(2,1)}, u32[]{:S(2)}, u32[]{:S(2)}) %collective-permute-start.18) | collective-permute-done | bytes 655392 | tf_op jit(solution)/shard_map/ppermute | solution.py:37
  235.4 3.2 %collective-permute-start.19 = (bf16[4,160,128]{2,1,0:T(8,128)(2,1)S(1)}, bf16[4,160,128]{2,1,0:T(8,128)(2,1)S(1)}, u32[]{:S(2)}, u32[]{:S(2)}) collective-permute-start(bf16[4,160,128]{2,1,0:T(8,128)(2,1)S(1)} %get-tuple-element.50), channel_id=1, source_target_pairs={{0,2},{2,4},{4,6},{6,0},{1,3},{3,5},{5,7},{7,1},{8,10},{10,12},{12... | collective-permute-start | bytes 491528 | tf_op jit(solution)/shard_map/ppermute | solution.py:51
  238.6 3.3 %collective-permute-start.20 = (bf16[4,160,128]{2,1,0:T(8,128)(2,1)S(1)}, bf16[4,160,128]{2,1,0:T(8,128)(2,1)S(1)}, u32[]{:S(2)}, u32[]{:S(2)}) collective-permute-start(bf16[4,160,128]{2,1,0:T(8,128)(2,1)S(1)} %get-tuple-element.52), channel_id=1, source_target_pairs={{0,4},{2,6},{4,0},{6,2},{1,5},{3,7},{5,1},{7,3},{8,12},{10,14},{12... | collective-permute-start | bytes 491528 | tf_op jit(solution)/shard_map/ppermute | solution.py:51
  241.9 3.4 %collective-permute-start.21 = (bf16[4,160,128]{2,1,0:T(8,128)(2,1)S(1)}, bf16[4,160,128]{2,1,0:T(8,128)(2,1)S(1)}, u32[]{:S(2)}, u32[]{:S(2)}) collective-permute-start(bf16[4,160,128]{2,1,0:T(8,128)(2,1)S(1)} %get-tuple-element.51), channel_id=1, source_target_pairs={{0,6},{2,0},{4,2},{6,4},{1,7},{3,1},{5,3},{7,5},{8,14},{10,8},{12,... | collective-permute-start | bytes 491528 | tf_op jit(solution)/shard_map/ppermute | solution.py:51
  245.3 7.1 %collective-permute-done.20 = bf16[4,160,128]{2,1,0:T(8,128)(2,1)S(1)} collective-permute-done((bf16[4,160,128]{2,1,0:T(8,128)(2,1)S(1)}, bf16[4,160,128]{2,1,0:T(8,128)(2,1)S(1)}, u32[]{:S(2)}, u32[]{:S(2)}) %collective-permute-start.20) | collective-permute-done | bytes 163872 | tf_op jit(solution)/shard_map/ppermute | solution.py:51
  256.3 3.5 %all-to-all-start.8 = ((bf16[4,2,160,128]{3,2,1,0:T(8,128)(2,1)}), bf16[4,2,160,128]{3,2,1,0:T(8,128)(2,1)S(1)}, u32[]{:S(2)}, u32[]{:S(2)}) async-start(bf16[4,2,160,128]{3,2,1,0:T(8,128)(2,1)} %pad_maximum_fusion.1), calls=%async_computation.8 | async-start | bytes 655360 | tf_op jit(solution)/shard_map/all_to_all | solution.py:33
  260.4 22.0 %all-to-all-done.8 = bf16[4,2,160,128]{3,2,1,0:T(8,128)(2,1)S(1)} async-done(((bf16[4,2,160,128]{3,2,1,0:T(8,128)(2,1)}), bf16[4,2,160,128]{3,2,1,0:T(8,128)(2,1)S(1)}, u32[]{:S(2)}, u32[]{:S(2)}) %all-to-all-start.8) | async-done | bytes 327712 | tf_op jit(solution)/shard_map/all_to_all | solution.py:33
  (109 shorter events, 60.0 us)
Async XLA Ops:
  5.7 53.0 %all-to-all-start = ((bf16[4,2,2,128,640]{4,3,2,1,0:T(8,128)(2,1)}), bf16[4,2,2,128,640]{4,3,2,1,0:T(8,128)(2,1)S(1)}, u32[]{:S(2)}, u32[]{:S(2)}) async-start(bf16[4,2,2,128,640]{4,3,2,1,0:T(8,128)(2,1)} %rows_by_x.1), calls=%async_computation | async-start | bytes 5242880 | tf_op jit(solution)/shard_map/all_to_all | solution.py:33
  11.0 5.0 %collective-permute-start = (f32[64,128]{1,0:T(8,128)S(1)}, f32[64,128]{1,0:T(8,128)S(1)}, u32[]{:S(2)}, u32[]{:S(2)}) collective-permute-start(f32[64,128]{1,0:T(8,128)S(1)} %convolution_bitcast_fusion), channel_id=1, source_target_pairs={{0,1},{1,0},{2,3},{3,2},{4,5},{5,4},{6,7},{7,6},{8,9},{9,8},{10,11... | collective-permute-start | bytes 98312 | tf_op jit(solution)/shard_map/ppermute | solution.py:56
  15.9 25.1 %collective-permute-start.1 = (bf16[2,320,432]{2,1,0:T(8,128)(2,1)}, bf16[2,320,432]{2,1,0:T(8,128)(2,1)}, u32[]{:S(2)}, u32[]{:S(2)}) collective-permute-start(bf16[2,320,432]{2,1,0:T(8,128)(2,1)} %refs_0_), channel_id=1, source_target_pairs={{0,256},{256,0},{1,257},{257,1},{2,258},{258,2},{3,259},{259,3},{4... | collective-permute-start | bytes 1658888 | tf_op jit(solution)/shard_map/ppermute | solution.py:37
  18.8 22.2 %collective-permute-start.2 = (bf16[320,432]{1,0:T(8,128)(2,1)S(1)}, bf16[320,432]{1,0:T(8,128)(2,1)S(1)}, u32[]{:S(2)}, u32[]{:S(2)}) collective-permute-start(bf16[320,432]{1,0:T(8,128)(2,1)S(1)} %bitcast.98), channel_id=1, source_target_pairs={{0,256},{256,0},{1,257},{257,1},{2,258},{258,2},{3,259},{259,3},{4... | collective-permute-start | bytes 829448 | tf_op jit(solution)/shard_map/ppermute | solution.py:37
  22.7 5.1 %collective-permute-start.3 = (f32[64,128]{1,0:T(8,128)S(1)}, f32[64,128]{1,0:T(8,128)S(1)}, u32[]{:S(2)}, u32[]{:S(2)}) collective-permute-start(f32[64,128]{1,0:T(8,128)S(1)} %add.99), channel_id=1, source_target_pairs={{0,2},{2,0},{4,6},{6,4},{1,3},{3,1},{5,7},{7,5},{8,10},{10,8},{12,... | collective-permute-start | bytes 98312 | tf_op jit(solution)/shard_map/ppermute | solution.py:56
  27.8 10.2 %collective-permute-start.4 = (f32[64,128]{1,0:T(8,128)S(1)}, f32[64,128]{1,0:T(8,128)S(1)}, u32[]{:S(2)}, u32[]{:S(2)}) collective-permute-start(f32[64,128]{1,0:T(8,128)S(1)} %add.100), channel_id=1, source_target_pairs={{0,4},{2,6},{4,0},{6,2},{1,5},{3,7},{5,1},{7,3},{8,12},{10,14},{12... | collective-permute-start | bytes 98312 | tf_op jit(solution)/shard_map/ppermute | solution.py:56
  32.7 26.1 %collective-permute-start.6 = (bf16[2,320,432]{2,1,0:T(8,128)(2,1)}, bf16[2,320,432]{2,1,0:T(8,128)(2,1)}, u32[]{:S(2)}, u32[]{:S(2)}) collective-permute-start(bf16[2,320,432]{2,1,0:T(8,128)(2,1)} %refs_0_), channel_id=1, source_target_pairs={{0,32},{32,0},{1,33},{33,1},{2,34},{34,2},{3,35},{35,3},{4,36},{36... | collective-permute-start | bytes 1658888 | tf_op jit(solution)/shard_map/ppermute | solution.py:37
  42.1 16.7 %collective-permute-start.8 = (bf16[2,320,432]{2,1,0:T(8,128)(2,1)S(1)}, bf16[2,320,432]{2,1,0:T(8,128)(2,1)}, u32[]{:S(2)}, u32[]{:S(2)}) collective-permute-start(bf16[2,320,432]{2,1,0:T(8,128)(2,1)S(1)} %pad_maximum_fusion.refs_4_.refs_0_), channel_id=1, source_target_pairs={{0,32},{32,0},{1,33},{33,1},{2,34},{34,2},{3,35},{35,3},{4,36},{36... | collective-permute-start | bytes 1658888 | tf_op jit(solution)/shard_map/ppermute | solution.py:37
  46.7 12.1 %collective-permute-start.7 = (bf16[2,320,432]{2,1,0:T(8,128)(2,1)}, bf16[2,320,432]{2,1,0:T(8,128)(2,1)}, u32[]{:S(2)}, u32[]{:S(2)}) collective-permute-start(bf16[2,320,432]{2,1,0:T(8,128)(2,1)} %collective-permute-done.1.refs_1_), channel_id=1, source_target_pairs={{0,32},{32,0},{1,33},{33,1},{2,34},{34,2},{3,35},{35,3},{4,36},{36... | collective-permute-start | bytes 1658888 | tf_op jit(solution)/shard_map/ppermute | solution.py:37
  48.6 10.1 %collective-permute-start.5 = (f32[64,128]{1,0:T(8,128)S(1)}, f32[64,128]{1,0:T(8,128)S(1)}, u32[]{:S(2)}, u32[]{:S(2)}) collective-permute-start(f32[64,128]{1,0:T(8,128)S(1)} %add.101), channel_id=1, source_target_pairs={{0,8},{8,0},{16,24},{24,16},{1,9},{9,1},{17,25},{25,17},{2,10},{10... | collective-permute-start | bytes 98312 | tf_op jit(solution)/shard_map/ppermute | solution.py:56
  67.1 20.9 %all-to-all-start.1 = ((bf16[4,3,432,128]{3,2,1,0:T(8,128)(2,1)}), bf16[4,3,432,128]{3,2,1,0:T(8,128)(2,1)S(1)}, u32[]{:S(2)}, u32[]{:S(2)}) async-start(bf16[4,3,432,128]{3,2,1,0:T(8,128)(2,1)} %partials.1), calls=%async_computation.1 | async-start | bytes 2654208 | tf_op jit(solution)/shard_map/all_to_all | solution.py:33
  71.5 18.7 %collective-permute-start.9 = (f32[64,128]{1,0:T(8,128)S(1)}, f32[64,128]{1,0:T(8,128)S(1)}, u32[]{:S(2)}, u32[]{:S(2)}) collective-permute-start(f32[64,128]{1,0:T(8,128)S(1)} %add.102), channel_id=1, source_target_pairs={{0,16},{8,24},{16,0},{24,8},{1,17},{9,25},{17,1},{25,9},{2,18},{10... | collective-permute-start | bytes 98312 | tf_op jit(solution)/shard_map/ppermute | solution.py:56
  88.0 28.8 %collective-permute-start.12 = (bf16[2,320,432]{2,1,0:T(8,128)(2,1)S(1)}, bf16[2,320,432]{2,1,0:T(8,128)(2,1)S(1)}, u32[]{:S(2)}, u32[]{:S(2)}) collective-permute-start(bf16[2,320,432]{2,1,0:T(8,128)(2,1)S(1)} %copy-done.2), channel_id=1, source_target_pairs={{0,64},{64,128},{128,192},{192,0},{1,65},{65,129},{129,193},{193,1... | collective-permute-start | bytes 1658888 | tf_op jit(solution)/shard_map/ppermute | solution.py:51
  94.8 12.2 %all-to-all-start.2 = ((bf16[8,64,128]{2,1,0:T(8,128)(2,1)}), bf16[8,64,128]{2,1,0:T(8,128)(2,1)S(1)}, u32[]{:S(2)}, u32[]{:S(2)}) async-start(bf16[8,64,128]{2,1,0:T(8,128)(2,1)} %broadcast_in_dim.57), calls=%async_computation.2 | async-start | bytes 262144 | tf_op jit(solution)/shard_map/all_to_all | solution.py:33
  102.4 37.2 %collective-permute-start.14 = (bf16[2,320,432]{2,1,0:T(8,128)(2,1)S(1)}, bf16[2,320,432]{2,1,0:T(8,128)(2,1)S(1)}, u32[]{:S(2)}, u32[]{:S(2)}) collective-permute-start(bf16[2,320,432]{2,1,0:T(8,128)(2,1)S(1)} %copy-done.2), channel_id=1, source_target_pairs={{0,192},{64,0},{128,64},{192,128},{1,193},{65,1},{129,65},{193,129... | collective-permute-start | bytes 1658888 | tf_op jit(solution)/shard_map/ppermute | solution.py:51
  107.7 21.0 %all-to-all-start.3 = ((bf16[4,64,128]{2,1,0:T(8,128)(2,1)}), bf16[4,64,128]{2,1,0:T(8,128)(2,1)S(1)}, u32[]{:S(2)}, u32[]{:S(2)}) async-start(bf16[4,64,128]{2,1,0:T(8,128)(2,1)} %broadcast_in_dim.58), calls=%async_computation.3 | async-start | bytes 131072 | tf_op jit(solution)/shard_map/all_to_all | solution.py:33
  116.8 29.1 %copy-start.5 = (bf16[2,320,432]{2,1,0:T(8,128)(2,1)}, bf16[2,320,432]{2,1,0:T(8,128)(2,1)S(1)}, u32[]{:S(2)}) copy-start(bf16[2,320,432]{2,1,0:T(8,128)(2,1)S(1)} %collective-permute-done.12.refs_1_) | copy-start | bytes 1658884
  116.8 24.9 %collective-permute-start.13 = (bf16[2,320,432]{2,1,0:T(8,128)(2,1)S(1)}, bf16[2,320,432]{2,1,0:T(8,128)(2,1)S(1)}, u32[]{:S(2)}, u32[]{:S(2)}) collective-permute-start(bf16[2,320,432]{2,1,0:T(8,128)(2,1)S(1)} %collective-permute-done.12.refs_1_), channel_id=1, source_target_pairs={{0,64},{64,128},{128,192},{192,0},{1,65},{65,129},{129,193},{193,1... | collective-permute-start | bytes 1658888 | tf_op jit(solution)/shard_map/ppermute | solution.py:51
  118.7 12.4 %collective-permute-start.10 = (bf16[64,432]{1,0:T(8,128)(2,1)}, bf16[64,432]{1,0:T(8,128)(2,1)S(1)}, u32[]{:S(2)}, u32[]{:S(2)}) collective-permute-start(bf16[64,432]{1,0:T(8,128)(2,1)} %get-tuple-element.35), channel_id=1, source_target_pairs={{0,256},{1,257},{2,258},{3,259},{4,260},{5,261},{6,262},{7,263},{8... | collective-permute-start | bytes 165896 | tf_op jit(solution)/shard_map/ppermute | solution.py:312
  129.8 11.8 %collective-permute-start.11 = (bf16[64,160]{1,0:T(8,128)(2,1)S(1)}, bf16[64,160]{1,0:T(8,128)(2,1)S(1)}, u32[]{:S(2)}, u32[]{:S(2)}) collective-permute-start(bf16[64,160]{1,0:T(8,128)(2,1)S(1)} %fusion.1), channel_id=1, source_target_pairs={{0,256},{1,257},{2,258},{3,259},{4,260},{5,261},{6,262},{7,263},{8... | collective-permute-start | bytes 61448 | tf_op jit(solution)/shard_map/ppermute | solution.py:312
  131.9 18.3 %collective-permute-start.15 = (bf16[2,320,432]{2,1,0:T(8,128)(2,1)S(1)}, bf16[2,320,432]{2,1,0:T(8,128)(2,1)S(1)}, u32[]{:S(2)}, u32[]{:S(2)}) collective-permute-start(bf16[2,320,432]{2,1,0:T(8,128)(2,1)S(1)} %collective-permute-done.12.refs_1_), channel_id=1, source_target_pairs={{0,32},{32,0},{1,33},{33,1},{2,34},{34,2},{3,35},{35,3},{4,36},{36... | collective-permute-start | bytes 1658888 | tf_op jit(solution)/shard_map/ppermute | solution.py:37
  139.6 10.6 %collective-permute-start.17 = (bf16[2,320,432]{2,1,0:T(8,128)(2,1)S(1)}, bf16[2,320,432]{2,1,0:T(8,128)(2,1)S(1)}, u32[]{:S(2)}, u32[]{:S(2)}) collective-permute-start(bf16[2,320,432]{2,1,0:T(8,128)(2,1)S(1)} %collective-permute-done.14.refs_3_), channel_id=1, source_target_pairs={{0,32},{32,0},{1,33},{33,1},{2,34},{34,2},{3,35},{35,3},{4,36},{36... | collective-permute-start | bytes 1658888 | tf_op jit(solution)/shard_map/ppermute | solution.py:37
  141.7 8.6 %collective-permute-start.16 = (bf16[2,320,432]{2,1,0:T(8,128)(2,1)S(1)}, bf16[2,320,432]{2,1,0:T(8,128)(2,1)}, u32[]{:S(2)}, u32[]{:S(2)}) collective-permute-start(bf16[2,320,432]{2,1,0:T(8,128)(2,1)S(1)} %collective-permute-done.13.refs_2_), channel_id=1, source_target_pairs={{0,32},{32,0},{1,33},{33,1},{2,34},{34,2},{3,35},{35,3},{4,36},{36... | collective-permute-start | bytes 1658888 | tf_op jit(solution)/shard_map/ppermute | solution.py:37
  145.8 15.3 %all-to-all-start.4 = ((bf16[8,64,592]{2,1,0:T(8,128)(2,1)}), bf16[8,64,592]{2,1,0:T(8,128)(2,1)}, u32[]{:S(2)}, u32[]{:S(2)}) async-start(bf16[8,64,592]{2,1,0:T(8,128)(2,1)} %broadcast_in_dim.59), calls=%async_computation.4 | async-start | bytes 1310720 | tf_op jit(solution)/shard_map/all_to_all | solution.py:33
  164.9 9.3 %all-to-all-start.5 = ((bf16[8,64,128]{2,1,0:T(8,128)(2,1)}), bf16[8,64,128]{2,1,0:T(8,128)(2,1)S(1)}, u32[]{:S(2)}, u32[]{:S(2)}) async-start(bf16[8,64,128]{2,1,0:T(8,128)(2,1)} %broadcast_in_dim.60), calls=%async_computation.5 | async-start | bytes 262144 | tf_op jit(solution)/shard_map/all_to_all | solution.py:33
  174.9 18.4 %all-to-all-start.6 = ((bf16[4,64,128]{2,1,0:T(8,128)(2,1)}), bf16[4,64,128]{2,1,0:T(8,128)(2,1)S(1)}, u32[]{:S(2)}, u32[]{:S(2)}) async-start(bf16[4,64,128]{2,1,0:T(8,128)(2,1)} %broadcast_in_dim.61), calls=%async_computation.6 | async-start | bytes 131072 | tf_op jit(solution)/shard_map/all_to_all | solution.py:33
  199.5 55.8 %all-to-all-start.7 = ((bf16[8,4,160,128]{3,2,1,0:T(8,128)(2,1)}), bf16[8,4,160,128]{3,2,1,0:T(8,128)(2,1)S(1)}, u32[]{:S(2)}, u32[]{:S(2)}) async-start(bf16[8,4,160,128]{3,2,1,0:T(8,128)(2,1)} %bitcast.91), calls=%async_computation.7 | async-start | bytes 2621440 | tf_op jit(solution)/shard_map/all_to_all | solution.py:33
  205.2 28.9 %collective-permute-start.18 = (bf16[4,4,160,128]{3,2,1,0:T(8,128)(2,1)S(1)}, bf16[4,4,160,128]{3,2,1,0:T(8,128)(2,1)}, u32[]{:S(2)}, u32[]{:S(2)}) collective-permute-start(bf16[4,4,160,128]{3,2,1,0:T(8,128)(2,1)S(1)} %dynamic-slice_bitcast_fusion), channel_id=1, source_target_pairs={{0,1},{1,0},{2,3},{3,2},{4,5},{5,4},{6,7},{7,6},{8,9},{9,8},{10,11... | collective-permute-start | bytes 1966088 | tf_op jit(solution)/shard_map/ppermute | solution.py:37
  235.4 9.9 %collective-permute-start.19 = (bf16[4,160,128]{2,1,0:T(8,128)(2,1)S(1)}, bf16[4,160,128]{2,1,0:T(8,128)(2,1)S(1)}, u32[]{:S(2)}, u32[]{:S(2)}) collective-permute-start(bf16[4,160,128]{2,1,0:T(8,128)(2,1)S(1)} %get-tuple-element.50), channel_id=1, source_target_pairs={{0,2},{2,4},{4,6},{6,0},{1,3},{3,5},{5,7},{7,1},{8,10},{10,12},{12... | collective-permute-start | bytes 491528 | tf_op jit(solution)/shard_map/ppermute | solution.py:51
  238.6 13.7 %collective-permute-start.20 = (bf16[4,160,128]{2,1,0:T(8,128)(2,1)S(1)}, bf16[4,160,128]{2,1,0:T(8,128)(2,1)S(1)}, u32[]{:S(2)}, u32[]{:S(2)}) collective-permute-start(bf16[4,160,128]{2,1,0:T(8,128)(2,1)S(1)} %get-tuple-element.52), channel_id=1, source_target_pairs={{0,4},{2,6},{4,0},{6,2},{1,5},{3,7},{5,1},{7,3},{8,12},{10,14},{12... | collective-permute-start | bytes 491528 | tf_op jit(solution)/shard_map/ppermute | solution.py:51
  241.9 13.3 %collective-permute-start.21 = (bf16[4,160,128]{2,1,0:T(8,128)(2,1)S(1)}, bf16[4,160,128]{2,1,0:T(8,128)(2,1)S(1)}, u32[]{:S(2)}, u32[]{:S(2)}) collective-permute-start(bf16[4,160,128]{2,1,0:T(8,128)(2,1)S(1)} %get-tuple-element.51), channel_id=1, source_target_pairs={{0,6},{2,0},{4,2},{6,4},{1,7},{3,1},{5,3},{7,5},{8,14},{10,8},{12,... | collective-permute-start | bytes 491528 | tf_op jit(solution)/shard_map/ppermute | solution.py:51
  256.3 26.1 %all-to-all-start.8 = ((bf16[4,2,160,128]{3,2,1,0:T(8,128)(2,1)}), bf16[4,2,160,128]{3,2,1,0:T(8,128)(2,1)S(1)}, u32[]{:S(2)}, u32[]{:S(2)}) async-start(bf16[4,2,160,128]{3,2,1,0:T(8,128)(2,1)} %pad_maximum_fusion.1), calls=%async_computation.8 | async-start | bytes 655360 | tf_op jit(solution)/shard_map/all_to_all | solution.py:33
  (16 other events, 175.8 us)

commit v4 on v3

--- a/solution.py
+++ b/solution.py
@@ -105,21 +105,22 @@
 
 
 def partial_kernel(flag_ref, rows_ref, *refs):
-    weight_refs, down_refs = refs[:4], refs[4:6]
-    out_ref, weight, down, held, in_sems, out_sems = refs[6:]
+    block_refs = refs[:4]
+    out_ref, weight, held, in_sems, out_sems = refs[4:]
     role, core = flag_ref[0], flag_ref[1]
-    depth = weight_refs[0].shape[1]
-    weight_loads, down_loads = [], []
+    depth = block_refs[0].shape[1]
+    loads = []
     for i in range(2):
         side = core if i == 0 else 1 - core
         place = pl.ds(pl.multiple_of(side * depth, depth), depth)
         for j in range(2):
             half = role if j == 0 else 1 - role
             n = 2 * i + j
-            down_loads.append(pltpu.make_async_copy(down_refs[i].at[j], down.at[half, place, :], in_sems.at[n]))
-            weight_loads.append(pltpu.make_async_copy(weight_refs[n], weight.at[half, :, place, :], in_sems.at[4 + n]))
-    for copy in down_loads + weight_loads:
+            loads.append(pltpu.make_async_copy(block_refs[n], weight.at[half, :, place, :], in_sems.at[n]))
+    for copy in loads:
         copy.start()
+    for copy in loads:
+        copy.wait()
 
     count, group = rows_ref.shape[0], rows_ref.shape[3]
 
@@ -127,15 +128,10 @@
         return jnp.concatenate([rows_ref[x, which, half] for x in range(count)], axis=0)
 
     stores = []
-    for k in (2, 0, 1):
-        for copy in {2: down_loads, 0: weight_loads, 1: []}[k]:
-            copy.wait()
+    for k in range(3):
         total = 0.0
         for half in range(2):
-            if k < 2:
-                total += dot(all_rows(0, half), weight[half, k], ((1,), (0,)))
-            else:
-                total += dot(all_rows(1, half), down[half], ((1,), (0,)))
+            total += dot(all_rows(k // 2, half), weight[half, k], ((1,), (0,)))
         turned = total.astype(BF).T
         for x in range(count):
             held[k, x] = turned[:, x * group : (x + 1) * group]
@@ -146,23 +142,22 @@
         copy.wait()
 
 
-def partials(flags, rows, weights, downs):
+def partials(flags, rows, blocks):
     count, _, _, group, _ = rows.shape
-    _, depth, cols = weights[0].shape
+    kinds, depth, cols = blocks[0].shape
     return pl.pallas_call(
         partial_kernel,
-        out_shape=jax.ShapeDtypeStruct((count, 3, cols, group), BF),
-        in_specs=[SMEM, VMEM] + [ANY] * 6,
+        out_shape=jax.ShapeDtypeStruct((count, kinds, cols, group), BF),
+        in_specs=[SMEM, VMEM] + [ANY] * 4,
         out_specs=ANY,
         scratch_shapes=[
-            pltpu.VMEM((2, 2, 2 * depth, cols), BF),
-            pltpu.VMEM((2, 2 * depth, cols), BF),
-            pltpu.VMEM((3, count, cols, group), BF),
-            pltpu.SemaphoreType.DMA((8,)),
-            pltpu.SemaphoreType.DMA((3,)),
+            pltpu.VMEM((2, kinds, 2 * depth, cols), BF),
+            pltpu.VMEM((kinds, count, cols, group), BF),
+            pltpu.SemaphoreType.DMA((4,)),
+            pltpu.SemaphoreType.DMA((kinds,)),
         ],
         name="partials",
-    )(flags, rows, *weights, *downs)
+    )(flags, rows, *blocks)
 
 
 def middle_kernel(flag_ref, pieces_ref, reduced_ref, lift_ref, base_ref, hidden_ref, through_ref, grad_ref):
@@ -285,22 +280,22 @@
     row_weight = KEEP_RATE ** staleness.astype(F32)
     rows = rows_by_x(token_batch, cotangent, row_weight[:, None])
     rows = exchange(rows, "x")
-    own_weight, own_down, reduced = lax.optimization_barrier((frozen_gate_up_weight, down_weight.T, reduced))
-
-    other_half = swapped(own_weight, "role")
-    other_down = swapped(own_down, "role")
+    own, reduced = lax.optimization_barrier(
+        (jnp.concatenate([frozen_gate_up_weight, down_weight.T[None]]), reduced)
+    )
+
+    other = swapped(own, "role")
     reduced = plus_partner(plus_partner(reduced, "zl", 1), "zl", 2)
-    other_half, other_down, reduced = lax.optimization_barrier((other_half, other_down, reduced))
-    weights = (own_weight, other_half, swapped(own_weight, "core"), swapped(other_half, "core"))
-    down_pair = jnp.stack([own_down, other_down])
-    downs = (down_pair, swapped(down_pair, "core"))
+    other, reduced = lax.optimization_barrier((other, reduced))
+    near_blocks = (own, other, swapped(own, "core"), swapped(other, "core"))
     reduced = plus_partner(reduced, "zh", 1)
     rows, reduced = lax.optimization_barrier((rows, reduced))
-    pieces = exchange(partials(flags, rows, weights, downs), "x")
+    pieces = exchange(partials(flags, rows, near_blocks), "x")
     reduced = plus_partner(reduced, "zh", 2).astype(BF)
     base, hidden_old, through_part, out_part = middle(flags, pieces, reduced, out_bf)
 
-    down_first, _ = lax.optimization_barrier((down_pair, pieces))
+    later_blocks, _ = lax.optimization_barrier((near_blocks, pieces))
+    down_first, down_core = (jnp.stack([a[2], b[2]]) for a, b in (later_blocks[:2], later_blocks[2:]))
     through = sum_first(spread(through_part, NEAR)).astype(BF)
     through = spread(through, "zh")
     through = sum_first(through).astype(BF)
@@ -319,7 +314,7 @@
     packed, same_core = lax.optimization_barrier((packed, same_core))
     grads = spread(packed, DP)
     other_across = swapped(same_core[1], "core")
-    blocks = [down_pair, *same_core, downs[1], other_behind, other_across, other_ahead]
+    blocks = [down_first, *same_core, down_core, other_behind, other_across, other_ahead]
     old_parts = layer_call(old_kernel, group_rows, slice_width, blocks, flags, hidden_old)
     grads, old_parts = lax.optimization_barrier((grads, old_parts))
     grads = sum_first(grads)
@@ -344,7 +339,9 @@
     renewed = spread(renewed, NEAR)
     renewed = sum_first(spread(sum_first(renewed).astype(BF), "zh")).astype(BF)
     near_old = shifted_sum(pair, "zl")
-    new_parts = layer_call(new_kernel, group_rows, slice_width, blocks, flags, base, renewed, new_out.astype(BF))
+    new_parts = layer_call(
+        new_kernel, group_rows, slice_width, blocks, flags, base, renewed, new_out.astype(BF)
+    )
     near_new = sum_first(exchange(new_parts.reshape(8, 4, slice_width, group_rows), NEAR))
     near = jnp.stack([near_old, near_new], axis=1).astype(BF)
     layers = sum_first(exchange(near, "zh"))

time: 285 us -> 285 us (level)
  starting transfers between devices: 135 us -> 128 us
  local copies, waits for them, and re-layouts: 7.76 us -> 12 us
    ppermute x9 -> x7, starting transfers between devices: 33.5 us -> 26.6 us  [swapped(): return lax.ppermute(value, axis, [(0, 1), (1, 0)])]
    ppermute x9 -> x7, waiting for transfers between devices: 29.7 us -> 34 us  [swapped(): return lax.ppermute(value, axis, [(0, 1), (1, 0)])]
    slice x0 -> x4, local copies, waits for them, and re-layouts: none -> 4.19 us  [the longest x2 2.2 us: step(): a[2]]
  transfers between devices with their start and end apart: 31 -> 29, of which waited for: 14 -> 14; matrix products, arithmetic and copies ran while one was open for 4% -> 6% of each run, Pallas kernels for 3% -> 3%
where the time goes in v4:
time: 285 us; the launch traced here: 283 us
  starting transfers between devices  128 us (45%)
  waiting for transfers between devices  101 us (35%)
  Pallas kernels  24.4 us (9%)
  other arithmetic  13 us (5%)
  local copies, waits for them, and re-layouts  12 us (4%)
  matrix products  3.32 us (1%)
    all_to_all x9, waiting for transfers between devices, exchange(): return lax.all_to_all(pieces, axis, split_axis=0, concat_axis=0, tiled=True)  52.1 us
    all_to_all x9, starting transfers between devices, exchange(): return lax.all_to_all(pieces, axis, split_axis=0, concat_axis=0, tiled=True)  49.8 us
    ppermute x7, waiting for transfers between devices, swapped(): return lax.ppermute(value, axis, [(0, 1), (1, 0)])  34 us
    ppermute x5, starting transfers between devices, plus_partner(): lax.ppermute(value, axis, [(i, i ^ step) for i in range(count)])  30.6 us
    ppermute x7, starting transfers between devices, swapped(): return lax.ppermute(value, axis, [(0, 1), (1, 0)])  26.6 us
    ppermute x6, starting transfers between devices, shifted(): lax.ppermute(value, axis, [(i, (i + step) % count) for i in range(count)])  18.2 us
    pallas_call x2, Pallas kernels, layer_call(): pl.pallas_call(kernel, out_shape=jax.ShapeDtypeStruct((32, width, group),...  10.7 us
    ppermute x6, waiting for transfers between devices, shifted(): lax.ppermute(value, axis, [(i, (i + step) % count) for i in range(count)])  9.92 us
  transfers between devices with their start and end apart: 29, of which 14 were waited for; matrix products, arithmetic and copies ran while one was open for 6% of the time, Pallas kernels for 3%

profile of v4, /device:TPU:57, one launch (start us, length us, event | category | flops | bytes accessed | tf_op | source)
XLA Modules:
  0.0 282.9 jit_solution(4607369062242227986)
XLA Ops:
  2.0 3.7 %rows_by_x.1 = bf16[4,2,2,128,640]{4,3,2,1,0:T(8,128)(2,1)} custom-call(bf16[128,5120]{1,0:T(8,128)(2,1)} %bitcast.94, bf16[128,5120]{1,0:T(8,128)(2,1)} %cotangent_ref.1, f32[128,1]{1,0:T(8,128)} %copy.25.scale_ref), custom_call_target="tpu_custom_call" | custom-call | tf_op jit(solution)/shard_map/rows_by_x/pallas_call | solution.py:98
  5.7 4.1 %all-to-all-start = ((bf16[4,2,2,128,640]{4,3,2,1,0:T(8,128)(2,1)}), bf16[4,2,2,128,640]{4,3,2,1,0:T(8,128)(2,1)S(1)}, u32[]{:S(2)}, u32[]{:S(2)}) async-start(bf16[4,2,2,128,640]{4,3,2,1,0:T(8,128)(2,1)} %rows_by_x.1), calls=%async_computation | async-start | bytes 5242880 | tf_op jit(solution)/shard_map/all_to_all | solution.py:33
  23.8 4.9 %collective-permute-start.3 = (f32[64,128]{1,0:T(8,128)S(1)}, f32[64,128]{1,0:T(8,128)S(1)}, u32[]{:S(2)}, u32[]{:S(2)}) collective-permute-start(f32[64,128]{1,0:T(8,128)S(1)} %add.100), channel_id=1, source_target_pairs={{0,4},{2,6},{4,0},{6,2},{1,5},{3,7},{5,1},{7,3},{8,12},{10,14},{12... | collective-permute-start | bytes 98312 | tf_op jit(solution)/shard_map/ppermute | solution.py:56
  28.7 5.1 %collective-permute-start.5 = (bf16[3,320,432]{2,1,0:T(8,128)(2,1)}, bf16[3,320,432]{2,1,0:T(8,128)(2,1)}, u32[]{:S(2)}, u32[]{:S(2)}) collective-permute-start(bf16[3,320,432]{2,1,0:T(8,128)(2,1)} %pad_maximum_fusion.refs_0_), channel_id=1, source_target_pairs={{0,32},{32,0},{1,33},{33,1},{2,34},{34,2},{3,35},{35,3},{4,36},{36... | collective-permute-start | bytes 2488328 | tf_op jit(solution)/shard_map/ppermute | solution.py:37
  33.8 7.3 %collective-permute-done.1.refs_1_ = bf16[3,320,432]{2,1,0:T(8,128)(2,1)} collective-permute-done((bf16[3,320,432]{2,1,0:T(8,128)(2,1)}, bf16[3,320,432]{2,1,0:T(8,128)(2,1)}, u32[]{:S(2)}, u32[]{:S(2)}) %collective-permute-start.1) | collective-permute-done | bytes 829472 | tf_op jit(solution)/shard_map/ppermute | solution.py:37
  41.2 4.6 %collective-permute-start.6 = (bf16[3,320,432]{2,1,0:T(8,128)(2,1)}, bf16[3,320,432]{2,1,0:T(8,128)(2,1)}, u32[]{:S(2)}, u32[]{:S(2)}) collective-permute-start(bf16[3,320,432]{2,1,0:T(8,128)(2,1)} %collective-permute-done.1.refs_1_), channel_id=1, source_target_pairs={{0,32},{32,0},{1,33},{33,1},{2,34},{34,2},{3,35},{35,3},{4,36},{36... | collective-permute-start | bytes 2488328 | tf_op jit(solution)/shard_map/ppermute | solution.py:37
  45.7 8.8 %collective-permute-start.4 = (f32[64,128]{1,0:T(8,128)S(1)}, f32[64,128]{1,0:T(8,128)S(1)}, u32[]{:S(2)}, u32[]{:S(2)}) collective-permute-start(f32[64,128]{1,0:T(8,128)S(1)} %add.101), channel_id=1, source_target_pairs={{0,8},{8,0},{16,24},{24,16},{1,9},{9,1},{17,25},{25,17},{2,10},{10... | collective-permute-start | bytes 98312 | tf_op jit(solution)/shard_map/ppermute | solution.py:56
  57.8 7.4 %partials.1 = bf16[4,3,432,128]{3,2,1,0:T(8,128)(2,1)} custom-call(s32[3]{0:T(128)} %pad_add_fusion.flag_ref, bf16[4,2,2,128,640]{4,3,2,1,0:T(8,128)(2,1)} %copy-done, bf16[3,320,432]{2,1,0:T(8,128)(2,1)} %pad_maximum_fusion.refs_0_, bf16[3,320,432]{2,1,0:T(8,128)(2,1)} %collective-permute-done.1.refs_1_, ...), custom_call_target="tpu_custom_call" | custom-call | tf_op jit(solution)/shard_map/partials/pallas_call | solution.py:148
  65.2 4.4 %all-to-all-start.1 = ((bf16[4,3,432,128]{3,2,1,0:T(8,128)(2,1)}), bf16[4,3,432,128]{3,2,1,0:T(8,128)(2,1)S(1)}, u32[]{:S(2)}, u32[]{:S(2)}) async-start(bf16[4,3,432,128]{3,2,1,0:T(8,128)(2,1)} %partials.1), calls=%async_computation.1 | async-start | bytes 2654208 | tf_op jit(solution)/shard_map/all_to_all | solution.py:33
  70.2 12.6 %collective-permute-start.7 = (f32[64,128]{1,0:T(8,128)S(1)}, f32[64,128]{1,0:T(8,128)S(1)}, u32[]{:S(2)}, u32[]{:S(2)}) collective-permute-start(f32[64,128]{1,0:T(8,128)S(1)} %add.102), channel_id=1, source_target_pairs={{0,16},{8,24},{16,0},{24,8},{1,17},{9,25},{17,1},{25,9},{2,18},{10... | collective-permute-start | bytes 98312 | tf_op jit(solution)/shard_map/ppermute | solution.py:56
  82.8 4.1 %all-to-all-done.1.pieces_ref = bf16[4,3,432,128]{3,2,1,0:T(8,128)(2,1)S(1)} async-done(((bf16[4,3,432,128]{3,2,1,0:T(8,128)(2,1)}), bf16[4,3,432,128]{3,2,1,0:T(8,128)(2,1)S(1)}, u32[]{:S(2)}, u32[]{:S(2)}) %all-to-all-start.1) | async-done | bytes 1327136 | tf_op jit(solution)/shard_map/all_to_all | solution.py:33
  96.1 6.4 %all-to-all-start.2 = ((bf16[8,64,128]{2,1,0:T(8,128)(2,1)}), bf16[8,64,128]{2,1,0:T(8,128)(2,1)S(1)}, u32[]{:S(2)}, u32[]{:S(2)}) async-start(bf16[8,64,128]{2,1,0:T(8,128)(2,1)} %broadcast_in_dim.61), calls=%async_computation.2 | async-start | bytes 262144 | tf_op jit(solution)/shard_map/all_to_all | solution.py:33
  102.5 4.3 %collective-permute-start.12 = (bf16[2,320,432]{2,1,0:T(8,128)(2,1)S(1)}, bf16[2,320,432]{2,1,0:T(8,128)(2,1)S(1)}, u32[]{:S(2)}, u32[]{:S(2)}) collective-permute-start(bf16[2,320,432]{2,1,0:T(8,128)(2,1)S(1)} %pad_maximum_fusion.1.refs_0_), channel_id=1, source_target_pairs={{0,192},{64,0},{128,64},{192,128},{1,193},{65,1},{129,65},{193,129... | collective-permute-start | bytes 1658888 | tf_op jit(solution)/shard_map/ppermute | solution.py:51
  107.7 9.5 %all-to-all-start.3 = ((bf16[4,64,128]{2,1,0:T(8,128)(2,1)}), bf16[4,64,128]{2,1,0:T(8,128)(2,1)S(1)}, u32[]{:S(2)}, u32[]{:S(2)}) async-start(bf16[4,64,128]{2,1,0:T(8,128)(2,1)} %broadcast_in_dim.62), calls=%async_computation.3 | async-start | bytes 131072 | tf_op jit(solution)/shard_map/all_to_all | solution.py:33
  120.5 8.7 %all-to-all-done.3 = bf16[4,64,128]{2,1,0:T(8,128)(2,1)S(1)} async-done(((bf16[4,64,128]{2,1,0:T(8,128)(2,1)}), bf16[4,64,128]{2,1,0:T(8,128)(2,1)S(1)}, u32[]{:S(2)}, u32[]{:S(2)}) %all-to-all-start.3) | async-done | bytes 65568 | tf_op jit(solution)/shard_map/all_to_all | solution.py:33
  132.5 6.8 %collective-permute-start.13 = (bf16[2,320,432]{2,1,0:T(8,128)(2,1)S(1)}, bf16[2,320,432]{2,1,0:T(8,128)(2,1)S(1)}, u32[]{:S(2)}, u32[]{:S(2)}) collective-permute-start(bf16[2,320,432]{2,1,0:T(8,128)(2,1)S(1)} %collective-permute-done.10.refs_1_), channel_id=1, source_target_pairs={{0,32},{32,0},{1,33},{33,1},{2,34},{34,2},{3,35},{35,3},{4,36},{36... | collective-permute-start | bytes 1658888 | tf_op jit(solution)/shard_map/ppermute | solution.py:37
  141.4 3.2 %collective-permute-start.14 = (bf16[2,320,432]{2,1,0:T(8,128)(2,1)S(1)}, bf16[2,320,432]{2,1,0:T(8,128)(2,1)}, u32[]{:S(2)}, u32[]{:S(2)}) collective-permute-start(bf16[2,320,432]{2,1,0:T(8,128)(2,1)S(1)} %collective-permute-done.11.refs_2_), channel_id=1, source_target_pairs={{0,32},{32,0},{1,33},{33,1},{2,34},{34,2},{3,35},{35,3},{4,36},{36... | collective-permute-start | bytes 1658888 | tf_op jit(solution)/shard_map/ppermute | solution.py:37
  145.5 4.7 %all-to-all-start.4 = ((bf16[8,64,592]{2,1,0:T(8,128)(2,1)}), bf16[8,64,592]{2,1,0:T(8,128)(2,1)}, u32[]{:S(2)}, u32[]{:S(2)}) async-start(bf16[8,64,592]{2,1,0:T(8,128)(2,1)} %broadcast_in_dim.63), calls=%async_computation.4 | async-start | bytes 1310720 | tf_op jit(solution)/shard_map/all_to_all | solution.py:33
  154.2 5.1 %shard_map.179 = bf16[32,160,128]{2,1,0:T(8,128)(2,1)} custom-call(s32[3]{0:T(128)} %pad_add_fusion.flag_ref, bf16[432,128]{1,0:T(8,128)(2,1)} %get-tuple-element.39.hidden_ref, bf16[2,320,432]{2,1,0:T(8,128)(2,1)} %copy-done.1, bf16[2,320,432]{2,1,0:T(8,128)(2,1)} %copy-done.4, bf16[2,320,432]{2,1,0:T(8,128)(2,1)} %copy-done.6, ...), custom_call_target="tpu_custom_call" | custom-call | tf_op jit(solution)/shard_map/pallas_call | solution.py:239
  164.9 4.7 %all-to-all-start.5 = ((bf16[8,64,128]{2,1,0:T(8,128)(2,1)}), bf16[8,64,128]{2,1,0:T(8,128)(2,1)S(1)}, u32[]{:S(2)}, u32[]{:S(2)}) async-start(bf16[8,64,128]{2,1,0:T(8,128)(2,1)} %broadcast_in_dim.64), calls=%async_computation.5 | async-start | bytes 262144 | tf_op jit(solution)/shard_map/all_to_all | solution.py:33
  169.6 4.6 %all-to-all-done.5 = bf16[8,64,128]{2,1,0:T(8,128)(2,1)S(1)} async-done(((bf16[8,64,128]{2,1,0:T(8,128)(2,1)}), bf16[8,64,128]{2,1,0:T(8,128)(2,1)S(1)}, u32[]{:S(2)}, u32[]{:S(2)}) %all-to-all-start.5) | async-done | bytes 131104 | tf_op jit(solution)/shard_map/all_to_all | solution.py:33
  174.9 6.7 %all-to-all-start.6 = ((bf16[4,64,128]{2,1,0:T(8,128)(2,1)}), bf16[4,64,128]{2,1,0:T(8,128)(2,1)S(1)}, u32[]{:S(2)}, u32[]{:S(2)}) async-start(bf16[4,64,128]{2,1,0:T(8,128)(2,1)} %broadcast_in_dim.65), calls=%async_computation.6 | async-start | bytes 131072 | tf_op jit(solution)/shard_map/all_to_all | solution.py:33
  182.4 10.8 %all-to-all-done.6 = bf16[4,64,128]{2,1,0:T(8,128)(2,1)S(1)} async-done(((bf16[4,64,128]{2,1,0:T(8,128)(2,1)}), bf16[4,64,128]{2,1,0:T(8,128)(2,1)S(1)}, u32[]{:S(2)}, u32[]{:S(2)}) %all-to-all-start.6) | async-done | bytes 65568 | tf_op jit(solution)/shard_map/all_to_all | solution.py:33
  193.9 5.6 %shard_map.180 = bf16[32,160,128]{2,1,0:T(8,128)(2,1)} custom-call(s32[3]{0:T(128)} %pad_add_fusion.flag_ref, f32[2,432,128]{2,1,0:T(8,128)} %get-tuple-element.46.base_ref, bf16[64,128]{1,0:T(8,128)(2,1)} %reduce_sum.79.reduced_ref, bf16[2,32,432]{2,1,0:T(8,128)(2,1)} %get-tuple-element.48.lift_ref, bf16[2,320,432]{2,1,0:T(8,128)(2,1)} %copy-done.1, ...), custom_call_target="tpu_custom_call" | custom-call | tf_op jit(solution)/shard_map/pallas_call | solution.py:239
  199.5 5.7 %all-to-all-start.7 = ((bf16[8,4,160,128]{3,2,1,0:T(8,128)(2,1)}), bf16[8,4,160,128]{3,2,1,0:T(8,128)(2,1)S(1)}, u32[]{:S(2)}, u32[]{:S(2)}) async-start(bf16[8,4,160,128]{3,2,1,0:T(8,128)(2,1)} %bitcast.91), calls=%async_computation.7 | async-start | bytes 2621440 | tf_op jit(solution)/shard_map/all_to_all | solution.py:33
  207.4 26.6 %collective-permute-done.16 = bf16[4,4,160,128]{3,2,1,0:T(8,128)(2,1)} collective-permute-done((bf16[4,4,160,128]{3,2,1,0:T(8,128)(2,1)S(1)}, bf16[4,4,160,128]{3,2,1,0:T(8,128)(2,1)}, u32[]{:S(2)}, u32[]{:S(2)}) %collective-permute-start.16) | collective-permute-done | bytes 655392 | tf_op jit(solution)/shard_map/ppermute | solution.py:37
  235.4 3.2 %collective-permute-start.17 = (bf16[4,160,128]{2,1,0:T(8,128)(2,1)S(1)}, bf16[4,160,128]{2,1,0:T(8,128)(2,1)S(1)}, u32[]{:S(2)}, u32[]{:S(2)}) collective-permute-start(bf16[4,160,128]{2,1,0:T(8,128)(2,1)S(1)} %get-tuple-element.52), channel_id=1, source_target_pairs={{0,2},{2,4},{4,6},{6,0},{1,3},{3,5},{5,7},{7,1},{8,10},{10,12},{12... | collective-permute-start | bytes 491528 | tf_op jit(solution)/shard_map/ppermute | solution.py:51
  238.6 3.3 %collective-permute-start.18 = (bf16[4,160,128]{2,1,0:T(8,128)(2,1)S(1)}, bf16[4,160,128]{2,1,0:T(8,128)(2,1)S(1)}, u32[]{:S(2)}, u32[]{:S(2)}) collective-permute-start(bf16[4,160,128]{2,1,0:T(8,128)(2,1)S(1)} %get-tuple-element.54), channel_id=1, source_target_pairs={{0,4},{2,6},{4,0},{6,2},{1,5},{3,7},{5,1},{7,3},{8,12},{10,14},{12... | collective-permute-start | bytes 491528 | tf_op jit(solution)/shard_map/ppermute | solution.py:51
  241.9 3.4 %collective-permute-start.19 = (bf16[4,160,128]{2,1,0:T(8,128)(2,1)S(1)}, bf16[4,160,128]{2,1,0:T(8,128)(2,1)S(1)}, u32[]{:S(2)}, u32[]{:S(2)}) collective-permute-start(bf16[4,160,128]{2,1,0:T(8,128)(2,1)S(1)} %get-tuple-element.53), channel_id=1, source_target_pairs={{0,6},{2,0},{4,2},{6,4},{1,7},{3,1},{5,3},{7,5},{8,14},{10,8},{12,... | collective-permute-start | bytes 491528 | tf_op jit(solution)/shard_map/ppermute | solution.py:51
  245.2 7.1 %collective-permute-done.18 = bf16[4,160,128]{2,1,0:T(8,128)(2,1)S(1)} collective-permute-done((bf16[4,160,128]{2,1,0:T(8,128)(2,1)S(1)}, bf16[4,160,128]{2,1,0:T(8,128)(2,1)S(1)}, u32[]{:S(2)}, u32[]{:S(2)}) %collective-permute-start.18) | collective-permute-done | bytes 163872 | tf_op jit(solution)/shard_map/ppermute | solution.py:51
  256.2 3.5 %all-to-all-start.8 = ((bf16[4,2,160,128]{3,2,1,0:T(8,128)(2,1)}), bf16[4,2,160,128]{3,2,1,0:T(8,128)(2,1)S(1)}, u32[]{:S(2)}, u32[]{:S(2)}) async-start(bf16[4,2,160,128]{3,2,1,0:T(8,128)(2,1)} %pad_maximum_fusion.3), calls=%async_computation.8 | async-start | bytes 655360 | tf_op jit(solution)/shard_map/all_to_all | solution.py:33
  260.4 21.9 %all-to-all-done.8 = bf16[4,2,160,128]{3,2,1,0:T(8,128)(2,1)S(1)} async-done(((bf16[4,2,160,128]{3,2,1,0:T(8,128)(2,1)}), bf16[4,2,160,128]{3,2,1,0:T(8,128)(2,1)S(1)}, u32[]{:S(2)}, u32[]{:S(2)}) %all-to-all-start.8) | async-done | bytes 327712 | tf_op jit(solution)/shard_map/all_to_all | solution.py:33
  (109 shorter events, 58.4 us)
Async XLA Ops:
  5.7 50.6 %all-to-all-start = ((bf16[4,2,2,128,640]{4,3,2,1,0:T(8,128)(2,1)}), bf16[4,2,2,128,640]{4,3,2,1,0:T(8,128)(2,1)S(1)}, u32[]{:S(2)}, u32[]{:S(2)}) async-start(bf16[4,2,2,128,640]{4,3,2,1,0:T(8,128)(2,1)} %rows_by_x.1), calls=%async_computation | async-start | bytes 5242880 | tf_op jit(solution)/shard_map/all_to_all | solution.py:33
  11.0 5.0 %collective-permute-start = (f32[64,128]{1,0:T(8,128)S(1)}, f32[64,128]{1,0:T(8,128)S(1)}, u32[]{:S(2)}, u32[]{:S(2)}) collective-permute-start(f32[64,128]{1,0:T(8,128)S(1)} %convolution_bitcast_fusion), channel_id=1, source_target_pairs={{0,1},{1,0},{2,3},{3,2},{4,5},{5,4},{6,7},{7,6},{8,9},{9,8},{10,11... | collective-permute-start | bytes 98312 | tf_op jit(solution)/shard_map/ppermute | solution.py:56
  15.9 25.2 %collective-permute-start.1 = (bf16[3,320,432]{2,1,0:T(8,128)(2,1)}, bf16[3,320,432]{2,1,0:T(8,128)(2,1)}, u32[]{:S(2)}, u32[]{:S(2)}) collective-permute-start(bf16[3,320,432]{2,1,0:T(8,128)(2,1)} %pad_maximum_fusion.refs_0_), channel_id=1, source_target_pairs={{0,256},{256,0},{1,257},{257,1},{2,258},{258,2},{3,259},{259,3},{4... | collective-permute-start | bytes 2488328 | tf_op jit(solution)/shard_map/ppermute | solution.py:37
  18.8 5.0 %collective-permute-start.2 = (f32[64,128]{1,0:T(8,128)S(1)}, f32[64,128]{1,0:T(8,128)S(1)}, u32[]{:S(2)}, u32[]{:S(2)}) collective-permute-start(f32[64,128]{1,0:T(8,128)S(1)} %add.99), channel_id=1, source_target_pairs={{0,2},{2,0},{4,6},{6,4},{1,3},{3,1},{5,7},{7,5},{8,10},{10,8},{12,... | collective-permute-start | bytes 98312 | tf_op jit(solution)/shard_map/ppermute | solution.py:56
  23.8 10.0 %collective-permute-start.3 = (f32[64,128]{1,0:T(8,128)S(1)}, f32[64,128]{1,0:T(8,128)S(1)}, u32[]{:S(2)}, u32[]{:S(2)}) collective-permute-start(f32[64,128]{1,0:T(8,128)S(1)} %add.100), channel_id=1, source_target_pairs={{0,4},{2,6},{4,0},{6,2},{1,5},{3,7},{5,1},{7,3},{8,12},{10,14},{12... | collective-permute-start | bytes 98312 | tf_op jit(solution)/shard_map/ppermute | solution.py:56
  28.7 27.7 %collective-permute-start.5 = (bf16[3,320,432]{2,1,0:T(8,128)(2,1)}, bf16[3,320,432]{2,1,0:T(8,128)(2,1)}, u32[]{:S(2)}, u32[]{:S(2)}) collective-permute-start(bf16[3,320,432]{2,1,0:T(8,128)(2,1)} %pad_maximum_fusion.refs_0_), channel_id=1, source_target_pairs={{0,32},{32,0},{1,33},{33,1},{2,34},{34,2},{3,35},{35,3},{4,36},{36... | collective-permute-start | bytes 2488328 | tf_op jit(solution)/shard_map/ppermute | solution.py:37
  41.2 15.2 %collective-permute-start.6 = (bf16[3,320,432]{2,1,0:T(8,128)(2,1)}, bf16[3,320,432]{2,1,0:T(8,128)(2,1)}, u32[]{:S(2)}, u32[]{:S(2)}) collective-permute-start(bf16[3,320,432]{2,1,0:T(8,128)(2,1)} %collective-permute-done.1.refs_1_), channel_id=1, source_target_pairs={{0,32},{32,0},{1,33},{33,1},{2,34},{34,2},{3,35},{35,3},{4,36},{36... | collective-permute-start | bytes 2488328 | tf_op jit(solution)/shard_map/ppermute | solution.py:37
  45.7 10.6 %collective-permute-start.4 = (f32[64,128]{1,0:T(8,128)S(1)}, f32[64,128]{1,0:T(8,128)S(1)}, u32[]{:S(2)}, u32[]{:S(2)}) collective-permute-start(f32[64,128]{1,0:T(8,128)S(1)} %add.101), channel_id=1, source_target_pairs={{0,8},{8,0},{16,24},{24,16},{1,9},{9,1},{17,25},{25,17},{2,10},{10... | collective-permute-start | bytes 98312 | tf_op jit(solution)/shard_map/ppermute | solution.py:56
  65.2 21.7 %all-to-all-start.1 = ((bf16[4,3,432,128]{3,2,1,0:T(8,128)(2,1)}), bf16[4,3,432,128]{3,2,1,0:T(8,128)(2,1)S(1)}, u32[]{:S(2)}, u32[]{:S(2)}) async-start(bf16[4,3,432,128]{3,2,1,0:T(8,128)(2,1)} %partials.1), calls=%async_computation.1 | async-start | bytes 2654208 | tf_op jit(solution)/shard_map/all_to_all | solution.py:33
  70.2 21.2 %collective-permute-start.7 = (f32[64,128]{1,0:T(8,128)S(1)}, f32[64,128]{1,0:T(8,128)S(1)}, u32[]{:S(2)}, u32[]{:S(2)}) collective-permute-start(f32[64,128]{1,0:T(8,128)S(1)} %add.102), channel_id=1, source_target_pairs={{0,16},{8,24},{16,0},{24,8},{1,17},{9,25},{17,1},{25,9},{2,18},{10... | collective-permute-start | bytes 98312 | tf_op jit(solution)/shard_map/ppermute | solution.py:56
  89.2 43.3 %copy-start.1 = (bf16[2,320,432]{2,1,0:T(8,128)(2,1)}, bf16[2,320,432]{2,1,0:T(8,128)(2,1)S(1)}, u32[]{:S(2)}) copy-start(bf16[2,320,432]{2,1,0:T(8,128)(2,1)S(1)} %pad_maximum_fusion.1.refs_0_) | copy-start | bytes 1658884
  89.2 28.1 %collective-permute-start.10 = (bf16[2,320,432]{2,1,0:T(8,128)(2,1)S(1)}, bf16[2,320,432]{2,1,0:T(8,128)(2,1)S(1)}, u32[]{:S(2)}, u32[]{:S(2)}) collective-permute-start(bf16[2,320,432]{2,1,0:T(8,128)(2,1)S(1)} %pad_maximum_fusion.1.refs_0_), channel_id=1, source_target_pairs={{0,64},{64,128},{128,192},{192,0},{1,65},{65,129},{129,193},{193,1... | collective-permute-start | bytes 1658888 | tf_op jit(solution)/shard_map/ppermute | solution.py:51
  96.1 11.0 %all-to-all-start.2 = ((bf16[8,64,128]{2,1,0:T(8,128)(2,1)}), bf16[8,64,128]{2,1,0:T(8,128)(2,1)S(1)}, u32[]{:S(2)}, u32[]{:S(2)}) async-start(bf16[8,64,128]{2,1,0:T(8,128)(2,1)} %broadcast_in_dim.61), calls=%async_computation.2 | async-start | bytes 262144 | tf_op jit(solution)/shard_map/all_to_all | solution.py:33
  102.5 36.8 %collective-permute-start.12 = (bf16[2,320,432]{2,1,0:T(8,128)(2,1)S(1)}, bf16[2,320,432]{2,1,0:T(8,128)(2,1)S(1)}, u32[]{:S(2)}, u32[]{:S(2)}) collective-permute-start(bf16[2,320,432]{2,1,0:T(8,128)(2,1)S(1)} %pad_maximum_fusion.1.refs_0_), channel_id=1, source_target_pairs={{0,192},{64,0},{128,64},{192,128},{1,193},{65,1},{129,65},{193,129... | collective-permute-start | bytes 1658888 | tf_op jit(solution)/shard_map/ppermute | solution.py:51
  107.7 21.5 %all-to-all-start.3 = ((bf16[4,64,128]{2,1,0:T(8,128)(2,1)}), bf16[4,64,128]{2,1,0:T(8,128)(2,1)S(1)}, u32[]{:S(2)}, u32[]{:S(2)}) async-start(bf16[4,64,128]{2,1,0:T(8,128)(2,1)} %broadcast_in_dim.62), calls=%async_computation.3 | async-start | bytes 131072 | tf_op jit(solution)/shard_map/all_to_all | solution.py:33
  117.3 28.2 %copy-start.4 = (bf16[2,320,432]{2,1,0:T(8,128)(2,1)}, bf16[2,320,432]{2,1,0:T(8,128)(2,1)S(1)}, u32[]{:S(2)}) copy-start(bf16[2,320,432]{2,1,0:T(8,128)(2,1)S(1)} %collective-permute-done.10.refs_1_) | copy-start | bytes 1658884
  117.3 24.1 %collective-permute-start.11 = (bf16[2,320,432]{2,1,0:T(8,128)(2,1)S(1)}, bf16[2,320,432]{2,1,0:T(8,128)(2,1)S(1)}, u32[]{:S(2)}, u32[]{:S(2)}) collective-permute-start(bf16[2,320,432]{2,1,0:T(8,128)(2,1)S(1)} %collective-permute-done.10.refs_1_), channel_id=1, source_target_pairs={{0,64},{64,128},{128,192},{192,0},{1,65},{65,129},{129,193},{193,1... | collective-permute-start | bytes 1658888 | tf_op jit(solution)/shard_map/ppermute | solution.py:51
  119.2 12.5 %collective-permute-start.8 = (bf16[64,432]{1,0:T(8,128)(2,1)}, bf16[64,432]{1,0:T(8,128)(2,1)S(1)}, u32[]{:S(2)}, u32[]{:S(2)}) collective-permute-start(bf16[64,432]{1,0:T(8,128)(2,1)} %get-tuple-element.34), channel_id=1, source_target_pairs={{0,256},{1,257},{2,258},{3,259},{4,260},{5,261},{6,262},{7,263},{8... | collective-permute-start | bytes 165896 | tf_op jit(solution)/shard_map/ppermute | solution.py:307
  130.4 10.9 %collective-permute-start.9 = (bf16[64,160]{1,0:T(8,128)(2,1)S(1)}, bf16[64,160]{1,0:T(8,128)(2,1)S(1)}, u32[]{:S(2)}, u32[]{:S(2)}) collective-permute-start(bf16[64,160]{1,0:T(8,128)(2,1)S(1)} %fusion.1), channel_id=1, source_target_pairs={{0,256},{1,257},{2,258},{3,259},{4,260},{5,261},{6,262},{7,263},{8... | collective-permute-start | bytes 61448 | tf_op jit(solution)/shard_map/ppermute | solution.py:307
  132.5 20.6 %collective-permute-start.13 = (bf16[2,320,432]{2,1,0:T(8,128)(2,1)S(1)}, bf16[2,320,432]{2,1,0:T(8,128)(2,1)S(1)}, u32[]{:S(2)}, u32[]{:S(2)}) collective-permute-start(bf16[2,320,432]{2,1,0:T(8,128)(2,1)S(1)} %collective-permute-done.10.refs_1_), channel_id=1, source_target_pairs={{0,32},{32,0},{1,33},{33,1},{2,34},{34,2},{3,35},{35,3},{4,36},{36... | collective-permute-start | bytes 1658888 | tf_op jit(solution)/shard_map/ppermute | solution.py:37
  139.3 13.9 %collective-permute-start.15 = (bf16[2,320,432]{2,1,0:T(8,128)(2,1)S(1)}, bf16[2,320,432]{2,1,0:T(8,128)(2,1)S(1)}, u32[]{:S(2)}, u32[]{:S(2)}) collective-permute-start(bf16[2,320,432]{2,1,0:T(8,128)(2,1)S(1)} %collective-permute-done.12.refs_3_), channel_id=1, source_target_pairs={{0,32},{32,0},{1,33},{33,1},{2,34},{34,2},{3,35},{35,3},{4,36},{36... | collective-permute-start | bytes 1658888 | tf_op jit(solution)/shard_map/ppermute | solution.py:37
  141.4 11.8 %collective-permute-start.14 = (bf16[2,320,432]{2,1,0:T(8,128)(2,1)S(1)}, bf16[2,320,432]{2,1,0:T(8,128)(2,1)}, u32[]{:S(2)}, u32[]{:S(2)}) collective-permute-start(bf16[2,320,432]{2,1,0:T(8,128)(2,1)S(1)} %collective-permute-done.11.refs_2_), channel_id=1, source_target_pairs={{0,32},{32,0},{1,33},{33,1},{2,34},{34,2},{3,35},{35,3},{4,36},{36... | collective-permute-start | bytes 1658888 | tf_op jit(solution)/shard_map/ppermute | solution.py:37
  145.5 15.6 %all-to-all-start.4 = ((bf16[8,64,592]{2,1,0:T(8,128)(2,1)}), bf16[8,64,592]{2,1,0:T(8,128)(2,1)}, u32[]{:S(2)}, u32[]{:S(2)}) async-start(bf16[8,64,592]{2,1,0:T(8,128)(2,1)} %broadcast_in_dim.63), calls=%async_computation.4 | async-start | bytes 1310720 | tf_op jit(solution)/shard_map/all_to_all | solution.py:33
  159.4 22.2 %copy-start.13 = (f32[2,32,432]{2,1,0:T(8,128)S(1)}, f32[2,32,432]{2,1,0:T(8,128)}, u32[]{:S(2)}) copy-start(f32[2,32,432]{2,1,0:T(8,128)} %param.22) | copy-start | bytes 331780
  164.9 9.3 %all-to-all-start.5 = ((bf16[8,64,128]{2,1,0:T(8,128)(2,1)}), bf16[8,64,128]{2,1,0:T(8,128)(2,1)S(1)}, u32[]{:S(2)}, u32[]{:S(2)}) async-start(bf16[8,64,128]{2,1,0:T(8,128)(2,1)} %broadcast_in_dim.64), calls=%async_computation.5 | async-start | bytes 262144 | tf_op jit(solution)/shard_map/all_to_all | solution.py:33
  174.9 18.4 %all-to-all-start.6 = ((bf16[4,64,128]{2,1,0:T(8,128)(2,1)}), bf16[4,64,128]{2,1,0:T(8,128)(2,1)S(1)}, u32[]{:S(2)}, u32[]{:S(2)}) async-start(bf16[4,64,128]{2,1,0:T(8,128)(2,1)} %broadcast_in_dim.65), calls=%async_computation.6 | async-start | bytes 131072 | tf_op jit(solution)/shard_map/all_to_all | solution.py:33
  199.5 55.8 %all-to-all-start.7 = ((bf16[8,4,160,128]{3,2,1,0:T(8,128)(2,1)}), bf16[8,4,160,128]{3,2,1,0:T(8,128)(2,1)S(1)}, u32[]{:S(2)}, u32[]{:S(2)}) async-start(bf16[8,4,160,128]{3,2,1,0:T(8,128)(2,1)} %bitcast.91), calls=%async_computation.7 | async-start | bytes 2621440 | tf_op jit(solution)/shard_map/all_to_all | solution.py:33
  205.2 28.9 %collective-permute-start.16 = (bf16[4,4,160,128]{3,2,1,0:T(8,128)(2,1)S(1)}, bf16[4,4,160,128]{3,2,1,0:T(8,128)(2,1)}, u32[]{:S(2)}, u32[]{:S(2)}) collective-permute-start(bf16[4,4,160,128]{3,2,1,0:T(8,128)(2,1)S(1)} %dynamic-slice_bitcast_fusion), channel_id=1, source_target_pairs={{0,1},{1,0},{2,3},{3,2},{4,5},{5,4},{6,7},{7,6},{8,9},{9,8},{10,11... | collective-permute-start | bytes 1966088 | tf_op jit(solution)/shard_map/ppermute | solution.py:37
  235.4 9.9 %collective-permute-start.17 = (bf16[4,160,128]{2,1,0:T(8,128)(2,1)S(1)}, bf16[4,160,128]{2,1,0:T(8,128)(2,1)S(1)}, u32[]{:S(2)}, u32[]{:S(2)}) collective-permute-start(bf16[4,160,128]{2,1,0:T(8,128)(2,1)S(1)} %get-tuple-element.52), channel_id=1, source_target_pairs={{0,2},{2,4},{4,6},{6,0},{1,3},{3,5},{5,7},{7,1},{8,10},{10,12},{12... | collective-permute-start | bytes 491528 | tf_op jit(solution)/shard_map/ppermute | solution.py:51
  238.6 13.7 %collective-permute-start.18 = (bf16[4,160,128]{2,1,0:T(8,128)(2,1)S(1)}, bf16[4,160,128]{2,1,0:T(8,128)(2,1)S(1)}, u32[]{:S(2)}, u32[]{:S(2)}) collective-permute-start(bf16[4,160,128]{2,1,0:T(8,128)(2,1)S(1)} %get-tuple-element.54), channel_id=1, source_target_pairs={{0,4},{2,6},{4,0},{6,2},{1,5},{3,7},{5,1},{7,3},{8,12},{10,14},{12... | collective-permute-start | bytes 491528 | tf_op jit(solution)/shard_map/ppermute | solution.py:51
  241.9 13.3 %collective-permute-start.19 = (bf16[4,160,128]{2,1,0:T(8,128)(2,1)S(1)}, bf16[4,160,128]{2,1,0:T(8,128)(2,1)S(1)}, u32[]{:S(2)}, u32[]{:S(2)}) collective-permute-start(bf16[4,160,128]{2,1,0:T(8,128)(2,1)S(1)} %get-tuple-element.53), channel_id=1, source_target_pairs={{0,6},{2,0},{4,2},{6,4},{1,7},{3,1},{5,3},{7,5},{8,14},{10,8},{12,... | collective-permute-start | bytes 491528 | tf_op jit(solution)/shard_map/ppermute | solution.py:51
  256.2 26.0 %all-to-all-start.8 = ((bf16[4,2,160,128]{3,2,1,0:T(8,128)(2,1)}), bf16[4,2,160,128]{3,2,1,0:T(8,128)(2,1)S(1)}, u32[]{:S(2)}, u32[]{:S(2)}) async-start(bf16[4,2,160,128]{3,2,1,0:T(8,128)(2,1)} %pad_maximum_fusion.3), calls=%async_computation.8 | async-start | bytes 655360 | tf_op jit(solution)/shard_map/all_to_all | solution.py:33
  (13 other events, 87.9 us)
